TPU v7x, 32 devices: a whole 2x2x4 slice. The times are simulated.
32 devices in a mesh: segment: 2 (over core), tp: 8 (over z, y), dp: 2 (over x).
Axes of the slice: x: 2, y: 2, z: 4, core: 2. Of those that a mesh axis runs over, the one named last changes fastest.
Arguments:
- inputs: bfloat16 [1, 256, 6144], P(None, 'dp', 'tp'), parts along dimension 1, may hold values from -6 to 6
- norm_gain: float32 [2, 6144], P('segment'), may hold values from 0.1 to 1.9
- w_in: bfloat16 [2, 24576, 6144], P('segment', 'tp'), may hold values from -0.109375 to 0.109375
- b_in: float32 [2, 24576], P('segment', 'tp'), may hold values from -3 to 3
- w_out: bfloat16 [2, 6144, 24576], P('segment', 'tp'), may hold values from -0.0546875 to 0.0546875
- b_out: float32 [2, 6144], P('segment', 'tp'), may hold values from -3 to 3
Outputs:
- sections_out: bfloat16 [2, 1, 256, 6144], P('segment', None, 'dp', 'tp'), parts along dimension 2
There are 2 independent parts, one for each index of `dp`. A program takes and returns all parts, laid end to end along the dimension named above; an argument that names none is the same for every part. Nothing has to cross between parts.
All inputs are finite; a program needn't handle non-finite values.
Results may differ from a plain program's by a relative error of at most 0.0058.
Values may be sent and summed in bfloat16 or wider, within the bound.
No kernel may reach another device: no remote copies, remote signals or barrier semaphores. Data moves between devices by JAX's collectives and lax.ppermute only.
A program may use at most 192 MiB of HBM per device.

v0:
```python
import functools

import jax
import jax.numpy as jnp
import numpy as np
from jax import lax
from jax.experimental import pallas as pl
from jax.experimental.pallas import tpu as pltpu
from jax.sharding import PartitionSpec as P

MIB = 1024 * 1024
VM = pl.BlockSpec(memory_space=pltpu.VMEM)
SM = pl.BlockSpec(memory_space=pltpu.SMEM)
ANY = pl.BlockSpec(memory_space=pl.ANY)


def shifted(value, axis, steps):
    count = lax.axis_size(axis)
    first, last = (max(0, -steps), min(count, count - steps))
    return lax.ppermute(value, axis, [(source, source + steps) for source in range(first, last)])


def contract(left, right):
    return lax.dot_general(
        left, right, (((1,), (1,)), ((), ())), preferred_element_type=jnp.float32
    )


def plain_section(local, gain, w_first, b_first, w_second, b_second):
    whole = lax.all_gather(local, "tp", axis=1, tiled=True)
    values = whole.astype(jnp.float32)
    center = jnp.mean(values, axis=1, keepdims=True)
    spread = jnp.mean((values - center) ** 2, axis=1, keepdims=True)
    normed = ((values - center) * lax.rsqrt(spread + 1e-05) * gain).astype(jnp.bfloat16)
    pre = contract(normed, w_first) + b_first
    hidden = jax.nn.gelu(pre, approximate=True).astype(jnp.bfloat16)
    branch = contract(lax.all_gather(hidden, "tp", axis=1, tiled=True), w_second)
    return (local.astype(jnp.float32) + branch + b_second).astype(jnp.bfloat16)


def plain_shards(inputs, norm_gain, w_in, b_in, w_out, b_out):
    batches, tok_rows, width = inputs.shape
    first_segment = lax.axis_index("segment") == 0
    incoming = jnp.zeros((tok_rows, width), jnp.bfloat16)
    results = []
    for tick in range(batches + 1):
        own = inputs[min(tick, batches - 1)]
        current = jnp.where(first_segment, own, incoming)
        result = plain_section(current, norm_gain[0], w_in[0], b_in[0], w_out[0], b_out[0])
        results.append(result)
        if tick < batches:
            incoming = shifted(result, "segment", 1)
    early = jnp.stack(results[:batches])
    late = jnp.stack(results[1:])
    chosen = jnp.where(first_segment, early, late)
    return chosen.reshape(1, batches, tok_rows, width)


def pallas(kernel, outs, specs, out_specs, scratch=(), limit=28, flops=0, moved=0):
    return pl.pallas_call(
        kernel,
        out_shape=outs,
        in_specs=specs,
        out_specs=out_specs,
        scratch_shapes=list(scratch),
        compiler_params=pltpu.CompilerParams(vmem_limit_bytes=limit * MIB),
        cost_estimate=pl.CostEstimate(flops=flops, bytes_accessed=moved, transcendentals=0),
    )


def normalize(pieces, spots, gain_ref, out_ref):
    width = out_ref.shape[0]
    total = 0.0
    for ref in pieces:
        total = total + jnp.sum(ref[...].astype(jnp.float32), axis=0, keepdims=True)
    center = total / width
    square = 0.0
    for ref in pieces:
        square = square + jnp.sum((ref[...].astype(jnp.float32) - center) ** 2, axis=0, keepdims=True)
    scale = lax.rsqrt(square / width + 1e-05)
    for ref, spot in zip(pieces, spots):
        rows = pl.ds(pl.multiple_of(spot, 64), ref.shape[0])
        value = (ref[...].astype(jnp.float32) - center) * scale * gain_ref[rows, :]
        out_ref[rows, :] = value.astype(jnp.bfloat16)


def first_kernel(offset, tile, slots, layout, info_ref, bias_ref, w_ref, *refs):
    out_ref, buf, sems = refs[-3:]
    rows = out_ref.shape[0]
    steps = rows // tile

    def copy(step, slot):
        start = pl.multiple_of(offset + step * tile, tile)
        return pltpu.make_async_copy(w_ref.at[0, pl.ds(start, tile), :], buf.at[slot], sems.at[slot])

    for step in range(min(slots, steps)):
        copy(step, step).start()
    if layout is None:
        normed_ref = refs[0]
    else:
        gain_ref, pieces, normed_ref = refs[0], refs[1:-4], refs[-4]
        part, half, places = layout
        seg = info_ref[0]
        spots = [info_ref[1 + k] * part + row + seg * half for k, row in places]
        spots += [info_ref[1 + k] * part + row + (1 - seg) * half for k, row in places]
        normalize(pieces, spots, gain_ref, normed_ref)

    def body(step, carry):
        slot = lax.rem(step, slots)
        copy(step, slot).wait()
        at = pl.multiple_of(step * tile, tile)
        pre = jnp.dot(buf[slot], normed_ref[...], preferred_element_type=jnp.float32)
        pre = pre + bias_ref[pl.ds(pl.multiple_of(offset + at, tile), tile), :]
        out_ref[pl.ds(at, tile), :] = jax.nn.gelu(pre, approximate=True).astype(jnp.bfloat16)

        @pl.when(step + slots < steps)
        def _():
            copy(step + slots, slot).start()

        return carry

    lax.fori_loop(0, steps, body, 0)


def first_matmul(info, bias, w, offset, rows, normed=None, gain=None, pieces=None, layout=None):
    tile = 256
    slots = min(6, rows // tile)
    width, tokens = w.shape[2], bias.shape[1]
    out = jax.ShapeDtypeStruct((rows, tokens), jnp.bfloat16)
    scratch = [pltpu.VMEM((slots, tile, width), jnp.bfloat16), pltpu.SemaphoreType.DMA((slots,))]
    cost = dict(flops=2 * rows * width * tokens, moved=2 * rows * width)
    if pieces is None:
        kernel = functools.partial(first_kernel, offset, tile, slots, None)
        return pallas(kernel, out, [SM, VM, ANY, VM], VM, scratch, **cost)(info, bias, w, normed)
    kernel = functools.partial(first_kernel, offset, tile, slots, layout)
    outs = [jax.ShapeDtypeStruct((width, tokens), jnp.bfloat16), out]
    call = pallas(kernel, outs, [SM, VM, ANY, VM] + [VM] * len(pieces), [VM, VM], scratch, **cost)
    return call(info, bias, w, gain, *pieces)


def pick_kernel(phase, info_ref, here_ref, crossed_ref, out_ref):
    @pl.when(info_ref[0] == phase)
    def _():
        out_ref[...] = here_ref[...]

    @pl.when(info_ref[0] != phase)
    def _():
        out_ref[...] = crossed_ref[...]


def pick(phase, info, here, crossed):
    out = jax.ShapeDtypeStruct(here.shape, here.dtype)
    return pallas(functools.partial(pick_kernel, phase), out, [SM, VM, VM], VM, limit=8)(info, here, crossed)


def relay_kernel(info_ref, kept_ref, swapped_ref, out_ref, own_ref):
    half = own_ref.shape[0]

    @pl.when(info_ref[0] == 0)
    def _():
        out_ref[...] = kept_ref[...]
        own_ref[...] = kept_ref[:half]

    @pl.when(info_ref[0] != 0)
    def _():
        out_ref[...] = swapped_ref[...]
        own_ref[...] = swapped_ref[half:]


def relay(info, kept, swapped):
    half = (kept.shape[0] // 2, kept.shape[1])
    outs = [jax.ShapeDtypeStruct(kept.shape, kept.dtype), jax.ShapeDtypeStruct(half, kept.dtype)]
    return pallas(relay_kernel, outs, [SM, VM, VM], [VM, VM], limit=8)(info, kept, swapped)


def halve_kernel(front_ref, back_ref, lower_ref, upper_ref):
    mid = lower_ref.shape[0]
    lower_ref[...] = front_ref[:mid]
    upper_ref[...] = back_ref[mid:]


def halve(front, back):
    mid = front.shape[0] // 2
    outs = [
        jax.ShapeDtypeStruct((mid, front.shape[1]), front.dtype),
        jax.ShapeDtypeStruct((front.shape[0] - mid, front.shape[1]), front.dtype),
    ]
    return pallas(halve_kernel, outs, [VM, VM], [VM, VM], limit=8)(front, back)


def second_kernel(places, first, ending, *refs):
    count = len(places)
    info_ref, w_ref = refs[:2]
    pieces, refs = refs[2 : 2 + count], refs[2 + count :]
    buf, joined, sems = refs[-3:]
    refs = refs[:-3]
    if not first:
        acc_ref, refs = refs[0], refs[1:]
    depth, tile = w_ref.shape[1], 256

    def tile_copies(t):
        at = 0
        for i, (k, scale, row) in enumerate(places):
            rows = pieces[i].shape[0]
            down = pl.ds(pl.multiple_of(t * tile, tile), tile)
            columns = pl.ds(pl.multiple_of(info_ref[1 + k] * scale + row, 128), rows)
            yield pltpu.make_async_copy(w_ref.at[0, down, columns], buf.at[down, pl.ds(at, rows)], sems.at[t, i])
            at += rows

    def start(t, carry):
        for copy in tile_copies(t):
            copy.start()
        return carry

    lax.fori_loop(0, depth // tile, start, 0)
    at = 0
    for ref in pieces:
        joined[pl.ds(at, ref.shape[0]), :] = ref[...]
        at += ref.shape[0]

    def body(t, carry):
        for copy in tile_copies(t):
            copy.wait()
        own = pl.ds(pl.multiple_of(t * tile, tile), tile)
        acc = jnp.dot(buf[own, :], joined[...], preferred_element_type=jnp.float32)
        if not first:
            acc = acc_ref[own, :] + acc
        if not ending:
            refs[0][own, :] = acc
            return carry
        local_ref, bias_ref = refs[:2]
        result = local_ref[own, :].astype(jnp.float32) + (acc + bias_ref[own, :])
        if ending == 1:
            refs[2][own, :] = result.astype(jnp.bfloat16)
        else:
            early_ref, out_ref = refs[2:]
            rounded = result.astype(jnp.bfloat16).astype(jnp.float32)
            result = jnp.where(info_ref[0] == 0, early_ref[own, :].astype(jnp.float32), rounded)
            out_ref[:, own] = result.T.astype(jnp.bfloat16)
        return carry

    lax.fori_loop(0, depth // tile, body, 0)


def second_matmul(info, acc, pieces, places, w, ends=()):
    depth, tokens = w.shape[1], pieces[0].shape[1]
    total = sum(piece.shape[0] for piece in pieces)
    ending = max(0, len(ends) - 1)
    args = [info, w, *pieces] + ([] if acc is None else [acc]) + list(ends)
    if ending == 2:
        out = jax.ShapeDtypeStruct((tokens, depth), jnp.bfloat16)
    else:
        out = jax.ShapeDtypeStruct((depth, tokens), jnp.bfloat16 if ending else jnp.float32)
    scratch = [
        pltpu.VMEM((depth, total), jnp.bfloat16),
        pltpu.VMEM((total, tokens), jnp.bfloat16),
        pltpu.SemaphoreType.DMA((depth // 256, len(pieces))),
    ]
    kernel = functools.partial(second_kernel, places, acc is None, ending)
    cost = dict(flops=2 * depth * total * tokens, moved=2 * depth * total)
    return pallas(kernel, out, [SM, ANY] + [VM] * (len(args) - 2), VM, scratch, **cost)(*args)


def ring_shards(ring, inputs, norm_gain, w_in, b_in, w_out, b_out):
    n = len(ring)
    last = n // 2
    tokens, part = inputs.shape[1:]
    half = part // 2
    width = norm_gain.shape[1]
    hidden = w_in.shape[1]
    side = hidden // 2
    seg = lax.axis_index("segment")
    place = {device: at for at, device in enumerate(ring)}
    behind = np.array([[ring[(place[t] - k) % n] for k in range(n)] for t in range(n)], np.int32)
    owner = jnp.asarray(behind)[lax.axis_index("tp")]
    info = jnp.concatenate([seg.reshape(1).astype(jnp.int32), owner])

    def hop(value, steps):
        return lax.ppermute(value, "tp", [(ring[at], ring[(at + steps) % n]) for at in range(n)])

    def swap(value):
        return lax.ppermute(value, "segment", [(0, 1), (1, 0)])

    local = inputs[0].T
    own = lax.dynamic_slice_in_dim(inputs[0], seg * half, half, 1).T
    gain = jnp.broadcast_to(norm_gain[0][:, None], (width, tokens))
    bias_in = jnp.broadcast_to(b_in[0][:, None], (hidden, tokens))
    bias_out = jnp.broadcast_to(b_out[0][:, None], (part, tokens))

    mid = half // 2
    x_places = [(0, 0)] + [(k, 0) for step in range(1, last) for k in (step, n - step)] + [(last, 0), (last, mid)]

    early = None
    for phase in range(2):
        front = back = own
        mine, theirs = [own], [swap(own)]
        for step in range(1, last + 1):
            if step == last:
                front, back = halve(front, back)
            front, back = hop(front, 1), hop(back, -1)
            if phase == 0 and step == 1:
                front, back, info, local = lax.optimization_barrier((front, back, info, local))
            if phase == 0 and step == 2:
                front, back, gain = lax.optimization_barrier((front, back, gain))
            if phase == 0 and step == 3:
                front, back, bias_in, bias_out = lax.optimization_barrier((front, back, bias_in, bias_out))
            mine += [front, back]
            theirs += [swap(front), swap(back)]
        normed, other = first_matmul(
            info, bias_in, w_in, side, side, gain=gain, pieces=mine + theirs, layout=(part, half, x_places)
        )
        crossed = swap(other)
        here = first_matmul(info, bias_in, w_in, 0, side, normed=normed)
        front = back = pick(phase, info, here, crossed)
        acc = None
        places, pieces = [(0, hidden, 0), (0, hidden, side)], [here, other]
        for step in range(1, last + 1):
            if step == last:
                front, back = halve(front, back)
            front, back = hop(front, 1), hop(back, -1)
            acc = second_matmul(info, acc, pieces, places, w_out)
            front, back, acc = lax.optimization_barrier((front, back, acc))
            at = side // 2 if step == last else 0
            places = [(step, hidden, 0), (n - step, hidden, at), (step, hidden, side), (n - step, hidden, side + at)]
            pieces = [front, back, swap(front), swap(back)]
        acc = second_matmul(info, acc, pieces[:2], places[:2], w_out)
        ends = [local, bias_out] + ([] if early is None else [early])
        result = second_matmul(info, acc, pieces[2:], places[2:], w_out, ends)
        if phase == 0:
            early = result
            local, own = relay(info, early, swap(early))
    return result.reshape(1, 1, tokens, part)


def snake(mesh):
    n = mesh.shape["tp"]
    return [2 * at for at in range(n // 2)] + [2 * at + 1 for at in reversed(range(n // 2))]


def solution(mesh):
    def shards(inputs, norm_gain, w_in, b_in, w_out, b_out):
        small = mesh.shape["tp"] == 8 and mesh.shape["segment"] == 2 and inputs.shape[0] == 1
        if small and inputs.shape[2] % 512 == 0 or small and inputs.shape[2] % 768 == 0:
            return ring_shards(snake(mesh), inputs, norm_gain, w_in, b_in, w_out, b_out)
        return plain_shards(inputs, norm_gain, w_in, b_in, w_out, b_out)

    return jax.shard_map(
        shards,
        mesh=mesh,
        in_specs=(
            P(None, "dp", "tp"),
            P("segment", None),
            P("segment", "tp", None),
            P("segment", "tp"),
            P("segment", "tp", None),
            P("segment", "tp"),
        ),
        out_specs=P("segment", None, "dp", "tp"),
        check_vma=False,
    )
```

profile of v0, /device:TPU:0, one launch (start us, length us, event | category | flops | bytes accessed | tf_op | source)
XLA Modules:
  0.0 198.3 jit_solution(6153638140110088474)
XLA Ops:
  0.0 0.9 constant_dynamic-slice_fusion
  1.0 3.0 %collective-permute-start.1 = (bf16[384,128]{1,0:T(8,128)(2,1)S(1)}, bf16[384,128]{1,0:T(8,128)(2,1)}, u32[]{:S(2)}, u32[]{:S(2)}) collective-permute-start(bf16[384,128]{1,0:T(8,128)(2,1)S(1)} %bitcast.13), channel_id=1, source_target_pairs={{0,2},{4,0},{8,4},{12,8},{14,12},{10,14},{6,10},{2,6},{1,3},{5,1},... | collective-permute-start | bytes 294920 | tf_op jit(solution)/shard_map/ppermute | solution.py:279
  4.2 1.1 copy.9
  5.3 0.7 dynamic-slice_bitcast_fusion
  6.1 1.0 collective-permute-done.1.refs_3_
  7.0 1.8 collective-permute-done.refs_2_
  8.9 1.9 collective-permute-start.3
  10.8 2.9 %collective-permute-done.2.refs_4_ = bf16[384,128]{1,0:T(8,128)(2,1)} collective-permute-done((bf16[384,128]{1,0:T(8,128)(2,1)}, bf16[384,128]{1,0:T(8,128)(2,1)}, u32[]{:S(2)}, u32[]{:S(2)}) %collective-permute-start.2) | collective-permute-done | bytes 98336 | tf_op jit(solution)/shard_map/ppermute | solution.py:279
  13.8 1.6 broadcast_in_dim.22.refs_0_
  15.5 2.0 %collective-permute-start.4 = (bf16[384,128]{1,0:T(8,128)(2,1)}, bf16[384,128]{1,0:T(8,128)(2,1)S(1)}, u32[]{:S(2)}, u32[]{:S(2)}) collective-permute-start(bf16[384,128]{1,0:T(8,128)(2,1)} %collective-permute-done.2.refs_4_), channel_id=1, source_target_pairs={{0,4},{4,8},{8,12},{12,14},{14,10},{10,6},{6,2},{2,0},{1,5},{5,9},... | collective-permute-start | bytes 294920 | tf_op jit(solution)/shard_map/ppermute | solution.py:279
  18.0 2.3 %collective-permute-done.4.front_ref.refs_6_ = bf16[384,128]{1,0:T(8,128)(2,1)S(1)} collective-permute-done((bf16[384,128]{1,0:T(8,128)(2,1)}, bf16[384,128]{1,0:T(8,128)(2,1)S(1)}, u32[]{:S(2)}, u32[]{:S(2)}) %collective-permute-start.4) | collective-permute-done | bytes 98336 | tf_op jit(solution)/shard_map/ppermute | solution.py:279
  20.4 2.0 %collective-permute-done.5.back_ref.refs_7_ = bf16[384,128]{1,0:T(8,128)(2,1)} collective-permute-done((bf16[384,128]{1,0:T(8,128)(2,1)}, bf16[384,128]{1,0:T(8,128)(2,1)}, u32[]{:S(2)}, u32[]{:S(2)}) %collective-permute-start.5) | collective-permute-done | bytes 98336 | tf_op jit(solution)/shard_map/ppermute | solution.py:279
  22.6 1.2 broadcast_in_dim.24.bias_ref
  23.7 0.9 shard_map.73
  24.7 1.6 collective-permute-start.6
  27.3 1.6 collective-permute-done.6.refs_8_
  28.9 1.5 collective-permute-done.7.refs_9_
  30.4 1.2 collective-permute-done.16.refs_18_
  31.6 10.3 %shard_map.74 = (bf16[6144,128]{1,0:T(8,128)(2,1)S(1)}, bf16[1536,128]{1,0:T(8,128)(2,1)S(1)}) custom-call(s32[9]{0:T(128)S(1)} %pad_add_fusion.info_ref.refs_0_, f32[3072,128]{1,0:T(8,128)S(1)} %broadcast_in_dim.24.bias_ref, bf16[1,3072,6144]{2,1,0:T(8,128)(2,1)} %w_ref.7, f32[6144,128]{1,0:T(8,128)S(1)} %broadcast_in_dim.22.refs_0_, ...), custom_call_target="tpu_custom_call" | custom-call | flops 2415919104 | bytes 18874368 | tf_op jit(solution)/shard_map/pallas_call | solution.py:138
  42.1 8.5 %shard_map.75.here_ref.refs_2_ = bf16[1536,128]{1,0:T(8,128)(2,1)S(1)} custom-call(s32[9]{0:T(128)S(1)} %pad_add_fusion.info_ref.refs_0_, f32[3072,128]{1,0:T(8,128)S(1)} %broadcast_in_dim.24.bias_ref, bf16[1,3072,6144]{2,1,0:T(8,128)(2,1)} %w_ref.7, bf16[6144,128]{1,0:T(8,128)(2,1)S(1)} %get-tuple-element.65.refs_0_), custom_call_target="tpu_custom_call" | custom-call | flops 2415919104 | bytes 18874368 | tf_op jit(solution)/shard_map/pallas_call | solution.py:134
  51.7 1.6 collective-permute-start.18
  53.3 3.7 %shard_map.77.refs_6_ = f32[768,128]{1,0:T(8,128)S(1)} custom-call(s32[9]{0:T(128)S(1)} %pad_add_fusion.info_ref.refs_0_, bf16[1,768,24576]{2,1,0:T(8,128)(2,1)} %refs_1_.23, bf16[1536,128]{1,0:T(8,128)(2,1)S(1)} %shard_map.75.here_ref.refs_2_, bf16[1536,128]{1,0:T(8,128)(2,1)S(1)} %get-tuple-element.66.refs_3_), custom_call_target="tpu_custom_call" | custom-call | flops 603979776 | bytes 4718592 | tf_op jit(solution)/shard_map/pallas_call | solution.py:261
  57.0 5.7 %collective-permute-done.19.refs_3_ = bf16[1536,128]{1,0:T(8,128)(2,1)S(1)} collective-permute-done((bf16[1536,128]{1,0:T(8,128)(2,1)S(1)}, bf16[1536,128]{1,0:T(8,128)(2,1)S(1)}, u32[]{:S(2)}, u32[]{:S(2)}) %collective-permute-start.19) | collective-permute-done | bytes 393248 | tf_op jit(solution)/shard_map/ppermute | solution.py:279
  63.3 1.6 collective-permute-start.20
  65.4 5.4 %shard_map.78.refs_6_ = f32[768,128]{1,0:T(8,128)S(1)} custom-call(s32[9]{0:T(128)S(1)} %pad_add_fusion.info_ref.refs_0_, bf16[1,768,24576]{2,1,0:T(8,128)(2,1)} %refs_1_.23, bf16[1536,128]{1,0:T(8,128)(2,1)S(1)} %collective-permute-done.18.refs_2_, bf16[1536,128]{1,0:T(8,128)(2,1)S(1)} %collective-permute-done.19.refs_3_, ...), custom_call_target="tpu_custom_call" | custom-call | flops 1207959552 | bytes 9437184 | tf_op jit(solution)/shard_map/pallas_call | solution.py:261
  70.8 3.6 %collective-permute-done.20.refs_2_ = bf16[1536,128]{1,0:T(8,128)(2,1)S(1)} collective-permute-done((bf16[1536,128]{1,0:T(8,128)(2,1)S(1)}, bf16[1536,128]{1,0:T(8,128)(2,1)S(1)}, u32[]{:S(2)}, u32[]{:S(2)}) %collective-permute-start.20) | collective-permute-done | bytes 393248 | tf_op jit(solution)/shard_map/ppermute | solution.py:279
  74.4 1.3 collective-permute-done.21.refs_3_
  76.2 1.6 collective-permute-start.24
  78.2 5.4 %shard_map.79.refs_6_ = f32[768,128]{1,0:T(8,128)S(1)} custom-call(s32[9]{0:T(128)S(1)} %pad_add_fusion.info_ref.refs_0_, bf16[1,768,24576]{2,1,0:T(8,128)(2,1)} %refs_1_.23, bf16[1536,128]{1,0:T(8,128)(2,1)S(1)} %collective-permute-done.20.refs_2_, bf16[1536,128]{1,0:T(8,128)(2,1)S(1)} %collective-permute-done.21.refs_3_, ...), custom_call_target="tpu_custom_call" | custom-call | flops 1207959552 | bytes 9437184 | tf_op jit(solution)/shard_map/pallas_call | solution.py:261
  83.6 3.6 %collective-permute-done.24.front_ref.refs_2_ = bf16[1536,128]{1,0:T(8,128)(2,1)S(1)} collective-permute-done((bf16[1536,128]{1,0:T(8,128)(2,1)S(1)}, bf16[1536,128]{1,0:T(8,128)(2,1)S(1)}, u32[]{:S(2)}, u32[]{:S(2)}) %collective-permute-start.24) | collective-permute-done | bytes 393248 | tf_op jit(solution)/shard_map/ppermute | solution.py:279
  87.2 1.3 collective-permute-done.25.back_ref.refs_3_
  89.0 1.6 collective-permute-start.28
  91.1 5.6 %shard_map.81.refs_4_ = f32[768,128]{1,0:T(8,128)S(1)} custom-call(s32[9]{0:T(128)S(1)} %pad_add_fusion.info_ref.refs_0_, bf16[1,768,24576]{2,1,0:T(8,128)(2,1)} %refs_1_.23, bf16[1536,128]{1,0:T(8,128)(2,1)S(1)} %collective-permute-done.24.front_ref.refs_2_, bf16[1536,128]{1,0:T(8,128)(2,1)S(1)} %collective-permute-done.25.back_ref.refs_3_, ...), custom_call_target="tpu_custom_call" | custom-call | flops 1207959552 | bytes 9437184 | tf_op jit(solution)/shard_map/pallas_call | solution.py:261
  97.6 2.8 %shard_map.82.refs_4_ = f32[768,128]{1,0:T(8,128)S(1)} custom-call(s32[9]{0:T(128)S(1)} %pad_add_fusion.info_ref.refs_0_, bf16[1,768,24576]{2,1,0:T(8,128)(2,1)} %refs_1_.23, bf16[768,128]{1,0:T(8,128)(2,1)S(1)} %collective-permute-done.28.refs_2_, bf16[768,128]{1,0:T(8,128)(2,1)S(1)} %collective-permute-done.29.refs_3_, f32[768,128]{1,0:T(8,128)S(1)} %shard_map.81.refs_4_), custom_call_target="tpu_custom_call" | custom-call | flops 301989888 | bytes 2359296 | tf_op jit(solution)/shard_map/pallas_call | solution.py:261
  100.5 2.8 %shard_map.83.kept_ref.refs_7_ = bf16[768,128]{1,0:T(8,128)(2,1)S(1)} custom-call(s32[9]{0:T(128)S(1)} %pad_add_fusion.info_ref.refs_0_, bf16[1,768,24576]{2,1,0:T(8,128)(2,1)} %refs_1_.23, bf16[768,128]{1,0:T(8,128)(2,1)S(1)} %collective-permute-done.32.refs_2_, bf16[768,128]{1,0:T(8,128)(2,1)S(1)} %collective-permute-done.33.refs_3_, ...), custom_call_target="tpu_custom_call" | custom-call | flops 301989888 | bytes 2359296 | tf_op jit(solution)/shard_map/pallas_call | solution.py:261
  103.4 1.4 collective-permute-done.34.swapped_ref
  105.9 1.5 collective-permute-start.35
  107.5 2.8 %collective-permute-done.36.refs_3_ = bf16[384,128]{1,0:T(8,128)(2,1)S(1)} collective-permute-done((bf16[384,128]{1,0:T(8,128)(2,1)S(1)}, bf16[384,128]{1,0:T(8,128)(2,1)S(1)}, u32[]{:S(2)}, u32[]{:S(2)}) %collective-permute-start.36) | collective-permute-done | bytes 98336 | tf_op jit(solution)/shard_map/ppermute | solution.py:279
  110.8 1.5 collective-permute-start.37
  112.3 2.6 %collective-permute-done.38.refs_5_ = bf16[384,128]{1,0:T(8,128)(2,1)S(1)} collective-permute-done((bf16[384,128]{1,0:T(8,128)(2,1)S(1)}, bf16[384,128]{1,0:T(8,128)(2,1)S(1)}, u32[]{:S(2)}, u32[]{:S(2)}) %collective-permute-start.38) | collective-permute-done | bytes 98336 | tf_op jit(solution)/shard_map/ppermute | solution.py:279
  115.4 1.5 collective-permute-start.39
  117.4 2.1 %collective-permute-done.40.back_ref.refs_7_ = bf16[384,128]{1,0:T(8,128)(2,1)S(1)} collective-permute-done((bf16[384,128]{1,0:T(8,128)(2,1)S(1)}, bf16[384,128]{1,0:T(8,128)(2,1)S(1)}, u32[]{:S(2)}, u32[]{:S(2)}) %collective-permute-start.40) | collective-permute-done | bytes 98336 | tf_op jit(solution)/shard_map/ppermute | solution.py:279
  120.0 1.6 collective-permute-start.41
  122.4 1.9 collective-permute-done.41.refs_8_
  124.2 1.7 collective-permute-done.42.refs_9_
  125.9 1.2 collective-permute-done.51.refs_18_
  127.2 9.6 %shard_map.86 = (bf16[6144,128]{1,0:T(8,128)(2,1)S(1)}, bf16[1536,128]{1,0:T(8,128)(2,1)S(1)}) custom-call(s32[9]{0:T(128)S(1)} %pad_add_fusion.info_ref.refs_0_, f32[3072,128]{1,0:T(8,128)S(1)} %broadcast_in_dim.24.bias_ref, bf16[1,3072,6144]{2,1,0:T(8,128)(2,1)} %w_ref.7, f32[6144,128]{1,0:T(8,128)S(1)} %broadcast_in_dim.22.refs_0_, ...), custom_call_target="tpu_custom_call" | custom-call | flops 2415919104 | bytes 18874368 | tf_op jit(solution)/shard_map/pallas_call | solution.py:138
  137.0 8.5 %shard_map.87.here_ref.refs_2_ = bf16[1536,128]{1,0:T(8,128)(2,1)S(1)} custom-call(s32[9]{0:T(128)S(1)} %pad_add_fusion.info_ref.refs_0_, f32[3072,128]{1,0:T(8,128)S(1)} %broadcast_in_dim.24.bias_ref, bf16[1,3072,6144]{2,1,0:T(8,128)(2,1)} %w_ref.7, bf16[6144,128]{1,0:T(8,128)(2,1)S(1)} %get-tuple-element.86.refs_0_), custom_call_target="tpu_custom_call" | custom-call | flops 2415919104 | bytes 18874368 | tf_op jit(solution)/shard_map/pallas_call | solution.py:134
  146.6 1.5 collective-permute-start.53
  148.2 3.7 %shard_map.89.refs_6_ = f32[768,128]{1,0:T(8,128)S(1)} custom-call(s32[9]{0:T(128)S(1)} %pad_add_fusion.info_ref.refs_0_, bf16[1,768,24576]{2,1,0:T(8,128)(2,1)} %refs_1_.23, bf16[1536,128]{1,0:T(8,128)(2,1)S(1)} %shard_map.87.here_ref.refs_2_, bf16[1536,128]{1,0:T(8,128)(2,1)S(1)} %get-tuple-element.87.refs_3_), custom_call_target="tpu_custom_call" | custom-call | flops 603979776 | bytes 4718592 | tf_op jit(solution)/shard_map/pallas_call | solution.py:261
  151.8 5.7 %collective-permute-done.54.refs_3_ = bf16[1536,128]{1,0:T(8,128)(2,1)S(1)} collective-permute-done((bf16[1536,128]{1,0:T(8,128)(2,1)S(1)}, bf16[1536,128]{1,0:T(8,128)(2,1)S(1)}, u32[]{:S(2)}, u32[]{:S(2)}) %collective-permute-start.54) | collective-permute-done | bytes 393248 | tf_op jit(solution)/shard_map/ppermute | solution.py:279
  158.2 1.5 collective-permute-start.55
  160.3 5.4 %shard_map.90.refs_6_ = f32[768,128]{1,0:T(8,128)S(1)} custom-call(s32[9]{0:T(128)S(1)} %pad_add_fusion.info_ref.refs_0_, bf16[1,768,24576]{2,1,0:T(8,128)(2,1)} %refs_1_.23, bf16[1536,128]{1,0:T(8,128)(2,1)S(1)} %collective-permute-done.53.refs_2_, bf16[1536,128]{1,0:T(8,128)(2,1)S(1)} %collective-permute-done.54.refs_3_, ...), custom_call_target="tpu_custom_call" | custom-call | flops 1207959552 | bytes 9437184 | tf_op jit(solution)/shard_map/pallas_call | solution.py:261
  165.7 3.6 %collective-permute-done.55.refs_2_ = bf16[1536,128]{1,0:T(8,128)(2,1)S(1)} collective-permute-done((bf16[1536,128]{1,0:T(8,128)(2,1)S(1)}, bf16[1536,128]{1,0:T(8,128)(2,1)S(1)}, u32[]{:S(2)}, u32[]{:S(2)}) %collective-permute-start.55) | collective-permute-done | bytes 393248 | tf_op jit(solution)/shard_map/ppermute | solution.py:279
  169.3 1.2 collective-permute-done.56.refs_3_
  171.0 1.0 collective-permute-start.59
  172.0 1.0 collective-permute-start.60
  173.0 5.4 %shard_map.91.refs_6_ = f32[768,128]{1,0:T(8,128)S(1)} custom-call(s32[9]{0:T(128)S(1)} %pad_add_fusion.info_ref.refs_0_, bf16[1,768,24576]{2,1,0:T(8,128)(2,1)} %refs_1_.23, bf16[1536,128]{1,0:T(8,128)(2,1)S(1)} %collective-permute-done.55.refs_2_, bf16[1536,128]{1,0:T(8,128)(2,1)S(1)} %collective-permute-done.56.refs_3_, ...), custom_call_target="tpu_custom_call" | custom-call | flops 1207959552 | bytes 9437184 | tf_op jit(solution)/shard_map/pallas_call | solution.py:261
  178.5 3.6 %collective-permute-done.59.front_ref.refs_2_ = bf16[1536,128]{1,0:T(8,128)(2,1)S(1)} collective-permute-done((bf16[1536,128]{1,0:T(8,128)(2,1)S(1)}, bf16[1536,128]{1,0:T(8,128)(2,1)S(1)}, u32[]{:S(2)}, u32[]{:S(2)}) %collective-permute-start.59) | collective-permute-done | bytes 393248 | tf_op jit(solution)/shard_map/ppermute | solution.py:279
  182.0 0.7 collective-permute-done.60.back_ref.refs_3_
  183.9 1.5 collective-permute-start.64
  185.4 5.6 %shard_map.93.refs_4_ = f32[768,128]{1,0:T(8,128)S(1)} custom-call(s32[9]{0:T(128)S(1)} %pad_add_fusion.info_ref.refs_0_, bf16[1,768,24576]{2,1,0:T(8,128)(2,1)} %refs_1_.23, bf16[1536,128]{1,0:T(8,128)(2,1)S(1)} %collective-permute-done.59.front_ref.refs_2_, bf16[1536,128]{1,0:T(8,128)(2,1)S(1)} %collective-permute-done.60.back_ref.refs_3_, ...), custom_call_target="tpu_custom_call" | custom-call | flops 1207959552 | bytes 9437184 | tf_op jit(solution)/shard_map/pallas_call | solution.py:261
  191.6 2.8 %shard_map.94.refs_4_ = f32[768,128]{1,0:T(8,128)S(1)} custom-call(s32[9]{0:T(128)S(1)} %pad_add_fusion.info_ref.refs_0_, bf16[1,768,24576]{2,1,0:T(8,128)(2,1)} %refs_1_.23, bf16[768,128]{1,0:T(8,128)(2,1)S(1)} %collective-permute-done.63.refs_2_, bf16[768,128]{1,0:T(8,128)(2,1)S(1)} %collective-permute-done.64.refs_3_, f32[768,128]{1,0:T(8,128)S(1)} %shard_map.93.refs_4_), custom_call_target="tpu_custom_call" | custom-call | flops 301989888 | bytes 2359296 | tf_op jit(solution)/shard_map/pallas_call | solution.py:261
  194.4 3.7 %shard_map.95 = bf16[128,768]{1,0:T(8,128)(2,1)} custom-call(s32[9]{0:T(128)S(1)} %pad_add_fusion.info_ref.refs_0_, bf16[1,768,24576]{2,1,0:T(8,128)(2,1)} %refs_1_.23, bf16[768,128]{1,0:T(8,128)(2,1)S(1)} %collective-permute-done.67.refs_2_, bf16[768,128]{1,0:T(8,128)(2,1)S(1)} %collective-permute-done.68.refs_3_, f32[768,128]{1,0:T(8,128)S(1)} %shard_map.94.refs_4_, ...), custom_call_target="tpu_custom_call" | custom-call | flops 301989888 | bytes 2359296 | tf_op jit(solution)/shard_map/pallas_call | solution.py:261
  (108 shorter events, 16.5 us)
Async XLA Ops:
  1.0 6.0 %collective-permute-start.1 = (bf16[384,128]{1,0:T(8,128)(2,1)S(1)}, bf16[384,128]{1,0:T(8,128)(2,1)}, u32[]{:S(2)}, u32[]{:S(2)}) collective-permute-start(bf16[384,128]{1,0:T(8,128)(2,1)S(1)} %bitcast.13), channel_id=1, source_target_pairs={{0,2},{4,0},{8,4},{12,8},{14,12},{10,14},{6,10},{2,6},{1,3},{5,1},... | collective-permute-start | bytes 294920 | tf_op jit(solution)/shard_map/ppermute | solution.py:279
  4.1 4.7 %collective-permute-start = (bf16[384,128]{1,0:T(8,128)(2,1)S(1)}, bf16[384,128]{1,0:T(8,128)(2,1)}, u32[]{:S(2)}, u32[]{:S(2)}) collective-permute-start(bf16[384,128]{1,0:T(8,128)(2,1)S(1)} %bitcast.14), channel_id=1, source_target_pairs={{0,4},{4,8},{8,12},{12,14},{14,10},{10,6},{6,2},{2,0},{1,5},{5,9},... | collective-permute-start | bytes 294920 | tf_op jit(solution)/shard_map/ppermute | solution.py:279
  8.8 4.9 %collective-permute-start.2 = (bf16[384,128]{1,0:T(8,128)(2,1)}, bf16[384,128]{1,0:T(8,128)(2,1)}, u32[]{:S(2)}, u32[]{:S(2)}) collective-permute-start(bf16[384,128]{1,0:T(8,128)(2,1)} %collective-permute-done.refs_2_), channel_id=1, source_target_pairs={{0,4},{4,8},{8,12},{12,14},{14,10},{10,6},{6,2},{2,0},{1,5},{5,9},... | collective-permute-start | bytes 294920 | tf_op jit(solution)/shard_map/ppermute | solution.py:279
  8.9 4.9 %collective-permute-start.3 = (bf16[384,128]{1,0:T(8,128)(2,1)}, bf16[384,128]{1,0:T(8,128)(2,1)}, u32[]{:S(2)}, u32[]{:S(2)}) collective-permute-start(bf16[384,128]{1,0:T(8,128)(2,1)} %collective-permute-done.1.refs_3_), channel_id=1, source_target_pairs={{0,2},{4,0},{8,4},{12,8},{14,12},{10,14},{6,10},{2,6},{1,3},{5,1},... | collective-permute-start | bytes 294920 | tf_op jit(solution)/shard_map/ppermute | solution.py:279
  15.5 4.9 %collective-permute-start.4 = (bf16[384,128]{1,0:T(8,128)(2,1)}, bf16[384,128]{1,0:T(8,128)(2,1)S(1)}, u32[]{:S(2)}, u32[]{:S(2)}) collective-permute-start(bf16[384,128]{1,0:T(8,128)(2,1)} %collective-permute-done.2.refs_4_), channel_id=1, source_target_pairs={{0,4},{4,8},{8,12},{12,14},{14,10},{10,6},{6,2},{2,0},{1,5},{5,9},... | collective-permute-start | bytes 294920 | tf_op jit(solution)/shard_map/ppermute | solution.py:279
  17.5 4.9 %collective-permute-start.5 = (bf16[384,128]{1,0:T(8,128)(2,1)}, bf16[384,128]{1,0:T(8,128)(2,1)}, u32[]{:S(2)}, u32[]{:S(2)}) collective-permute-start(bf16[384,128]{1,0:T(8,128)(2,1)} %collective-permute-done.3.refs_5_), channel_id=1, source_target_pairs={{0,2},{4,0},{8,4},{12,8},{14,12},{10,14},{6,10},{2,6},{1,3},{5,1},... | collective-permute-start | bytes 294920 | tf_op jit(solution)/shard_map/ppermute | solution.py:279
  17.5 7.1 %collective-permute-start.8 = (bf16[384,128]{1,0:T(8,128)(2,1)S(1)}, bf16[384,128]{1,0:T(8,128)(2,1)}, u32[]{:S(2)}, u32[]{:S(2)}) collective-permute-start(bf16[384,128]{1,0:T(8,128)(2,1)S(1)} %bitcast.15), channel_id=1, source_target_pairs={{0,16},{16,0},{1,17},{17,1},{2,18},{18,2},{3,19},{19,3},{4,20},{20... | collective-permute-start | bytes 294920 | tf_op jit(solution)/shard_map/ppermute | solution.py:282
  17.5 8.8 %collective-permute-start.9 = (bf16[384,128]{1,0:T(8,128)(2,1)}, bf16[384,128]{1,0:T(8,128)(2,1)}, u32[]{:S(2)}, u32[]{:S(2)}) collective-permute-start(bf16[384,128]{1,0:T(8,128)(2,1)} %collective-permute-done.refs_2_), channel_id=1, source_target_pairs={{0,16},{16,0},{1,17},{17,1},{2,18},{18,2},{3,19},{19,3},{4,20},{20... | collective-permute-start | bytes 294920 | tf_op jit(solution)/shard_map/ppermute | solution.py:282
  18.0 8.7 %collective-permute-start.10 = (bf16[384,128]{1,0:T(8,128)(2,1)}, bf16[384,128]{1,0:T(8,128)(2,1)}, u32[]{:S(2)}, u32[]{:S(2)}) collective-permute-start(bf16[384,128]{1,0:T(8,128)(2,1)} %collective-permute-done.1.refs_3_), channel_id=1, source_target_pairs={{0,16},{16,0},{1,17},{17,1},{2,18},{18,2},{3,19},{19,3},{4,20},{20... | collective-permute-start | bytes 294920 | tf_op jit(solution)/shard_map/ppermute | solution.py:282
  20.3 6.4 %collective-permute-start.11 = (bf16[384,128]{1,0:T(8,128)(2,1)}, bf16[384,128]{1,0:T(8,128)(2,1)}, u32[]{:S(2)}, u32[]{:S(2)}) collective-permute-start(bf16[384,128]{1,0:T(8,128)(2,1)} %collective-permute-done.2.refs_4_), channel_id=1, source_target_pairs={{0,16},{16,0},{1,17},{17,1},{2,18},{18,2},{3,19},{19,3},{4,20},{20... | collective-permute-start | bytes 294920 | tf_op jit(solution)/shard_map/ppermute | solution.py:282
  22.4 8.0 %collective-permute-start.12 = (bf16[384,128]{1,0:T(8,128)(2,1)}, bf16[384,128]{1,0:T(8,128)(2,1)S(1)}, u32[]{:S(2)}, u32[]{:S(2)}) collective-permute-start(bf16[384,128]{1,0:T(8,128)(2,1)} %collective-permute-done.3.refs_5_), channel_id=1, source_target_pairs={{0,16},{16,0},{1,17},{17,1},{2,18},{18,2},{3,19},{19,3},{4,20},{20... | collective-permute-start | bytes 294920 | tf_op jit(solution)/shard_map/ppermute | solution.py:282
  24.7 4.2 %collective-permute-start.6 = (bf16[192,128]{1,0:T(8,128)(2,1)S(1)}, bf16[192,128]{1,0:T(8,128)(2,1)S(1)}, u32[]{:S(2)}, u32[]{:S(2)}) collective-permute-start(bf16[192,128]{1,0:T(8,128)(2,1)S(1)} %get-tuple-element.63), channel_id=1, source_target_pairs={{0,4},{4,8},{8,12},{12,14},{14,10},{10,6},{6,2},{2,0},{1,5},{5,9},... | collective-permute-start | bytes 147464 | tf_op jit(solution)/shard_map/ppermute | solution.py:279
  26.3 4.1 %collective-permute-start.7 = (bf16[192,128]{1,0:T(8,128)(2,1)S(1)}, bf16[192,128]{1,0:T(8,128)(2,1)S(1)}, u32[]{:S(2)}, u32[]{:S(2)}) collective-permute-start(bf16[192,128]{1,0:T(8,128)(2,1)S(1)} %get-tuple-element.64), channel_id=1, source_target_pairs={{0,2},{4,0},{8,4},{12,8},{14,12},{10,14},{6,10},{2,6},{1,3},{5,1},... | collective-permute-start | bytes 147464 | tf_op jit(solution)/shard_map/ppermute | solution.py:279
  26.7 4.9 %collective-permute-start.13 = (bf16[384,128]{1,0:T(8,128)(2,1)S(1)}, bf16[384,128]{1,0:T(8,128)(2,1)S(1)}, u32[]{:S(2)}, u32[]{:S(2)}) collective-permute-start(bf16[384,128]{1,0:T(8,128)(2,1)S(1)} %collective-permute-done.4.front_ref.refs_6_), channel_id=1, source_target_pairs={{0,16},{16,0},{1,17},{17,1},{2,18},{18,2},{3,19},{19,3},{4,20},{20... | collective-permute-start | bytes 294920 | tf_op jit(solution)/shard_map/ppermute | solution.py:282
  26.7 4.9 %collective-permute-start.14 = (bf16[384,128]{1,0:T(8,128)(2,1)}, bf16[384,128]{1,0:T(8,128)(2,1)S(1)}, u32[]{:S(2)}, u32[]{:S(2)}) collective-permute-start(bf16[384,128]{1,0:T(8,128)(2,1)} %collective-permute-done.5.back_ref.refs_7_), channel_id=1, source_target_pairs={{0,16},{16,0},{1,17},{17,1},{2,18},{18,2},{3,19},{19,3},{4,20},{20... | collective-permute-start | bytes 294920 | tf_op jit(solution)/shard_map/ppermute | solution.py:282
  41.9 8.7 %collective-permute-start.17 = (bf16[1536,128]{1,0:T(8,128)(2,1)S(1)}, bf16[1536,128]{1,0:T(8,128)(2,1)S(1)}, u32[]{:S(2)}, u32[]{:S(2)}) collective-permute-start(bf16[1536,128]{1,0:T(8,128)(2,1)S(1)} %get-tuple-element.66.refs_3_), channel_id=1, source_target_pairs={{0,16},{16,0},{1,17},{17,1},{2,18},{18,2},{3,19},{19,3},{4,20},{20... | collective-permute-start | bytes 1179656 | tf_op jit(solution)/shard_map/ppermute | solution.py:282
  51.2 11.4 %collective-permute-start.19 = (bf16[1536,128]{1,0:T(8,128)(2,1)S(1)}, bf16[1536,128]{1,0:T(8,128)(2,1)S(1)}, u32[]{:S(2)}, u32[]{:S(2)}) collective-permute-start(bf16[1536,128]{1,0:T(8,128)(2,1)S(1)} %shard_map.76), channel_id=1, source_target_pairs={{0,2},{4,0},{8,4},{12,8},{14,12},{10,14},{6,10},{2,6},{1,3},{5,1},... | collective-permute-start | bytes 1179656 | tf_op jit(solution)/shard_map/ppermute | solution.py:279
  51.7 11.1 %collective-permute-start.18 = (bf16[1536,128]{1,0:T(8,128)(2,1)S(1)}, bf16[1536,128]{1,0:T(8,128)(2,1)S(1)}, u32[]{:S(2)}, u32[]{:S(2)}) collective-permute-start(bf16[1536,128]{1,0:T(8,128)(2,1)S(1)} %shard_map.76), channel_id=1, source_target_pairs={{0,4},{4,8},{8,12},{12,14},{14,10},{10,6},{6,2},{2,0},{1,5},{5,9},... | collective-permute-start | bytes 1179656 | tf_op jit(solution)/shard_map/ppermute | solution.py:279
  62.8 2.5 %collective-permute-start.22 = (bf16[1536,128]{1,0:T(8,128)(2,1)S(1)}, bf16[1536,128]{1,0:T(8,128)(2,1)S(1)}, u32[]{:S(2)}, u32[]{:S(2)}) collective-permute-start(bf16[1536,128]{1,0:T(8,128)(2,1)S(1)} %collective-permute-done.18.refs_2_), channel_id=1, source_target_pairs={{0,16},{16,0},{1,17},{17,1},{2,18},{18,2},{3,19},{19,3},{4,20},{20... | collective-permute-start | bytes 1179656 | tf_op jit(solution)/shard_map/ppermute | solution.py:282
  62.8 2.5 %collective-permute-start.23 = (bf16[1536,128]{1,0:T(8,128)(2,1)S(1)}, bf16[1536,128]{1,0:T(8,128)(2,1)S(1)}, u32[]{:S(2)}, u32[]{:S(2)}) collective-permute-start(bf16[1536,128]{1,0:T(8,128)(2,1)S(1)} %collective-permute-done.19.refs_3_), channel_id=1, source_target_pairs={{0,16},{16,0},{1,17},{17,1},{2,18},{18,2},{3,19},{19,3},{4,20},{20... | collective-permute-start | bytes 1179656 | tf_op jit(solution)/shard_map/ppermute | solution.py:282
  63.3 11.0 %collective-permute-start.20 = (bf16[1536,128]{1,0:T(8,128)(2,1)S(1)}, bf16[1536,128]{1,0:T(8,128)(2,1)S(1)}, u32[]{:S(2)}, u32[]{:S(2)}) collective-permute-start(bf16[1536,128]{1,0:T(8,128)(2,1)S(1)} %collective-permute-done.18.refs_2_), channel_id=1, source_target_pairs={{0,4},{4,8},{8,12},{12,14},{14,10},{10,6},{6,2},{2,0},{1,5},{5,9},... | collective-permute-start | bytes 1179656 | tf_op jit(solution)/shard_map/ppermute | solution.py:279
  64.9 10.7 %collective-permute-start.21 = (bf16[1536,128]{1,0:T(8,128)(2,1)S(1)}, bf16[1536,128]{1,0:T(8,128)(2,1)S(1)}, u32[]{:S(2)}, u32[]{:S(2)}) collective-permute-start(bf16[1536,128]{1,0:T(8,128)(2,1)S(1)} %collective-permute-done.19.refs_3_), channel_id=1, source_target_pairs={{0,2},{4,0},{8,4},{12,8},{14,12},{10,14},{6,10},{2,6},{1,3},{5,1},... | collective-permute-start | bytes 1179656 | tf_op jit(solution)/shard_map/ppermute | solution.py:279
  75.7 2.5 %collective-permute-start.26 = (bf16[1536,128]{1,0:T(8,128)(2,1)S(1)}, bf16[1536,128]{1,0:T(8,128)(2,1)S(1)}, u32[]{:S(2)}, u32[]{:S(2)}) collective-permute-start(bf16[1536,128]{1,0:T(8,128)(2,1)S(1)} %collective-permute-done.20.refs_2_), channel_id=1, source_target_pairs={{0,16},{16,0},{1,17},{17,1},{2,18},{18,2},{3,19},{19,3},{4,20},{20... | collective-permute-start | bytes 1179656 | tf_op jit(solution)/shard_map/ppermute | solution.py:282
  75.7 2.5 %collective-permute-start.27 = (bf16[1536,128]{1,0:T(8,128)(2,1)S(1)}, bf16[1536,128]{1,0:T(8,128)(2,1)S(1)}, u32[]{:S(2)}, u32[]{:S(2)}) collective-permute-start(bf16[1536,128]{1,0:T(8,128)(2,1)S(1)} %collective-permute-done.21.refs_3_), channel_id=1, source_target_pairs={{0,16},{16,0},{1,17},{17,1},{2,18},{18,2},{3,19},{19,3},{4,20},{20... | collective-permute-start | bytes 1179656 | tf_op jit(solution)/shard_map/ppermute | solution.py:282
  76.2 11.0 %collective-permute-start.24 = (bf16[1536,128]{1,0:T(8,128)(2,1)S(1)}, bf16[1536,128]{1,0:T(8,128)(2,1)S(1)}, u32[]{:S(2)}, u32[]{:S(2)}) collective-permute-start(bf16[1536,128]{1,0:T(8,128)(2,1)S(1)} %collective-permute-done.20.refs_2_), channel_id=1, source_target_pairs={{0,4},{4,8},{8,12},{12,14},{14,10},{10,6},{6,2},{2,0},{1,5},{5,9},... | collective-permute-start | bytes 1179656 | tf_op jit(solution)/shard_map/ppermute | solution.py:279
  77.8 10.7 %collective-permute-start.25 = (bf16[1536,128]{1,0:T(8,128)(2,1)S(1)}, bf16[1536,128]{1,0:T(8,128)(2,1)S(1)}, u32[]{:S(2)}, u32[]{:S(2)}) collective-permute-start(bf16[1536,128]{1,0:T(8,128)(2,1)S(1)} %collective-permute-done.21.refs_3_), channel_id=1, source_target_pairs={{0,2},{4,0},{8,4},{12,8},{14,12},{10,14},{6,10},{2,6},{1,3},{5,1},... | collective-permute-start | bytes 1179656 | tf_op jit(solution)/shard_map/ppermute | solution.py:279
  88.5 2.6 %collective-permute-start.30 = (bf16[1536,128]{1,0:T(8,128)(2,1)S(1)}, bf16[1536,128]{1,0:T(8,128)(2,1)S(1)}, u32[]{:S(2)}, u32[]{:S(2)}) collective-permute-start(bf16[1536,128]{1,0:T(8,128)(2,1)S(1)} %collective-permute-done.24.front_ref.refs_2_), channel_id=1, source_target_pairs={{0,16},{16,0},{1,17},{17,1},{2,18},{18,2},{3,19},{19,3},{4,20},{20... | collective-permute-start | bytes 1179656 | tf_op jit(solution)/shard_map/ppermute | solution.py:282
  88.5 2.6 %collective-permute-start.31 = (bf16[1536,128]{1,0:T(8,128)(2,1)S(1)}, bf16[1536,128]{1,0:T(8,128)(2,1)S(1)}, u32[]{:S(2)}, u32[]{:S(2)}) collective-permute-start(bf16[1536,128]{1,0:T(8,128)(2,1)S(1)} %collective-permute-done.25.back_ref.refs_3_), channel_id=1, source_target_pairs={{0,16},{16,0},{1,17},{17,1},{2,18},{18,2},{3,19},{19,3},{4,20},{20... | collective-permute-start | bytes 1179656 | tf_op jit(solution)/shard_map/ppermute | solution.py:282
  89.0 7.7 %collective-permute-start.28 = (bf16[768,128]{1,0:T(8,128)(2,1)S(1)}, bf16[768,128]{1,0:T(8,128)(2,1)S(1)}, u32[]{:S(2)}, u32[]{:S(2)}) collective-permute-start(bf16[768,128]{1,0:T(8,128)(2,1)S(1)} %get-tuple-element.75), channel_id=1, source_target_pairs={{0,4},{4,8},{8,12},{12,14},{14,10},{10,6},{6,2},{2,0},{1,5},{5,9},... | collective-permute-start | bytes 589832 | tf_op jit(solution)/shard_map/ppermute | solution.py:279
  90.6 6.5 %collective-permute-start.29 = (bf16[768,128]{1,0:T(8,128)(2,1)S(1)}, bf16[768,128]{1,0:T(8,128)(2,1)S(1)}, u32[]{:S(2)}, u32[]{:S(2)}) collective-permute-start(bf16[768,128]{1,0:T(8,128)(2,1)S(1)} %get-tuple-element.76), channel_id=1, source_target_pairs={{0,2},{4,0},{8,4},{12,8},{14,12},{10,14},{6,10},{2,6},{1,3},{5,1},... | collective-permute-start | bytes 589832 | tf_op jit(solution)/shard_map/ppermute | solution.py:279
  97.1 3.3 %collective-permute-start.32 = (bf16[768,128]{1,0:T(8,128)(2,1)S(1)}, bf16[768,128]{1,0:T(8,128)(2,1)S(1)}, u32[]{:S(2)}, u32[]{:S(2)}) collective-permute-start(bf16[768,128]{1,0:T(8,128)(2,1)S(1)} %collective-permute-done.28.refs_2_), channel_id=1, source_target_pairs={{0,16},{16,0},{1,17},{17,1},{2,18},{18,2},{3,19},{19,3},{4,20},{20... | collective-permute-start | bytes 589832 | tf_op jit(solution)/shard_map/ppermute | solution.py:282
  97.1 3.3 %collective-permute-start.33 = (bf16[768,128]{1,0:T(8,128)(2,1)S(1)}, bf16[768,128]{1,0:T(8,128)(2,1)S(1)}, u32[]{:S(2)}, u32[]{:S(2)}) collective-permute-start(bf16[768,128]{1,0:T(8,128)(2,1)S(1)} %collective-permute-done.29.refs_3_), channel_id=1, source_target_pairs={{0,16},{16,0},{1,17},{17,1},{2,18},{18,2},{3,19},{19,3},{4,20},{20... | collective-permute-start | bytes 589832 | tf_op jit(solution)/shard_map/ppermute | solution.py:282
  105.4 4.9 %collective-permute-start.36 = (bf16[384,128]{1,0:T(8,128)(2,1)S(1)}, bf16[384,128]{1,0:T(8,128)(2,1)S(1)}, u32[]{:S(2)}, u32[]{:S(2)}) collective-permute-start(bf16[384,128]{1,0:T(8,128)(2,1)S(1)} %get-tuple-element.83.refs_1_), channel_id=1, source_target_pairs={{0,2},{4,0},{8,4},{12,8},{14,12},{10,14},{6,10},{2,6},{1,3},{5,1},... | collective-permute-start | bytes 294920 | tf_op jit(solution)/shard_map/ppermute | solution.py:279
  105.9 4.8 %collective-permute-start.35 = (bf16[384,128]{1,0:T(8,128)(2,1)S(1)}, bf16[384,128]{1,0:T(8,128)(2,1)S(1)}, u32[]{:S(2)}, u32[]{:S(2)}) collective-permute-start(bf16[384,128]{1,0:T(8,128)(2,1)S(1)} %get-tuple-element.83.refs_1_), channel_id=1, source_target_pairs={{0,4},{4,8},{8,12},{12,14},{14,10},{10,6},{6,2},{2,0},{1,5},{5,9},... | collective-permute-start | bytes 294920 | tf_op jit(solution)/shard_map/ppermute | solution.py:279
  110.3 4.6 %collective-permute-start.38 = (bf16[384,128]{1,0:T(8,128)(2,1)S(1)}, bf16[384,128]{1,0:T(8,128)(2,1)S(1)}, u32[]{:S(2)}, u32[]{:S(2)}) collective-permute-start(bf16[384,128]{1,0:T(8,128)(2,1)S(1)} %collective-permute-done.36.refs_3_), channel_id=1, source_target_pairs={{0,2},{4,0},{8,4},{12,8},{14,12},{10,14},{6,10},{2,6},{1,3},{5,1},... | collective-permute-start | bytes 294920 | tf_op jit(solution)/shard_map/ppermute | solution.py:279
  110.8 4.6 %collective-permute-start.37 = (bf16[384,128]{1,0:T(8,128)(2,1)S(1)}, bf16[384,128]{1,0:T(8,128)(2,1)S(1)}, u32[]{:S(2)}, u32[]{:S(2)}) collective-permute-start(bf16[384,128]{1,0:T(8,128)(2,1)S(1)} %collective-permute-done.35.refs_2_), channel_id=1, source_target_pairs={{0,4},{4,8},{8,12},{12,14},{14,10},{10,6},{6,2},{2,0},{1,5},{5,9},... | collective-permute-start | bytes 294920 | tf_op jit(solution)/shard_map/ppermute | solution.py:279
  114.9 4.6 %collective-permute-start.40 = (bf16[384,128]{1,0:T(8,128)(2,1)S(1)}, bf16[384,128]{1,0:T(8,128)(2,1)S(1)}, u32[]{:S(2)}, u32[]{:S(2)}) collective-permute-start(bf16[384,128]{1,0:T(8,128)(2,1)S(1)} %collective-permute-done.38.refs_5_), channel_id=1, source_target_pairs={{0,2},{4,0},{8,4},{12,8},{14,12},{10,14},{6,10},{2,6},{1,3},{5,1},... | collective-permute-start | bytes 294920 | tf_op jit(solution)/shard_map/ppermute | solution.py:279
  115.4 4.6 %collective-permute-start.39 = (bf16[384,128]{1,0:T(8,128)(2,1)S(1)}, bf16[384,128]{1,0:T(8,128)(2,1)S(1)}, u32[]{:S(2)}, u32[]{:S(2)}) collective-permute-start(bf16[384,128]{1,0:T(8,128)(2,1)S(1)} %collective-permute-done.37.refs_4_), channel_id=1, source_target_pairs={{0,4},{4,8},{8,12},{12,14},{14,10},{10,6},{6,2},{2,0},{1,5},{5,9},... | collective-permute-start | bytes 294920 | tf_op jit(solution)/shard_map/ppermute | solution.py:279
  116.9 3.1 %collective-permute-start.43 = (bf16[384,128]{1,0:T(8,128)(2,1)S(1)}, bf16[384,128]{1,0:T(8,128)(2,1)S(1)}, u32[]{:S(2)}, u32[]{:S(2)}) collective-permute-start(bf16[384,128]{1,0:T(8,128)(2,1)S(1)} %get-tuple-element.83.refs_1_), channel_id=1, source_target_pairs={{0,16},{16,0},{1,17},{17,1},{2,18},{18,2},{3,19},{19,3},{4,20},{20... | collective-permute-start | bytes 294920 | tf_op jit(solution)/shard_map/ppermute | solution.py:282
  116.9 4.7 %collective-permute-start.45 = (bf16[384,128]{1,0:T(8,128)(2,1)S(1)}, bf16[384,128]{1,0:T(8,128)(2,1)S(1)}, u32[]{:S(2)}, u32[]{:S(2)}) collective-permute-start(bf16[384,128]{1,0:T(8,128)(2,1)S(1)} %collective-permute-done.36.refs_3_), channel_id=1, source_target_pairs={{0,16},{16,0},{1,17},{17,1},{2,18},{18,2},{3,19},{19,3},{4,20},{20... | collective-permute-start | bytes 294920 | tf_op jit(solution)/shard_map/ppermute | solution.py:282
  117.4 4.4 %collective-permute-start.44 = (bf16[384,128]{1,0:T(8,128)(2,1)S(1)}, bf16[384,128]{1,0:T(8,128)(2,1)S(1)}, u32[]{:S(2)}, u32[]{:S(2)}) collective-permute-start(bf16[384,128]{1,0:T(8,128)(2,1)S(1)} %collective-permute-done.35.refs_2_), channel_id=1, source_target_pairs={{0,16},{16,0},{1,17},{17,1},{2,18},{18,2},{3,19},{19,3},{4,20},{20... | collective-permute-start | bytes 294920 | tf_op jit(solution)/shard_map/ppermute | solution.py:282
  119.5 2.8 %collective-permute-start.47 = (bf16[384,128]{1,0:T(8,128)(2,1)S(1)}, bf16[384,128]{1,0:T(8,128)(2,1)S(1)}, u32[]{:S(2)}, u32[]{:S(2)}) collective-permute-start(bf16[384,128]{1,0:T(8,128)(2,1)S(1)} %collective-permute-done.38.refs_5_), channel_id=1, source_target_pairs={{0,16},{16,0},{1,17},{17,1},{2,18},{18,2},{3,19},{19,3},{4,20},{20... | collective-permute-start | bytes 294920 | tf_op jit(solution)/shard_map/ppermute | solution.py:282
  120.0 5.9 %collective-permute-start.46 = (bf16[384,128]{1,0:T(8,128)(2,1)S(1)}, bf16[384,128]{1,0:T(8,128)(2,1)S(1)}, u32[]{:S(2)}, u32[]{:S(2)}) collective-permute-start(bf16[384,128]{1,0:T(8,128)(2,1)S(1)} %collective-permute-done.37.refs_4_), channel_id=1, source_target_pairs={{0,16},{16,0},{1,17},{17,1},{2,18},{18,2},{3,19},{19,3},{4,20},{20... | collective-permute-start | bytes 294920 | tf_op jit(solution)/shard_map/ppermute | solution.py:282
  120.0 4.2 %collective-permute-start.41 = (bf16[192,128]{1,0:T(8,128)(2,1)S(1)}, bf16[192,128]{1,0:T(8,128)(2,1)S(1)}, u32[]{:S(2)}, u32[]{:S(2)}) collective-permute-start(bf16[192,128]{1,0:T(8,128)(2,1)S(1)} %get-tuple-element.84), channel_id=1, source_target_pairs={{0,4},{4,8},{8,12},{12,14},{14,10},{10,6},{6,2},{2,0},{1,5},{5,9},... | collective-permute-start | bytes 147464 | tf_op jit(solution)/shard_map/ppermute | solution.py:279
  121.6 4.3 %collective-permute-start.49 = (bf16[384,128]{1,0:T(8,128)(2,1)S(1)}, bf16[384,128]{1,0:T(8,128)(2,1)S(1)}, u32[]{:S(2)}, u32[]{:S(2)}) collective-permute-start(bf16[384,128]{1,0:T(8,128)(2,1)S(1)} %collective-permute-done.40.back_ref.refs_7_), channel_id=1, source_target_pairs={{0,16},{16,0},{1,17},{17,1},{2,18},{18,2},{3,19},{19,3},{4,20},{20... | collective-permute-start | bytes 294920 | tf_op jit(solution)/shard_map/ppermute | solution.py:282
  121.8 4.1 %collective-permute-start.42 = (bf16[192,128]{1,0:T(8,128)(2,1)S(1)}, bf16[192,128]{1,0:T(8,128)(2,1)S(1)}, u32[]{:S(2)}, u32[]{:S(2)}) collective-permute-start(bf16[192,128]{1,0:T(8,128)(2,1)S(1)} %get-tuple-element.85), channel_id=1, source_target_pairs={{0,2},{4,0},{8,4},{12,8},{14,12},{10,14},{6,10},{2,6},{1,3},{5,1},... | collective-permute-start | bytes 147464 | tf_op jit(solution)/shard_map/ppermute | solution.py:279
  122.3 4.8 %collective-permute-start.48 = (bf16[384,128]{1,0:T(8,128)(2,1)S(1)}, bf16[384,128]{1,0:T(8,128)(2,1)S(1)}, u32[]{:S(2)}, u32[]{:S(2)}) collective-permute-start(bf16[384,128]{1,0:T(8,128)(2,1)S(1)} %collective-permute-done.39.front_ref.refs_6_), channel_id=1, source_target_pairs={{0,16},{16,0},{1,17},{17,1},{2,18},{18,2},{3,19},{19,3},{4,20},{20... | collective-permute-start | bytes 294920 | tf_op jit(solution)/shard_map/ppermute | solution.py:282
  136.7 8.8 %collective-permute-start.52 = (bf16[1536,128]{1,0:T(8,128)(2,1)S(1)}, bf16[1536,128]{1,0:T(8,128)(2,1)S(1)}, u32[]{:S(2)}, u32[]{:S(2)}) collective-permute-start(bf16[1536,128]{1,0:T(8,128)(2,1)S(1)} %get-tuple-element.87.refs_3_), channel_id=1, source_target_pairs={{0,16},{16,0},{1,17},{17,1},{2,18},{18,2},{3,19},{19,3},{4,20},{20... | collective-permute-start | bytes 1179656 | tf_op jit(solution)/shard_map/ppermute | solution.py:282
  146.1 11.4 %collective-permute-start.54 = (bf16[1536,128]{1,0:T(8,128)(2,1)S(1)}, bf16[1536,128]{1,0:T(8,128)(2,1)S(1)}, u32[]{:S(2)}, u32[]{:S(2)}) collective-permute-start(bf16[1536,128]{1,0:T(8,128)(2,1)S(1)} %shard_map.88), channel_id=1, source_target_pairs={{0,2},{4,0},{8,4},{12,8},{14,12},{10,14},{6,10},{2,6},{1,3},{5,1},... | collective-permute-start | bytes 1179656 | tf_op jit(solution)/shard_map/ppermute | solution.py:279
  146.6 11.1 %collective-permute-start.53 = (bf16[1536,128]{1,0:T(8,128)(2,1)S(1)}, bf16[1536,128]{1,0:T(8,128)(2,1)S(1)}, u32[]{:S(2)}, u32[]{:S(2)}) collective-permute-start(bf16[1536,128]{1,0:T(8,128)(2,1)S(1)} %shard_map.88), channel_id=1, source_target_pairs={{0,4},{4,8},{8,12},{12,14},{14,10},{10,6},{6,2},{2,0},{1,5},{5,9},... | collective-permute-start | bytes 1179656 | tf_op jit(solution)/shard_map/ppermute | solution.py:279
  157.7 2.5 %collective-permute-start.57 = (bf16[1536,128]{1,0:T(8,128)(2,1)S(1)}, bf16[1536,128]{1,0:T(8,128)(2,1)S(1)}, u32[]{:S(2)}, u32[]{:S(2)}) collective-permute-start(bf16[1536,128]{1,0:T(8,128)(2,1)S(1)} %collective-permute-done.53.refs_2_), channel_id=1, source_target_pairs={{0,16},{16,0},{1,17},{17,1},{2,18},{18,2},{3,19},{19,3},{4,20},{20... | collective-permute-start | bytes 1179656 | tf_op jit(solution)/shard_map/ppermute | solution.py:282
  157.7 2.5 %collective-permute-start.58 = (bf16[1536,128]{1,0:T(8,128)(2,1)S(1)}, bf16[1536,128]{1,0:T(8,128)(2,1)S(1)}, u32[]{:S(2)}, u32[]{:S(2)}) collective-permute-start(bf16[1536,128]{1,0:T(8,128)(2,1)S(1)} %collective-permute-done.54.refs_3_), channel_id=1, source_target_pairs={{0,16},{16,0},{1,17},{17,1},{2,18},{18,2},{3,19},{19,3},{4,20},{20... | collective-permute-start | bytes 1179656 | tf_op jit(solution)/shard_map/ppermute | solution.py:282
  158.2 11.0 %collective-permute-start.55 = (bf16[1536,128]{1,0:T(8,128)(2,1)S(1)}, bf16[1536,128]{1,0:T(8,128)(2,1)S(1)}, u32[]{:S(2)}, u32[]{:S(2)}) collective-permute-start(bf16[1536,128]{1,0:T(8,128)(2,1)S(1)} %collective-permute-done.53.refs_2_), channel_id=1, source_target_pairs={{0,4},{4,8},{8,12},{12,14},{14,10},{10,6},{6,2},{2,0},{1,5},{5,9},... | collective-permute-start | bytes 1179656 | tf_op jit(solution)/shard_map/ppermute | solution.py:279
  159.8 10.7 %collective-permute-start.56 = (bf16[1536,128]{1,0:T(8,128)(2,1)S(1)}, bf16[1536,128]{1,0:T(8,128)(2,1)S(1)}, u32[]{:S(2)}, u32[]{:S(2)}) collective-permute-start(bf16[1536,128]{1,0:T(8,128)(2,1)S(1)} %collective-permute-done.54.refs_3_), channel_id=1, source_target_pairs={{0,2},{4,0},{8,4},{12,8},{14,12},{10,14},{6,10},{2,6},{1,3},{5,1},... | collective-permute-start | bytes 1179656 | tf_op jit(solution)/shard_map/ppermute | solution.py:279
  170.5 2.5 %collective-permute-start.61 = (bf16[1536,128]{1,0:T(8,128)(2,1)S(1)}, bf16[1536,128]{1,0:T(8,128)(2,1)S(1)}, u32[]{:S(2)}, u32[]{:S(2)}) collective-permute-start(bf16[1536,128]{1,0:T(8,128)(2,1)S(1)} %collective-permute-done.55.refs_2_), channel_id=1, source_target_pairs={{0,16},{16,0},{1,17},{17,1},{2,18},{18,2},{3,19},{19,3},{4,20},{20... | collective-permute-start | bytes 1179656 | tf_op jit(solution)/shard_map/ppermute | solution.py:282
  170.5 2.5 %collective-permute-start.62 = (bf16[1536,128]{1,0:T(8,128)(2,1)S(1)}, bf16[1536,128]{1,0:T(8,128)(2,1)S(1)}, u32[]{:S(2)}, u32[]{:S(2)}) collective-permute-start(bf16[1536,128]{1,0:T(8,128)(2,1)S(1)} %collective-permute-done.56.refs_3_), channel_id=1, source_target_pairs={{0,16},{16,0},{1,17},{17,1},{2,18},{18,2},{3,19},{19,3},{4,20},{20... | collective-permute-start | bytes 1179656 | tf_op jit(solution)/shard_map/ppermute | solution.py:282
  171.0 11.0 %collective-permute-start.59 = (bf16[1536,128]{1,0:T(8,128)(2,1)S(1)}, bf16[1536,128]{1,0:T(8,128)(2,1)S(1)}, u32[]{:S(2)}, u32[]{:S(2)}) collective-permute-start(bf16[1536,128]{1,0:T(8,128)(2,1)S(1)} %collective-permute-done.55.refs_2_), channel_id=1, source_target_pairs={{0,4},{4,8},{8,12},{12,14},{14,10},{10,6},{6,2},{2,0},{1,5},{5,9},... | collective-permute-start | bytes 1179656 | tf_op jit(solution)/shard_map/ppermute | solution.py:279
  172.0 10.7 %collective-permute-start.60 = (bf16[1536,128]{1,0:T(8,128)(2,1)S(1)}, bf16[1536,128]{1,0:T(8,128)(2,1)S(1)}, u32[]{:S(2)}, u32[]{:S(2)}) collective-permute-start(bf16[1536,128]{1,0:T(8,128)(2,1)S(1)} %collective-permute-done.56.refs_3_), channel_id=1, source_target_pairs={{0,2},{4,0},{8,4},{12,8},{14,12},{10,14},{6,10},{2,6},{1,3},{5,1},... | collective-permute-start | bytes 1179656 | tf_op jit(solution)/shard_map/ppermute | solution.py:279
  182.8 2.6 %collective-permute-start.65 = (bf16[1536,128]{1,0:T(8,128)(2,1)S(1)}, bf16[1536,128]{1,0:T(8,128)(2,1)S(1)}, u32[]{:S(2)}, u32[]{:S(2)}) collective-permute-start(bf16[1536,128]{1,0:T(8,128)(2,1)S(1)} %collective-permute-done.59.front_ref.refs_2_), channel_id=1, source_target_pairs={{0,16},{16,0},{1,17},{17,1},{2,18},{18,2},{3,19},{19,3},{4,20},{20... | collective-permute-start | bytes 1179656 | tf_op jit(solution)/shard_map/ppermute | solution.py:282
  182.8 2.6 %collective-permute-start.66 = (bf16[1536,128]{1,0:T(8,128)(2,1)S(1)}, bf16[1536,128]{1,0:T(8,128)(2,1)S(1)}, u32[]{:S(2)}, u32[]{:S(2)}) collective-permute-start(bf16[1536,128]{1,0:T(8,128)(2,1)S(1)} %collective-permute-done.60.back_ref.refs_3_), channel_id=1, source_target_pairs={{0,16},{16,0},{1,17},{17,1},{2,18},{18,2},{3,19},{19,3},{4,20},{20... | collective-permute-start | bytes 1179656 | tf_op jit(solution)/shard_map/ppermute | solution.py:282
  183.3 7.7 %collective-permute-start.63 = (bf16[768,128]{1,0:T(8,128)(2,1)S(1)}, bf16[768,128]{1,0:T(8,128)(2,1)S(1)}, u32[]{:S(2)}, u32[]{:S(2)}) collective-permute-start(bf16[768,128]{1,0:T(8,128)(2,1)S(1)} %get-tuple-element.96), channel_id=1, source_target_pairs={{0,4},{4,8},{8,12},{12,14},{14,10},{10,6},{6,2},{2,0},{1,5},{5,9},... | collective-permute-start | bytes 589832 | tf_op jit(solution)/shard_map/ppermute | solution.py:279
  183.9 7.2 %collective-permute-start.64 = (bf16[768,128]{1,0:T(8,128)(2,1)S(1)}, bf16[768,128]{1,0:T(8,128)(2,1)S(1)}, u32[]{:S(2)}, u32[]{:S(2)}) collective-permute-start(bf16[768,128]{1,0:T(8,128)(2,1)S(1)} %get-tuple-element.97), channel_id=1, source_target_pairs={{0,2},{4,0},{8,4},{12,8},{14,12},{10,14},{6,10},{2,6},{1,3},{5,1},... | collective-permute-start | bytes 589832 | tf_op jit(solution)/shard_map/ppermute | solution.py:279
  191.0 3.4 %collective-permute-start.67 = (bf16[768,128]{1,0:T(8,128)(2,1)S(1)}, bf16[768,128]{1,0:T(8,128)(2,1)S(1)}, u32[]{:S(2)}, u32[]{:S(2)}) collective-permute-start(bf16[768,128]{1,0:T(8,128)(2,1)S(1)} %collective-permute-done.63.refs_2_), channel_id=1, source_target_pairs={{0,16},{16,0},{1,17},{17,1},{2,18},{18,2},{3,19},{19,3},{4,20},{20... | collective-permute-start | bytes 589832 | tf_op jit(solution)/shard_map/ppermute | solution.py:282
  191.1 3.3 %collective-permute-start.68 = (bf16[768,128]{1,0:T(8,128)(2,1)S(1)}, bf16[768,128]{1,0:T(8,128)(2,1)S(1)}, u32[]{:S(2)}, u32[]{:S(2)}) collective-permute-start(bf16[768,128]{1,0:T(8,128)(2,1)S(1)} %collective-permute-done.64.refs_3_), channel_id=1, source_target_pairs={{0,16},{16,0},{1,17},{17,1},{2,18},{18,2},{3,19},{19,3},{4,20},{20... | collective-permute-start | bytes 589832 | tf_op jit(solution)/shard_map/ppermute | solution.py:282
  (6 other events, 27.5 us)
where the time goes:
time: 199 us; the launch traced here: 198 us
  Pallas kernels  91.9 us (46%)
  waiting for transfers between devices  59.6 us (30%)
  starting transfers between devices  40.4 us (20%)
  local copies, waits for them, and re-layouts  5.75 us (3%)
    ppermute x32, waiting for transfers between devices, hop(): lax.ppermute(value, 'tp', [(ring[at], ring[(at + steps) % n]) for at in r...  55.7 us
    pallas_call x12, Pallas kernels, second_matmul(): pallas(kernel, out, [SM, ANY] + [VM] * (len(args) - 2), VM, scratch, **cost)  52.3 us
    ppermute x32, starting transfers between devices, hop(): lax.ppermute(value, 'tp', [(ring[at], ring[(at + steps) % n]) for at in r...  33.9 us
    pallas_call x2, Pallas kernels, first_matmul(): return call(info, bias, w, gain, *pieces)  19.8 us
    pallas_call x2, Pallas kernels, first_matmul(): pallas(kernel, out, [SM, VM, ANY, VM], VM, scratch, **cost)  17 us
    ppermute x37, starting transfers between devices, swap(): return lax.ppermute(value, 'segment', [(0, 1), (1, 0)])  6.45 us
  transfers between devices with their start and end apart: 69, of which 30 were waited for; matrix products, arithmetic and copies ran while one was open for 2% of the time, Pallas kernels for 32%

commit v1 on v0

--- a/solution.py
+++ b/solution.py
@@ -12,6 +12,7 @@
 VM = pl.BlockSpec(memory_space=pltpu.VMEM)
 SM = pl.BlockSpec(memory_space=pltpu.SMEM)
 ANY = pl.BlockSpec(memory_space=pl.ANY)
+CHUNKS = 1
 
 
 def shifted(value, axis, steps):
@@ -84,73 +85,107 @@
         out_ref[rows, :] = value.astype(jnp.bfloat16)
 
 
-def first_kernel(offset, tile, slots, layout, info_ref, bias_ref, w_ref, *refs):
-    out_ref, buf, sems = refs[-3:]
-    rows = out_ref.shape[0]
-    steps = rows // tile
-
-    def copy(step, slot):
+def first_kernel(offset, held, coming, layout, info_ref, bias_ref, w_ref, *refs):
+    tile = 256
+    buf, sems = refs[-2:]
+    refs = refs[:-2]
+    if coming is not None:
+        next_buf, refs = refs[-1], refs[:-1]
+    out_ref, refs = refs[-1], refs[:-1]
+    if held:
+        block_ref, refs = refs[0], refs[1:]
+    steps = out_ref.shape[0] // tile
+    streamed = steps - held
+
+    def copy(step):
         start = pl.multiple_of(offset + step * tile, tile)
-        return pltpu.make_async_copy(w_ref.at[0, pl.ds(start, tile), :], buf.at[slot], sems.at[slot])
-
-    for step in range(min(slots, steps)):
-        copy(step, step).start()
+        return pltpu.make_async_copy(w_ref.at[0, pl.ds(start, tile), :], buf.at[step - held], sems.at[step - held])
+
+    def copy_next():
+        return pltpu.make_async_copy(w_ref.at[0, pl.ds(coming, next_buf.shape[0]), :], next_buf, sems.at[streamed])
+
+    for step in range(held, steps):
+        copy(step).start()
+    if coming is not None:
+        copy_next().start()
     if layout is None:
         normed_ref = refs[0]
     else:
-        gain_ref, pieces, normed_ref = refs[0], refs[1:-4], refs[-4]
+        gain_ref, pieces, normed_ref = refs[0], refs[1:-1], refs[-1]
         part, half, places = layout
         seg = info_ref[0]
         spots = [info_ref[1 + k] * part + row + seg * half for k, row in places]
         spots += [info_ref[1 + k] * part + row + (1 - seg) * half for k, row in places]
         normalize(pieces, spots, gain_ref, normed_ref)
 
-    def body(step, carry):
-        slot = lax.rem(step, slots)
-        copy(step, slot).wait()
+    def finish(step, weights):
         at = pl.multiple_of(step * tile, tile)
-        pre = jnp.dot(buf[slot], normed_ref[...], preferred_element_type=jnp.float32)
+        pre = jnp.dot(weights, normed_ref[...], preferred_element_type=jnp.float32)
         pre = pre + bias_ref[pl.ds(pl.multiple_of(offset + at, tile), tile), :]
         out_ref[pl.ds(at, tile), :] = jax.nn.gelu(pre, approximate=True).astype(jnp.bfloat16)
 
-        @pl.when(step + slots < steps)
-        def _():
-            copy(step + slots, slot).start()
-
-        return carry
-
-    lax.fori_loop(0, steps, body, 0)
-
-
-def first_matmul(info, bias, w, offset, rows, normed=None, gain=None, pieces=None, layout=None):
+    def at_hand(step, carry):
+        finish(step, block_ref[pl.ds(pl.multiple_of(step * tile, tile), tile), :])
+        return carry
+
+    def stream(step, carry):
+        copy(step).wait()
+        finish(step, buf[step - held])
+        return carry
+
+    if held:
+        lax.fori_loop(0, held, at_hand, 0)
+    lax.fori_loop(held, steps, stream, 0)
+    if coming is not None:
+        copy_next().wait()
+
+
+def first_matmul(info, bias, w, offset, rows, block=None, coming=None, ahead=0, normed=None, gain=None, pieces=(), layout=None):
     tile = 256
-    slots = min(6, rows // tile)
     width, tokens = w.shape[2], bias.shape[1]
-    out = jax.ShapeDtypeStruct((rows, tokens), jnp.bfloat16)
-    scratch = [pltpu.VMEM((slots, tile, width), jnp.bfloat16), pltpu.SemaphoreType.DMA((slots,))]
-    cost = dict(flops=2 * rows * width * tokens, moved=2 * rows * width)
-    if pieces is None:
-        kernel = functools.partial(first_kernel, offset, tile, slots, None)
-        return pallas(kernel, out, [SM, VM, ANY, VM], VM, scratch, **cost)(info, bias, w, normed)
-    kernel = functools.partial(first_kernel, offset, tile, slots, layout)
-    outs = [jax.ShapeDtypeStruct((width, tokens), jnp.bfloat16), out]
-    call = pallas(kernel, outs, [SM, VM, ANY, VM] + [VM] * len(pieces), [VM, VM], scratch, **cost)
-    return call(info, bias, w, gain, *pieces)
-
-
-def pick_kernel(phase, info_ref, here_ref, crossed_ref, out_ref):
+    held = 0 if block is None else block.shape[0] // tile
+    streamed = rows // tile - held
+    outs = [jax.ShapeDtypeStruct((rows, tokens), jnp.bfloat16)]
+    if layout is None:
+        args = [normed]
+    else:
+        args = [gain, *pieces]
+        outs = [jax.ShapeDtypeStruct((width, tokens), jnp.bfloat16)] + outs
+    if block is not None:
+        args = [block, *args]
+    if coming is not None:
+        outs.append(jax.ShapeDtypeStruct((ahead, width), jnp.bfloat16))
+    call = pallas(
+        functools.partial(first_kernel, offset, held, coming, layout),
+        outs,
+        [SM, VM, ANY] + [VM] * len(args),
+        [VM] * len(outs),
+        [pltpu.VMEM((streamed, tile, width), jnp.bfloat16), pltpu.SemaphoreType.DMA((streamed + 1,))],
+        flops=2 * rows * width * tokens,
+        moved=2 * rows * width,
+    )
+    results = call(info, bias, w, *args)
+    return results if len(outs) > 1 else results[0]
+
+
+def pick_kernel(phase, info_ref, here_ref, crossed_ref, *outs):
+    rows = outs[0].shape[0]
+
     @pl.when(info_ref[0] == phase)
     def _():
-        out_ref[...] = here_ref[...]
+        for number, out_ref in enumerate(outs):
+            out_ref[...] = here_ref[pl.ds(number * rows, rows), :]
 
     @pl.when(info_ref[0] != phase)
     def _():
-        out_ref[...] = crossed_ref[...]
-
-
-def pick(phase, info, here, crossed):
-    out = jax.ShapeDtypeStruct(here.shape, here.dtype)
-    return pallas(functools.partial(pick_kernel, phase), out, [SM, VM, VM], VM, limit=8)(info, here, crossed)
+        for number, out_ref in enumerate(outs):
+            out_ref[...] = crossed_ref[pl.ds(number * rows, rows), :]
+
+
+def pick(phase, info, here, crossed, count):
+    out = jax.ShapeDtypeStruct((here.shape[0] // count, here.shape[1]), here.dtype)
+    kernel = functools.partial(pick_kernel, phase)
+    return pallas(kernel, [out] * count, [SM, VM, VM], [VM] * count, limit=8)(info, here, crossed)
 
 
 def relay_kernel(info_ref, kept_ref, swapped_ref, out_ref, own_ref):
@@ -188,41 +223,64 @@
     return pallas(halve_kernel, outs, [VM, VM], [VM, VM], limit=8)(front, back)
 
 
-def second_kernel(places, first, ending, *refs):
+def column_copies(info_ref, w_ref, buf, sems, places, t, tile):
+    down = pl.ds(pl.multiple_of(t * tile, tile), tile)
+    at = 0
+    for i, (k, scale, row, rows) in enumerate(places):
+        columns = pl.ds(pl.multiple_of(info_ref[1 + k] * scale + row, 128), rows)
+        yield pltpu.make_async_copy(w_ref.at[0, down, columns], buf.at[down, pl.ds(at, rows)], sems.at[t, i])
+        at += rows
+
+
+def second_kernel(places, coming, held, first, ending, *refs):
     count = len(places)
     info_ref, w_ref = refs[:2]
     pieces, refs = refs[2 : 2 + count], refs[2 + count :]
-    buf, joined, sems = refs[-3:]
-    refs = refs[:-3]
+    if held is not None:
+        buf, refs = refs[0], refs[1:]
     if not first:
         acc_ref, refs = refs[0], refs[1:]
+    if coming:
+        next_sems, refs = refs[-1], refs[:-1]
+    if held is None:
+        buf, sems, refs = refs[-2], refs[-1], refs[:-2]
+    joined, refs = refs[-1], refs[:-1]
+    if coming:
+        next_buf, refs = refs[-1], refs[:-1]
     depth, tile = w_ref.shape[1], 256
-
-    def tile_copies(t):
-        at = 0
-        for i, (k, scale, row) in enumerate(places):
-            rows = pieces[i].shape[0]
-            down = pl.ds(pl.multiple_of(t * tile, tile), tile)
-            columns = pl.ds(pl.multiple_of(info_ref[1 + k] * scale + row, 128), rows)
-            yield pltpu.make_async_copy(w_ref.at[0, down, columns], buf.at[down, pl.ds(at, rows)], sems.at[t, i])
-            at += rows
+    tiles = depth // tile
 
     def start(t, carry):
-        for copy in tile_copies(t):
+        for copy in column_copies(info_ref, w_ref, buf, sems, places, t, tile):
             copy.start()
         return carry
 
-    lax.fori_loop(0, depth // tile, start, 0)
+    def start_next(t, carry):
+        for copy in column_copies(info_ref, w_ref, next_buf, next_sems, coming, t, tile):
+            copy.start()
+        return carry
+
+    def wait_next(t, carry):
+        for copy in column_copies(info_ref, w_ref, next_buf, next_sems, coming, t, tile):
+            copy.wait()
+        return carry
+
+    if held is None:
+        lax.fori_loop(0, tiles, start, 0)
+    if coming:
+        lax.fori_loop(0, tiles, start_next, 0)
     at = 0
     for ref in pieces:
         joined[pl.ds(at, ref.shape[0]), :] = ref[...]
         at += ref.shape[0]
+    span = pl.ds(0 if held is None else held, at)
 
     def body(t, carry):
-        for copy in tile_copies(t):
-            copy.wait()
+        if held is None:
+            for copy in column_copies(info_ref, w_ref, buf, sems, places, t, tile):
+                copy.wait()
         own = pl.ds(pl.multiple_of(t * tile, tile), tile)
-        acc = jnp.dot(buf[own, :], joined[...], preferred_element_type=jnp.float32)
+        acc = jnp.dot(buf[own, span], joined[...], preferred_element_type=jnp.float32)
         if not first:
             acc = acc_ref[own, :] + acc
         if not ending:
@@ -239,26 +297,38 @@
             out_ref[:, own] = result.T.astype(jnp.bfloat16)
         return carry
 
-    lax.fori_loop(0, depth // tile, body, 0)
-
-
-def second_matmul(info, acc, pieces, places, w, ends=()):
+    lax.fori_loop(0, tiles, body, 0)
+    if coming:
+        lax.fori_loop(0, tiles, wait_next, 0)
+
+
+def second_matmul(info, acc, pieces, places, w, coming=(), buf=None, held=None, ends=()):
     depth, tokens = w.shape[1], pieces[0].shape[1]
     total = sum(piece.shape[0] for piece in pieces)
+    ahead = sum(rows for *_, rows in coming)
     ending = max(0, len(ends) - 1)
-    args = [info, w, *pieces] + ([] if acc is None else [acc]) + list(ends)
+    args = [info, w, *pieces]
+    args += ([] if buf is None else [buf]) + ([] if acc is None else [acc]) + list(ends)
     if ending == 2:
         out = jax.ShapeDtypeStruct((tokens, depth), jnp.bfloat16)
     else:
         out = jax.ShapeDtypeStruct((depth, tokens), jnp.bfloat16 if ending else jnp.float32)
-    scratch = [
-        pltpu.VMEM((depth, total), jnp.bfloat16),
-        pltpu.VMEM((total, tokens), jnp.bfloat16),
-        pltpu.SemaphoreType.DMA((depth // 256, len(pieces))),
-    ]
-    kernel = functools.partial(second_kernel, places, acc is None, ending)
+    outs, out_specs = [out], [VM]
+    scratch = [pltpu.VMEM((total, tokens), jnp.bfloat16)]
+    if buf is None:
+        scratch += [
+            pltpu.VMEM((depth, total), jnp.bfloat16),
+            pltpu.SemaphoreType.DMA((depth // 256, len(pieces))),
+        ]
+    if coming:
+        outs.append(jax.ShapeDtypeStruct((depth, ahead), jnp.bfloat16))
+        out_specs.append(VM)
+        scratch.append(pltpu.SemaphoreType.DMA((depth // 256, len(coming))))
+    kernel = functools.partial(second_kernel, places, coming, held, acc is None, ending)
     cost = dict(flops=2 * depth * total * tokens, moved=2 * depth * total)
-    return pallas(kernel, out, [SM, ANY] + [VM] * (len(args) - 2), VM, scratch, **cost)(*args)
+    call = pallas(kernel, outs, [SM, ANY] + [VM] * (len(args) - 2), out_specs, scratch, **cost)
+    results = call(*args)
+    return results if coming else results[0]
 
 
 def ring_shards(ring, inputs, norm_gain, w_in, b_in, w_out, b_out):
@@ -281,12 +351,11 @@
     def swap(value):
         return lax.ppermute(value, "segment", [(0, 1), (1, 0)])
 
+    def over_lanes(row):
+        return jnp.broadcast_to(row[0][:, None], (row.shape[1], tokens))
+
     local = inputs[0].T
     own = lax.dynamic_slice_in_dim(inputs[0], seg * half, half, 1).T
-    gain = jnp.broadcast_to(norm_gain[0][:, None], (width, tokens))
-    bias_in = jnp.broadcast_to(b_in[0][:, None], (hidden, tokens))
-    bias_out = jnp.broadcast_to(b_out[0][:, None], (part, tokens))
-
     mid = half // 2
     x_places = [(0, 0)] + [(k, 0) for step in range(1, last) for k in (step, n - step)] + [(last, 0), (last, mid)]
 
@@ -297,35 +366,55 @@
         for step in range(1, last + 1):
             if step == last:
                 front, back = halve(front, back)
+            ready = front
             front, back = hop(front, 1), hop(back, -1)
             if phase == 0 and step == 1:
                 front, back, info, local = lax.optimization_barrier((front, back, info, local))
             if phase == 0 and step == 2:
-                front, back, gain = lax.optimization_barrier((front, back, gain))
+                _, gain = lax.optimization_barrier((ready, norm_gain))
+                front, back, gain = lax.optimization_barrier((front, back, over_lanes(gain)))
             if phase == 0 and step == 3:
-                front, back, bias_in, bias_out = lax.optimization_barrier((front, back, bias_in, bias_out))
+                _, bias_in, bias_out = lax.optimization_barrier((ready, b_in, b_out))
+                front, back, bias_in, bias_out = lax.optimization_barrier(
+                    (front, back, over_lanes(bias_in), over_lanes(bias_out))
+                )
             mine += [front, back]
             theirs += [swap(front), swap(back)]
-        normed, other = first_matmul(
-            info, bias_in, w_in, side, side, gain=gain, pieces=mine + theirs, layout=(part, half, x_places)
+        ahead = side // 3
+        layout = (part, half, x_places)
+        normed, other, block = first_matmul(
+            info, bias_in, w_in, side, side, coming=0, ahead=ahead, gain=gain, pieces=mine + theirs, layout=layout
         )
         crossed = swap(other)
-        here = first_matmul(info, bias_in, w_in, 0, side, normed=normed)
-        front = back = pick(phase, info, here, crossed)
-        acc = None
-        places, pieces = [(0, hidden, 0), (0, hidden, side)], [here, other]
+        here = first_matmul(info, bias_in, w_in, 0, side, block=block, normed=normed)
+        fronts = pick(phase, info, here, crossed, CHUNKS)
+        backs = list(fronts)
+        fronts = list(fronts)
+        chunk = side // CHUNKS
+        plans = [[(0, hidden, 0, side), (0, hidden, side, side)]]
         for step in range(1, last + 1):
-            if step == last:
-                front, back = halve(front, back)
-            front, back = hop(front, 1), hop(back, -1)
-            acc = second_matmul(info, acc, pieces, places, w_out)
-            front, back, acc = lax.optimization_barrier((front, back, acc))
-            at = side // 2 if step == last else 0
-            places = [(step, hidden, 0), (n - step, hidden, at), (step, hidden, side), (n - step, hidden, side + at)]
-            pieces = [front, back, swap(front), swap(back)]
-        acc = second_matmul(info, acc, pieces[:2], places[:2], w_out)
+            rows, at = (chunk // 2, chunk // 2) if step == last else (chunk, 0)
+            plan = []
+            for c in range(CHUNKS):
+                plan += [(step, hidden, c * chunk, rows), (n - step, hidden, c * chunk + at, rows)]
+            plans.append(plan + [(k, hidden, row + side, rows) for k, _, row, _ in plan])
+        acc = buf = held = None
+        pieces = [here, other]
+        for step in range(1, last + 1):
+            for c in range(CHUNKS):
+                if step == last:
+                    fronts[c], backs[c] = halve(fronts[c], backs[c])
+                fronts[c], backs[c] = hop(fronts[c], 1), hop(backs[c], -1)
+            acc, buf = second_matmul(info, acc, pieces, plans[step - 1], w_out, plans[step], buf, held)
+            held = 0
+            for c in range(CHUNKS):
+                fronts[c], backs[c], _ = lax.optimization_barrier((fronts[c], backs[c], acc))
+            pieces = [piece for pair in zip(fronts, backs) for piece in pair]
+            pieces += [swap(piece) for piece in pieces]
+        count = len(pieces) // 2
+        acc = second_matmul(info, acc, pieces[:count], plans[last][:count], w_out, buf=buf, held=0)
         ends = [local, bias_out] + ([] if early is None else [early])
-        result = second_matmul(info, acc, pieces[2:], places[2:], w_out, ends)
+        result = second_matmul(info, acc, pieces[count:], plans[last][count:], w_out, buf=buf, held=side, ends=ends)
         if phase == 0:
             early = result
             local, own = relay(info, early, swap(early))

time: 199 us -> 190 us (0.955)
  Pallas kernels: 91.9 us -> 80.8 us
    pallas_call x18, Pallas kernels: 90.3 us -> 79.2 us  [the longest x12 44.4 us: second_matmul(): results = call(*args)]
  transfers between devices with their start and end apart: 69 -> 69, of which waited for: 30 -> 33; matrix products, arithmetic and copies ran while one was open for 2% -> 2% of each run, Pallas kernels for 32% -> 29%
where the time goes in v1:
time: 190 us
  Pallas kernels  80.8 us (43%)
  waiting for transfers between devices  61.4 us (32%)
  starting transfers between devices  40.6 us (21%)
  local copies, waits for them, and re-layouts  5.73 us (3%)
    ppermute x32, waiting for transfers between devices, hop(): lax.ppermute(value, 'tp', [(ring[at], ring[(at + steps) % n]) for at in r...  57.4 us
    pallas_call x12, Pallas kernels, second_matmul(): results = call(*args)  44.4 us
    ppermute x32, starting transfers between devices, hop(): lax.ppermute(value, 'tp', [(ring[at], ring[(at + steps) % n]) for at in r...  33.9 us
    pallas_call x4, Pallas kernels, first_matmul(): results = call(info, bias, w, *args)  33.7 us
    ppermute x37, starting transfers between devices, swap(): return lax.ppermute(value, 'segment', [(0, 1), (1, 0)])  6.66 us
    ppermute x37, waiting for transfers between devices, swap(): return lax.ppermute(value, 'segment', [(0, 1), (1, 0)])  3.95 us
  transfers between devices with their start and end apart: 69, of which 33 were waited for; matrix products, arithmetic and copies ran while one was open for 2% of the time, Pallas kernels for 29%

profile of v1, /device:TPU:0, one launch (start us, length us, event | category | flops | bytes accessed | tf_op | source)
XLA Modules:
  0.0 189.6 jit_solution(10344328961210352548)
XLA Ops:
  0.0 0.9 constant_dynamic-slice_fusion
  1.0 3.1 %collective-permute-start = (bf16[384,128]{1,0:T(8,128)(2,1)S(1)}, bf16[384,128]{1,0:T(8,128)(2,1)}, u32[]{:S(2)}, u32[]{:S(2)}) collective-permute-start(bf16[384,128]{1,0:T(8,128)(2,1)S(1)} %bitcast.13), channel_id=1, source_target_pairs={{0,4},{4,8},{8,12},{12,14},{14,10},{10,6},{6,2},{2,0},{1,5},{5,9},... | collective-permute-start | bytes 294920 | tf_op jit(solution)/shard_map/ppermute | solution.py:349
  4.1 1.1 copy.9
  6.0 1.0 collective-permute-done.refs_2_
  7.0 1.9 collective-permute-done.1.refs_3_
  8.8 1.6 collective-permute-start.2
  10.9 2.9 %collective-permute-done.2.refs_4_ = bf16[384,128]{1,0:T(8,128)(2,1)} collective-permute-done((bf16[384,128]{1,0:T(8,128)(2,1)}, bf16[384,128]{1,0:T(8,128)(2,1)}, u32[]{:S(2)}, u32[]{:S(2)}) %collective-permute-start.2) | collective-permute-done | bytes 98336 | tf_op jit(solution)/shard_map/ppermute | solution.py:349
  13.8 1.6 collective-permute-done.3.refs_5_
  15.3 1.6 broadcast_in_dim.22.refs_0_
  16.9 1.6 collective-permute-start.4
  19.5 2.3 %collective-permute-done.4.front_ref.refs_6_ = bf16[384,128]{1,0:T(8,128)(2,1)S(1)} collective-permute-done((bf16[384,128]{1,0:T(8,128)(2,1)}, bf16[384,128]{1,0:T(8,128)(2,1)S(1)}, u32[]{:S(2)}, u32[]{:S(2)}) %collective-permute-start.4) | collective-permute-done | bytes 98336 | tf_op jit(solution)/shard_map/ppermute | solution.py:349
  22.5 1.0 collective-permute-done.5.back_ref.refs_7_
  23.5 1.2 broadcast_in_dim.24.bias_ref
  24.9 0.9 shard_map.73
  25.8 1.6 collective-permute-start.6
  28.4 1.6 collective-permute-done.6.refs_8_
  30.0 1.5 collective-permute-done.7.refs_9_
  31.4 1.2 collective-permute-done.16.refs_18_
  32.7 10.6 %shard_map.74 = (bf16[6144,128]{1,0:T(8,128)(2,1)S(1)}, bf16[1536,128]{1,0:T(8,128)(2,1)S(1)}, bf16[512,6144]{1,0:T(8,128)(2,1)S(1)}) custom-call(s32[9]{0:T(128)S(1)} %pad_add_fusion.info_ref.refs_0_, f32[3072,128]{1,0:T(8,128)S(1)} %broadcast_in_dim.24.bias_ref, bf16[1,3072,6144]{2,1,0:T(8,128)(2,1)} %w_ref.7, f32[6144,128]{1,0:T(8,128)S(1)} %broadcast_in_dim.22.refs_0_, ...), custom_call_target="tpu_custom_call" | custom-call | flops 2415919104 | bytes 18874368 | tf_op jit(solution)/shard_map/pallas_call | solution.py:167
  43.5 6.6 %shard_map.75.here_ref.refs_2_ = bf16[1536,128]{1,0:T(8,128)(2,1)S(1)} custom-call(s32[9]{0:T(128)S(1)} %pad_add_fusion.info_ref.refs_0_, f32[3072,128]{1,0:T(8,128)S(1)} %broadcast_in_dim.24.bias_ref, bf16[1,3072,6144]{2,1,0:T(8,128)(2,1)} %w_ref.7, bf16[512,6144]{1,0:T(8,128)(2,1)S(1)} %get-tuple-element.81.refs_0_, ...), custom_call_target="tpu_custom_call" | custom-call | flops 2415919104 | bytes 18874368 | tf_op jit(solution)/shard_map/pallas_call | solution.py:167
  50.7 1.2 collective-permute-start.18
  52.8 5.8 %shard_map.77 = (f32[768,128]{1,0:T(8,128)S(1)}, bf16[768,6144]{1,0:T(8,128)(2,1)S(1)}) custom-call(s32[9]{0:T(128)S(1)} %pad_add_fusion.info_ref.refs_0_, bf16[1,768,24576]{2,1,0:T(8,128)(2,1)} %refs_1_.23, bf16[1536,128]{1,0:T(8,128)(2,1)S(1)} %shard_map.75.here_ref.refs_2_, bf16[1536,128]{1,0:T(8,128)(2,1)S(1)} %get-tuple-element.83.refs_3_), custom_call_target="tpu_custom_call" | custom-call | flops 603979776 | bytes 4718592 | tf_op jit(solution)/shard_map/pallas_call | solution.py:330
  58.6 3.5 %collective-permute-done.18.refs_2_ = bf16[1536,128]{1,0:T(8,128)(2,1)S(1)} collective-permute-done((bf16[1536,128]{1,0:T(8,128)(2,1)S(1)}, bf16[1536,128]{1,0:T(8,128)(2,1)S(1)}, u32[]{:S(2)}, u32[]{:S(2)}) %collective-permute-start.18) | collective-permute-done | bytes 393248 | tf_op jit(solution)/shard_map/ppermute | solution.py:349
  64.0 1.6 collective-permute-start.21
  65.6 4.4 %shard_map.78 = (f32[768,128]{1,0:T(8,128)S(1)}, bf16[768,6144]{1,0:T(8,128)(2,1)S(1)}) custom-call(s32[9]{0:T(128)S(1)} %pad_add_fusion.info_ref.refs_0_, bf16[1,768,24576]{2,1,0:T(8,128)(2,1)} %refs_1_.23, bf16[1536,128]{1,0:T(8,128)(2,1)S(1)} %collective-permute-done.18.refs_2_, bf16[1536,128]{1,0:T(8,128)(2,1)S(1)} %collective-permute-done.19.refs_3_, ...), custom_call_target="tpu_custom_call" | custom-call | flops 1207959552 | bytes 9437184 | tf_op jit(solution)/shard_map/pallas_call | solution.py:330
  69.9 4.6 %collective-permute-done.20.refs_2_ = bf16[1536,128]{1,0:T(8,128)(2,1)S(1)} collective-permute-done((bf16[1536,128]{1,0:T(8,128)(2,1)S(1)}, bf16[1536,128]{1,0:T(8,128)(2,1)S(1)}, u32[]{:S(2)}, u32[]{:S(2)}) %collective-permute-start.20) | collective-permute-done | bytes 393248 | tf_op jit(solution)/shard_map/ppermute | solution.py:349
  75.7 1.6 collective-permute-start.25
  77.3 4.5 %shard_map.79 = (f32[768,128]{1,0:T(8,128)S(1)}, bf16[768,6144]{1,0:T(8,128)(2,1)S(1)}) custom-call(s32[9]{0:T(128)S(1)} %pad_add_fusion.info_ref.refs_0_, bf16[1,768,24576]{2,1,0:T(8,128)(2,1)} %refs_1_.23, bf16[1536,128]{1,0:T(8,128)(2,1)S(1)} %collective-permute-done.20.refs_2_, bf16[1536,128]{1,0:T(8,128)(2,1)S(1)} %collective-permute-done.21.refs_3_, ...), custom_call_target="tpu_custom_call" | custom-call | flops 1207959552 | bytes 9437184 | tf_op jit(solution)/shard_map/pallas_call | solution.py:330
  81.8 4.5 %collective-permute-done.24.front_ref.refs_2_ = bf16[1536,128]{1,0:T(8,128)(2,1)S(1)} collective-permute-done((bf16[1536,128]{1,0:T(8,128)(2,1)S(1)}, bf16[1536,128]{1,0:T(8,128)(2,1)S(1)}, u32[]{:S(2)}, u32[]{:S(2)}) %collective-permute-start.24) | collective-permute-done | bytes 393248 | tf_op jit(solution)/shard_map/ppermute | solution.py:349
  87.5 1.6 collective-permute-start.29
  89.0 3.8 %shard_map.81 = (f32[768,128]{1,0:T(8,128)S(1)}, bf16[768,3072]{1,0:T(8,128)(2,1)S(1)}) custom-call(s32[9]{0:T(128)S(1)} %pad_add_fusion.info_ref.refs_0_, bf16[1,768,24576]{2,1,0:T(8,128)(2,1)} %refs_1_.23, bf16[1536,128]{1,0:T(8,128)(2,1)S(1)} %collective-permute-done.24.front_ref.refs_2_, bf16[1536,128]{1,0:T(8,128)(2,1)S(1)} %collective-permute-done.25.back_ref.refs_3_, ...), custom_call_target="tpu_custom_call" | custom-call | flops 1207959552 | bytes 9437184 | tf_op jit(solution)/shard_map/pallas_call | solution.py:330
  92.8 1.0 collective-permute-done.28.refs_2_
  94.6 1.6 shard_map.82.refs_5_
  96.3 1.6 shard_map.83.kept_ref.refs_8_
  98.0 1.4 collective-permute-done.34.swapped_ref
  100.9 1.2 collective-permute-start.36
  102.1 2.8 %collective-permute-done.35.refs_2_ = bf16[384,128]{1,0:T(8,128)(2,1)S(1)} collective-permute-done((bf16[384,128]{1,0:T(8,128)(2,1)S(1)}, bf16[384,128]{1,0:T(8,128)(2,1)S(1)}, u32[]{:S(2)}, u32[]{:S(2)}) %collective-permute-start.35) | collective-permute-done | bytes 98336 | tf_op jit(solution)/shard_map/ppermute | solution.py:349
  105.7 1.2 collective-permute-start.38
  106.9 2.6 %collective-permute-done.37.refs_4_ = bf16[384,128]{1,0:T(8,128)(2,1)S(1)} collective-permute-done((bf16[384,128]{1,0:T(8,128)(2,1)S(1)}, bf16[384,128]{1,0:T(8,128)(2,1)S(1)}, u32[]{:S(2)}, u32[]{:S(2)}) %collective-permute-start.37) | collective-permute-done | bytes 98336 | tf_op jit(solution)/shard_map/ppermute | solution.py:349
  110.3 1.2 collective-permute-start.40
  112.1 2.1 %collective-permute-done.39.front_ref.refs_6_ = bf16[384,128]{1,0:T(8,128)(2,1)S(1)} collective-permute-done((bf16[384,128]{1,0:T(8,128)(2,1)S(1)}, bf16[384,128]{1,0:T(8,128)(2,1)S(1)}, u32[]{:S(2)}, u32[]{:S(2)}) %collective-permute-start.39) | collective-permute-done | bytes 98336 | tf_op jit(solution)/shard_map/ppermute | solution.py:349
  115.0 1.6 collective-permute-start.41
  117.6 1.6 collective-permute-done.41.refs_8_
  119.2 1.5 collective-permute-done.42.refs_9_
  120.7 1.2 collective-permute-done.51.refs_18_
  121.9 9.9 %shard_map.86 = (bf16[6144,128]{1,0:T(8,128)(2,1)S(1)}, bf16[1536,128]{1,0:T(8,128)(2,1)S(1)}, bf16[512,6144]{1,0:T(8,128)(2,1)S(1)}) custom-call(s32[9]{0:T(128)S(1)} %pad_add_fusion.info_ref.refs_0_, f32[3072,128]{1,0:T(8,128)S(1)} %broadcast_in_dim.24.bias_ref, bf16[1,3072,6144]{2,1,0:T(8,128)(2,1)} %w_ref.7, f32[6144,128]{1,0:T(8,128)S(1)} %broadcast_in_dim.22.refs_0_, ...), custom_call_target="tpu_custom_call" | custom-call | flops 2415919104 | bytes 18874368 | tf_op jit(solution)/shard_map/pallas_call | solution.py:167
  132.1 6.6 %shard_map.87.here_ref.refs_2_ = bf16[1536,128]{1,0:T(8,128)(2,1)S(1)} custom-call(s32[9]{0:T(128)S(1)} %pad_add_fusion.info_ref.refs_0_, f32[3072,128]{1,0:T(8,128)S(1)} %broadcast_in_dim.24.bias_ref, bf16[1,3072,6144]{2,1,0:T(8,128)(2,1)} %w_ref.7, bf16[512,6144]{1,0:T(8,128)(2,1)S(1)} %get-tuple-element.107.refs_0_, ...), custom_call_target="tpu_custom_call" | custom-call | flops 2415919104 | bytes 18874368 | tf_op jit(solution)/shard_map/pallas_call | solution.py:167
  139.3 1.6 collective-permute-start.53
  141.4 5.8 %shard_map.89 = (f32[768,128]{1,0:T(8,128)S(1)}, bf16[768,6144]{1,0:T(8,128)(2,1)S(1)}) custom-call(s32[9]{0:T(128)S(1)} %pad_add_fusion.info_ref.refs_0_, bf16[1,768,24576]{2,1,0:T(8,128)(2,1)} %refs_1_.23, bf16[1536,128]{1,0:T(8,128)(2,1)S(1)} %shard_map.87.here_ref.refs_2_, bf16[1536,128]{1,0:T(8,128)(2,1)S(1)} %get-tuple-element.109.refs_3_), custom_call_target="tpu_custom_call" | custom-call | flops 603979776 | bytes 4718592 | tf_op jit(solution)/shard_map/pallas_call | solution.py:330
  147.2 3.5 %collective-permute-done.53.refs_2_ = bf16[1536,128]{1,0:T(8,128)(2,1)S(1)} collective-permute-done((bf16[1536,128]{1,0:T(8,128)(2,1)S(1)}, bf16[1536,128]{1,0:T(8,128)(2,1)S(1)}, u32[]{:S(2)}, u32[]{:S(2)}) %collective-permute-start.53) | collective-permute-done | bytes 393248 | tf_op jit(solution)/shard_map/ppermute | solution.py:349
  150.7 1.3 collective-permute-done.54.refs_3_
  152.5 1.5 collective-permute-start.55
  154.5 4.4 %shard_map.90 = (f32[768,128]{1,0:T(8,128)S(1)}, bf16[768,6144]{1,0:T(8,128)(2,1)S(1)}) custom-call(s32[9]{0:T(128)S(1)} %pad_add_fusion.info_ref.refs_0_, bf16[1,768,24576]{2,1,0:T(8,128)(2,1)} %refs_1_.23, bf16[1536,128]{1,0:T(8,128)(2,1)S(1)} %collective-permute-done.53.refs_2_, bf16[1536,128]{1,0:T(8,128)(2,1)S(1)} %collective-permute-done.54.refs_3_, ...), custom_call_target="tpu_custom_call" | custom-call | flops 1207959552 | bytes 9437184 | tf_op jit(solution)/shard_map/pallas_call | solution.py:330
  158.9 4.6 %collective-permute-done.55.refs_2_ = bf16[1536,128]{1,0:T(8,128)(2,1)S(1)} collective-permute-done((bf16[1536,128]{1,0:T(8,128)(2,1)S(1)}, bf16[1536,128]{1,0:T(8,128)(2,1)S(1)}, u32[]{:S(2)}, u32[]{:S(2)}) %collective-permute-start.55) | collective-permute-done | bytes 393248 | tf_op jit(solution)/shard_map/ppermute | solution.py:349
  163.5 1.2 collective-permute-done.56.refs_3_
  165.3 1.2 collective-permute-start.59
  167.3 4.5 %shard_map.91 = (f32[768,128]{1,0:T(8,128)S(1)}, bf16[768,6144]{1,0:T(8,128)(2,1)S(1)}) custom-call(s32[9]{0:T(128)S(1)} %pad_add_fusion.info_ref.refs_0_, bf16[1,768,24576]{2,1,0:T(8,128)(2,1)} %refs_1_.23, bf16[1536,128]{1,0:T(8,128)(2,1)S(1)} %collective-permute-done.55.refs_2_, bf16[1536,128]{1,0:T(8,128)(2,1)S(1)} %collective-permute-done.56.refs_3_, ...), custom_call_target="tpu_custom_call" | custom-call | flops 1207959552 | bytes 9437184 | tf_op jit(solution)/shard_map/pallas_call | solution.py:330
  171.8 4.5 %collective-permute-done.59.front_ref.refs_2_ = bf16[1536,128]{1,0:T(8,128)(2,1)S(1)} collective-permute-done((bf16[1536,128]{1,0:T(8,128)(2,1)S(1)}, bf16[1536,128]{1,0:T(8,128)(2,1)S(1)}, u32[]{:S(2)}, u32[]{:S(2)}) %collective-permute-start.59) | collective-permute-done | bytes 393248 | tf_op jit(solution)/shard_map/ppermute | solution.py:349
  176.3 0.9 collective-permute-done.60.back_ref.refs_3_
  178.3 1.5 collective-permute-start.64
  179.8 3.8 %shard_map.93 = (f32[768,128]{1,0:T(8,128)S(1)}, bf16[768,3072]{1,0:T(8,128)(2,1)S(1)}) custom-call(s32[9]{0:T(128)S(1)} %pad_add_fusion.info_ref.refs_0_, bf16[1,768,24576]{2,1,0:T(8,128)(2,1)} %refs_1_.23, bf16[1536,128]{1,0:T(8,128)(2,1)S(1)} %collective-permute-done.59.front_ref.refs_2_, bf16[1536,128]{1,0:T(8,128)(2,1)S(1)} %collective-permute-done.60.back_ref.refs_3_, ...), custom_call_target="tpu_custom_call" | custom-call | flops 1207959552 | bytes 9437184 | tf_op jit(solution)/shard_map/pallas_call | solution.py:330
  183.6 1.0 collective-permute-done.63.refs_2_
  185.4 1.6 shard_map.94.refs_5_
  187.0 2.5 %shard_map.95 = bf16[128,768]{1,0:T(8,128)(2,1)} custom-call(s32[9]{0:T(128)S(1)} %pad_add_fusion.info_ref.refs_0_, bf16[1,768,24576]{2,1,0:T(8,128)(2,1)} %refs_1_.23, bf16[768,128]{1,0:T(8,128)(2,1)S(1)} %collective-permute-done.67.refs_2_, bf16[768,128]{1,0:T(8,128)(2,1)S(1)} %collective-permute-done.68.refs_3_, ...), custom_call_target="tpu_custom_call" | custom-call | flops 301989888 | bytes 2359296 | tf_op jit(solution)/shard_map/pallas_call | solution.py:330
  (106 shorter events, 21.9 us)
Async XLA Ops:
  1.0 5.9 %collective-permute-start = (bf16[384,128]{1,0:T(8,128)(2,1)S(1)}, bf16[384,128]{1,0:T(8,128)(2,1)}, u32[]{:S(2)}, u32[]{:S(2)}) collective-permute-start(bf16[384,128]{1,0:T(8,128)(2,1)S(1)} %bitcast.13), channel_id=1, source_target_pairs={{0,4},{4,8},{8,12},{12,14},{14,10},{10,6},{6,2},{2,0},{1,5},{5,9},... | collective-permute-start | bytes 294920 | tf_op jit(solution)/shard_map/ppermute | solution.py:349
  4.1 4.7 %collective-permute-start.1 = (bf16[384,128]{1,0:T(8,128)(2,1)S(1)}, bf16[384,128]{1,0:T(8,128)(2,1)}, u32[]{:S(2)}, u32[]{:S(2)}) collective-permute-start(bf16[384,128]{1,0:T(8,128)(2,1)S(1)} %bitcast.14), channel_id=1, source_target_pairs={{0,2},{4,0},{8,4},{12,8},{14,12},{10,14},{6,10},{2,6},{1,3},{5,1},... | collective-permute-start | bytes 294920 | tf_op jit(solution)/shard_map/ppermute | solution.py:349
  8.8 4.9 %collective-permute-start.2 = (bf16[384,128]{1,0:T(8,128)(2,1)}, bf16[384,128]{1,0:T(8,128)(2,1)}, u32[]{:S(2)}, u32[]{:S(2)}) collective-permute-start(bf16[384,128]{1,0:T(8,128)(2,1)} %collective-permute-done.refs_2_), channel_id=1, source_target_pairs={{0,4},{4,8},{8,12},{12,14},{14,10},{10,6},{6,2},{2,0},{1,5},{5,9},... | collective-permute-start | bytes 294920 | tf_op jit(solution)/shard_map/ppermute | solution.py:349
  10.4 4.9 %collective-permute-start.3 = (bf16[384,128]{1,0:T(8,128)(2,1)}, bf16[384,128]{1,0:T(8,128)(2,1)}, u32[]{:S(2)}, u32[]{:S(2)}) collective-permute-start(bf16[384,128]{1,0:T(8,128)(2,1)} %collective-permute-done.1.refs_3_), channel_id=1, source_target_pairs={{0,2},{4,0},{8,4},{12,8},{14,12},{10,14},{6,10},{2,6},{1,3},{5,1},... | collective-permute-start | bytes 294920 | tf_op jit(solution)/shard_map/ppermute | solution.py:349
  16.9 4.9 %collective-permute-start.4 = (bf16[384,128]{1,0:T(8,128)(2,1)}, bf16[384,128]{1,0:T(8,128)(2,1)S(1)}, u32[]{:S(2)}, u32[]{:S(2)}) collective-permute-start(bf16[384,128]{1,0:T(8,128)(2,1)} %collective-permute-done.2.refs_4_), channel_id=1, source_target_pairs={{0,4},{4,8},{8,12},{12,14},{14,10},{10,6},{6,2},{2,0},{1,5},{5,9},... | collective-permute-start | bytes 294920 | tf_op jit(solution)/shard_map/ppermute | solution.py:349
  18.6 4.9 %collective-permute-start.5 = (bf16[384,128]{1,0:T(8,128)(2,1)}, bf16[384,128]{1,0:T(8,128)(2,1)}, u32[]{:S(2)}, u32[]{:S(2)}) collective-permute-start(bf16[384,128]{1,0:T(8,128)(2,1)} %collective-permute-done.3.refs_5_), channel_id=1, source_target_pairs={{0,2},{4,0},{8,4},{12,8},{14,12},{10,14},{6,10},{2,6},{1,3},{5,1},... | collective-permute-start | bytes 294920 | tf_op jit(solution)/shard_map/ppermute | solution.py:349
  19.0 6.7 %collective-permute-start.8 = (bf16[384,128]{1,0:T(8,128)(2,1)S(1)}, bf16[384,128]{1,0:T(8,128)(2,1)}, u32[]{:S(2)}, u32[]{:S(2)}) collective-permute-start(bf16[384,128]{1,0:T(8,128)(2,1)S(1)} %bitcast.15), channel_id=1, source_target_pairs={{0,16},{16,0},{1,17},{17,1},{2,18},{18,2},{3,19},{19,3},{4,20},{20... | collective-permute-start | bytes 294920 | tf_op jit(solution)/shard_map/ppermute | solution.py:352
  19.0 8.3 %collective-permute-start.9 = (bf16[384,128]{1,0:T(8,128)(2,1)}, bf16[384,128]{1,0:T(8,128)(2,1)}, u32[]{:S(2)}, u32[]{:S(2)}) collective-permute-start(bf16[384,128]{1,0:T(8,128)(2,1)} %collective-permute-done.refs_2_), channel_id=1, source_target_pairs={{0,16},{16,0},{1,17},{17,1},{2,18},{18,2},{3,19},{19,3},{4,20},{20... | collective-permute-start | bytes 294920 | tf_op jit(solution)/shard_map/ppermute | solution.py:352
  19.5 8.3 %collective-permute-start.10 = (bf16[384,128]{1,0:T(8,128)(2,1)}, bf16[384,128]{1,0:T(8,128)(2,1)}, u32[]{:S(2)}, u32[]{:S(2)}) collective-permute-start(bf16[384,128]{1,0:T(8,128)(2,1)} %collective-permute-done.1.refs_3_), channel_id=1, source_target_pairs={{0,16},{16,0},{1,17},{17,1},{2,18},{18,2},{3,19},{19,3},{4,20},{20... | collective-permute-start | bytes 294920 | tf_op jit(solution)/shard_map/ppermute | solution.py:352
  21.8 6.0 %collective-permute-start.11 = (bf16[384,128]{1,0:T(8,128)(2,1)}, bf16[384,128]{1,0:T(8,128)(2,1)}, u32[]{:S(2)}, u32[]{:S(2)}) collective-permute-start(bf16[384,128]{1,0:T(8,128)(2,1)} %collective-permute-done.2.refs_4_), channel_id=1, source_target_pairs={{0,16},{16,0},{1,17},{17,1},{2,18},{18,2},{3,19},{19,3},{4,20},{20... | collective-permute-start | bytes 294920 | tf_op jit(solution)/shard_map/ppermute | solution.py:352
  23.5 7.9 %collective-permute-start.12 = (bf16[384,128]{1,0:T(8,128)(2,1)}, bf16[384,128]{1,0:T(8,128)(2,1)S(1)}, u32[]{:S(2)}, u32[]{:S(2)}) collective-permute-start(bf16[384,128]{1,0:T(8,128)(2,1)} %collective-permute-done.3.refs_5_), channel_id=1, source_target_pairs={{0,16},{16,0},{1,17},{17,1},{2,18},{18,2},{3,19},{19,3},{4,20},{20... | collective-permute-start | bytes 294920 | tf_op jit(solution)/shard_map/ppermute | solution.py:352
  25.8 4.2 %collective-permute-start.6 = (bf16[192,128]{1,0:T(8,128)(2,1)S(1)}, bf16[192,128]{1,0:T(8,128)(2,1)S(1)}, u32[]{:S(2)}, u32[]{:S(2)}) collective-permute-start(bf16[192,128]{1,0:T(8,128)(2,1)S(1)} %get-tuple-element.79), channel_id=1, source_target_pairs={{0,4},{4,8},{8,12},{12,14},{14,10},{10,6},{6,2},{2,0},{1,5},{5,9},... | collective-permute-start | bytes 147464 | tf_op jit(solution)/shard_map/ppermute | solution.py:349
  27.3 4.1 %collective-permute-start.7 = (bf16[192,128]{1,0:T(8,128)(2,1)S(1)}, bf16[192,128]{1,0:T(8,128)(2,1)S(1)}, u32[]{:S(2)}, u32[]{:S(2)}) collective-permute-start(bf16[192,128]{1,0:T(8,128)(2,1)S(1)} %get-tuple-element.80), channel_id=1, source_target_pairs={{0,2},{4,0},{8,4},{12,8},{14,12},{10,14},{6,10},{2,6},{1,3},{5,1},... | collective-permute-start | bytes 147464 | tf_op jit(solution)/shard_map/ppermute | solution.py:349
  27.9 4.8 %collective-permute-start.13 = (bf16[384,128]{1,0:T(8,128)(2,1)S(1)}, bf16[384,128]{1,0:T(8,128)(2,1)S(1)}, u32[]{:S(2)}, u32[]{:S(2)}) collective-permute-start(bf16[384,128]{1,0:T(8,128)(2,1)S(1)} %collective-permute-done.4.front_ref.refs_6_), channel_id=1, source_target_pairs={{0,16},{16,0},{1,17},{17,1},{2,18},{18,2},{3,19},{19,3},{4,20},{20... | collective-permute-start | bytes 294920 | tf_op jit(solution)/shard_map/ppermute | solution.py:352
  27.9 4.8 %collective-permute-start.14 = (bf16[384,128]{1,0:T(8,128)(2,1)}, bf16[384,128]{1,0:T(8,128)(2,1)S(1)}, u32[]{:S(2)}, u32[]{:S(2)}) collective-permute-start(bf16[384,128]{1,0:T(8,128)(2,1)} %collective-permute-done.5.back_ref.refs_7_), channel_id=1, source_target_pairs={{0,16},{16,0},{1,17},{17,1},{2,18},{18,2},{3,19},{19,3},{4,20},{20... | collective-permute-start | bytes 294920 | tf_op jit(solution)/shard_map/ppermute | solution.py:352
  43.3 6.8 %collective-permute-start.17 = (bf16[1536,128]{1,0:T(8,128)(2,1)S(1)}, bf16[1536,128]{1,0:T(8,128)(2,1)S(1)}, u32[]{:S(2)}, u32[]{:S(2)}) collective-permute-start(bf16[1536,128]{1,0:T(8,128)(2,1)S(1)} %get-tuple-element.83.refs_3_), channel_id=1, source_target_pairs={{0,16},{16,0},{1,17},{17,1},{2,18},{18,2},{3,19},{19,3},{4,20},{20... | collective-permute-start | bytes 1179656 | tf_op jit(solution)/shard_map/ppermute | solution.py:352
  50.7 11.4 %collective-permute-start.18 = (bf16[1536,128]{1,0:T(8,128)(2,1)S(1)}, bf16[1536,128]{1,0:T(8,128)(2,1)S(1)}, u32[]{:S(2)}, u32[]{:S(2)}) collective-permute-start(bf16[1536,128]{1,0:T(8,128)(2,1)S(1)} %shard_map.76), channel_id=1, source_target_pairs={{0,4},{4,8},{8,12},{12,14},{14,10},{10,6},{6,2},{2,0},{1,5},{5,9},... | collective-permute-start | bytes 1179656 | tf_op jit(solution)/shard_map/ppermute | solution.py:349
  51.9 11.1 %collective-permute-start.19 = (bf16[1536,128]{1,0:T(8,128)(2,1)S(1)}, bf16[1536,128]{1,0:T(8,128)(2,1)S(1)}, u32[]{:S(2)}, u32[]{:S(2)}) collective-permute-start(bf16[1536,128]{1,0:T(8,128)(2,1)S(1)} %shard_map.76), channel_id=1, source_target_pairs={{0,2},{4,0},{8,4},{12,8},{14,12},{10,14},{6,10},{2,6},{1,3},{5,1},... | collective-permute-start | bytes 1179656 | tf_op jit(solution)/shard_map/ppermute | solution.py:349
  63.0 2.5 %collective-permute-start.22 = (bf16[1536,128]{1,0:T(8,128)(2,1)S(1)}, bf16[1536,128]{1,0:T(8,128)(2,1)S(1)}, u32[]{:S(2)}, u32[]{:S(2)}) collective-permute-start(bf16[1536,128]{1,0:T(8,128)(2,1)S(1)} %collective-permute-done.18.refs_2_), channel_id=1, source_target_pairs={{0,16},{16,0},{1,17},{17,1},{2,18},{18,2},{3,19},{19,3},{4,20},{20... | collective-permute-start | bytes 1179656 | tf_op jit(solution)/shard_map/ppermute | solution.py:352
  63.0 2.5 %collective-permute-start.23 = (bf16[1536,128]{1,0:T(8,128)(2,1)S(1)}, bf16[1536,128]{1,0:T(8,128)(2,1)S(1)}, u32[]{:S(2)}, u32[]{:S(2)}) collective-permute-start(bf16[1536,128]{1,0:T(8,128)(2,1)S(1)} %collective-permute-done.19.refs_3_), channel_id=1, source_target_pairs={{0,16},{16,0},{1,17},{17,1},{2,18},{18,2},{3,19},{19,3},{4,20},{20... | collective-permute-start | bytes 1179656 | tf_op jit(solution)/shard_map/ppermute | solution.py:352
  63.5 11.0 %collective-permute-start.20 = (bf16[1536,128]{1,0:T(8,128)(2,1)S(1)}, bf16[1536,128]{1,0:T(8,128)(2,1)S(1)}, u32[]{:S(2)}, u32[]{:S(2)}) collective-permute-start(bf16[1536,128]{1,0:T(8,128)(2,1)S(1)} %collective-permute-done.18.refs_2_), channel_id=1, source_target_pairs={{0,4},{4,8},{8,12},{12,14},{14,10},{10,6},{6,2},{2,0},{1,5},{5,9},... | collective-permute-start | bytes 1179656 | tf_op jit(solution)/shard_map/ppermute | solution.py:349
  64.0 10.7 %collective-permute-start.21 = (bf16[1536,128]{1,0:T(8,128)(2,1)S(1)}, bf16[1536,128]{1,0:T(8,128)(2,1)S(1)}, u32[]{:S(2)}, u32[]{:S(2)}) collective-permute-start(bf16[1536,128]{1,0:T(8,128)(2,1)S(1)} %collective-permute-done.19.refs_3_), channel_id=1, source_target_pairs={{0,2},{4,0},{8,4},{12,8},{14,12},{10,14},{6,10},{2,6},{1,3},{5,1},... | collective-permute-start | bytes 1179656 | tf_op jit(solution)/shard_map/ppermute | solution.py:349
  74.7 2.5 %collective-permute-start.26 = (bf16[1536,128]{1,0:T(8,128)(2,1)S(1)}, bf16[1536,128]{1,0:T(8,128)(2,1)S(1)}, u32[]{:S(2)}, u32[]{:S(2)}) collective-permute-start(bf16[1536,128]{1,0:T(8,128)(2,1)S(1)} %collective-permute-done.20.refs_2_), channel_id=1, source_target_pairs={{0,16},{16,0},{1,17},{17,1},{2,18},{18,2},{3,19},{19,3},{4,20},{20... | collective-permute-start | bytes 1179656 | tf_op jit(solution)/shard_map/ppermute | solution.py:352
  74.7 2.5 %collective-permute-start.27 = (bf16[1536,128]{1,0:T(8,128)(2,1)S(1)}, bf16[1536,128]{1,0:T(8,128)(2,1)S(1)}, u32[]{:S(2)}, u32[]{:S(2)}) collective-permute-start(bf16[1536,128]{1,0:T(8,128)(2,1)S(1)} %collective-permute-done.21.refs_3_), channel_id=1, source_target_pairs={{0,16},{16,0},{1,17},{17,1},{2,18},{18,2},{3,19},{19,3},{4,20},{20... | collective-permute-start | bytes 1179656 | tf_op jit(solution)/shard_map/ppermute | solution.py:352
  75.2 11.0 %collective-permute-start.24 = (bf16[1536,128]{1,0:T(8,128)(2,1)S(1)}, bf16[1536,128]{1,0:T(8,128)(2,1)S(1)}, u32[]{:S(2)}, u32[]{:S(2)}) collective-permute-start(bf16[1536,128]{1,0:T(8,128)(2,1)S(1)} %collective-permute-done.20.refs_2_), channel_id=1, source_target_pairs={{0,4},{4,8},{8,12},{12,14},{14,10},{10,6},{6,2},{2,0},{1,5},{5,9},... | collective-permute-start | bytes 1179656 | tf_op jit(solution)/shard_map/ppermute | solution.py:349
  75.7 10.7 %collective-permute-start.25 = (bf16[1536,128]{1,0:T(8,128)(2,1)S(1)}, bf16[1536,128]{1,0:T(8,128)(2,1)S(1)}, u32[]{:S(2)}, u32[]{:S(2)}) collective-permute-start(bf16[1536,128]{1,0:T(8,128)(2,1)S(1)} %collective-permute-done.21.refs_3_), channel_id=1, source_target_pairs={{0,2},{4,0},{8,4},{12,8},{14,12},{10,14},{6,10},{2,6},{1,3},{5,1},... | collective-permute-start | bytes 1179656 | tf_op jit(solution)/shard_map/ppermute | solution.py:349
  86.4 2.6 %collective-permute-start.30 = (bf16[1536,128]{1,0:T(8,128)(2,1)S(1)}, bf16[1536,128]{1,0:T(8,128)(2,1)S(1)}, u32[]{:S(2)}, u32[]{:S(2)}) collective-permute-start(bf16[1536,128]{1,0:T(8,128)(2,1)S(1)} %collective-permute-done.24.front_ref.refs_2_), channel_id=1, source_target_pairs={{0,16},{16,0},{1,17},{17,1},{2,18},{18,2},{3,19},{19,3},{4,20},{20... | collective-permute-start | bytes 1179656 | tf_op jit(solution)/shard_map/ppermute | solution.py:352
  86.4 2.6 %collective-permute-start.31 = (bf16[1536,128]{1,0:T(8,128)(2,1)S(1)}, bf16[1536,128]{1,0:T(8,128)(2,1)S(1)}, u32[]{:S(2)}, u32[]{:S(2)}) collective-permute-start(bf16[1536,128]{1,0:T(8,128)(2,1)S(1)} %collective-permute-done.25.back_ref.refs_3_), channel_id=1, source_target_pairs={{0,16},{16,0},{1,17},{17,1},{2,18},{18,2},{3,19},{19,3},{4,20},{20... | collective-permute-start | bytes 1179656 | tf_op jit(solution)/shard_map/ppermute | solution.py:352
  87.0 6.9 %collective-permute-start.28 = (bf16[768,128]{1,0:T(8,128)(2,1)S(1)}, bf16[768,128]{1,0:T(8,128)(2,1)S(1)}, u32[]{:S(2)}, u32[]{:S(2)}) collective-permute-start(bf16[768,128]{1,0:T(8,128)(2,1)S(1)} %get-tuple-element.95), channel_id=1, source_target_pairs={{0,4},{4,8},{8,12},{12,14},{14,10},{10,6},{6,2},{2,0},{1,5},{5,9},... | collective-permute-start | bytes 589832 | tf_op jit(solution)/shard_map/ppermute | solution.py:349
  87.5 6.6 %collective-permute-start.29 = (bf16[768,128]{1,0:T(8,128)(2,1)S(1)}, bf16[768,128]{1,0:T(8,128)(2,1)S(1)}, u32[]{:S(2)}, u32[]{:S(2)}) collective-permute-start(bf16[768,128]{1,0:T(8,128)(2,1)S(1)} %get-tuple-element.96), channel_id=1, source_target_pairs={{0,2},{4,0},{8,4},{12,8},{14,12},{10,14},{6,10},{2,6},{1,3},{5,1},... | collective-permute-start | bytes 589832 | tf_op jit(solution)/shard_map/ppermute | solution.py:349
  94.1 2.2 %collective-permute-start.32 = (bf16[768,128]{1,0:T(8,128)(2,1)S(1)}, bf16[768,128]{1,0:T(8,128)(2,1)S(1)}, u32[]{:S(2)}, u32[]{:S(2)}) collective-permute-start(bf16[768,128]{1,0:T(8,128)(2,1)S(1)} %collective-permute-done.28.refs_2_), channel_id=1, source_target_pairs={{0,16},{16,0},{1,17},{17,1},{2,18},{18,2},{3,19},{19,3},{4,20},{20... | collective-permute-start | bytes 589832 | tf_op jit(solution)/shard_map/ppermute | solution.py:352
  94.1 2.2 %collective-permute-start.33 = (bf16[768,128]{1,0:T(8,128)(2,1)S(1)}, bf16[768,128]{1,0:T(8,128)(2,1)S(1)}, u32[]{:S(2)}, u32[]{:S(2)}) collective-permute-start(bf16[768,128]{1,0:T(8,128)(2,1)S(1)} %collective-permute-done.29.refs_3_), channel_id=1, source_target_pairs={{0,16},{16,0},{1,17},{17,1},{2,18},{18,2},{3,19},{19,3},{4,20},{20... | collective-permute-start | bytes 589832 | tf_op jit(solution)/shard_map/ppermute | solution.py:352
  100.0 4.9 %collective-permute-start.35 = (bf16[384,128]{1,0:T(8,128)(2,1)S(1)}, bf16[384,128]{1,0:T(8,128)(2,1)S(1)}, u32[]{:S(2)}, u32[]{:S(2)}) collective-permute-start(bf16[384,128]{1,0:T(8,128)(2,1)S(1)} %get-tuple-element.104.refs_1_), channel_id=1, source_target_pairs={{0,4},{4,8},{8,12},{12,14},{14,10},{10,6},{6,2},{2,0},{1,5},{5,9},... | collective-permute-start | bytes 294920 | tf_op jit(solution)/shard_map/ppermute | solution.py:349
  100.9 4.8 %collective-permute-start.36 = (bf16[384,128]{1,0:T(8,128)(2,1)S(1)}, bf16[384,128]{1,0:T(8,128)(2,1)S(1)}, u32[]{:S(2)}, u32[]{:S(2)}) collective-permute-start(bf16[384,128]{1,0:T(8,128)(2,1)S(1)} %get-tuple-element.104.refs_1_), channel_id=1, source_target_pairs={{0,2},{4,0},{8,4},{12,8},{14,12},{10,14},{6,10},{2,6},{1,3},{5,1},... | collective-permute-start | bytes 294920 | tf_op jit(solution)/shard_map/ppermute | solution.py:349
  104.9 4.6 %collective-permute-start.37 = (bf16[384,128]{1,0:T(8,128)(2,1)S(1)}, bf16[384,128]{1,0:T(8,128)(2,1)S(1)}, u32[]{:S(2)}, u32[]{:S(2)}) collective-permute-start(bf16[384,128]{1,0:T(8,128)(2,1)S(1)} %collective-permute-done.35.refs_2_), channel_id=1, source_target_pairs={{0,4},{4,8},{8,12},{12,14},{14,10},{10,6},{6,2},{2,0},{1,5},{5,9},... | collective-permute-start | bytes 294920 | tf_op jit(solution)/shard_map/ppermute | solution.py:349
  105.7 4.6 %collective-permute-start.38 = (bf16[384,128]{1,0:T(8,128)(2,1)S(1)}, bf16[384,128]{1,0:T(8,128)(2,1)S(1)}, u32[]{:S(2)}, u32[]{:S(2)}) collective-permute-start(bf16[384,128]{1,0:T(8,128)(2,1)S(1)} %collective-permute-done.36.refs_3_), channel_id=1, source_target_pairs={{0,2},{4,0},{8,4},{12,8},{14,12},{10,14},{6,10},{2,6},{1,3},{5,1},... | collective-permute-start | bytes 294920 | tf_op jit(solution)/shard_map/ppermute | solution.py:349
  109.5 4.6 %collective-permute-start.39 = (bf16[384,128]{1,0:T(8,128)(2,1)S(1)}, bf16[384,128]{1,0:T(8,128)(2,1)S(1)}, u32[]{:S(2)}, u32[]{:S(2)}) collective-permute-start(bf16[384,128]{1,0:T(8,128)(2,1)S(1)} %collective-permute-done.37.refs_4_), channel_id=1, source_target_pairs={{0,4},{4,8},{8,12},{12,14},{14,10},{10,6},{6,2},{2,0},{1,5},{5,9},... | collective-permute-start | bytes 294920 | tf_op jit(solution)/shard_map/ppermute | solution.py:349
  110.3 4.6 %collective-permute-start.40 = (bf16[384,128]{1,0:T(8,128)(2,1)S(1)}, bf16[384,128]{1,0:T(8,128)(2,1)S(1)}, u32[]{:S(2)}, u32[]{:S(2)}) collective-permute-start(bf16[384,128]{1,0:T(8,128)(2,1)S(1)} %collective-permute-done.38.refs_5_), channel_id=1, source_target_pairs={{0,2},{4,0},{8,4},{12,8},{14,12},{10,14},{6,10},{2,6},{1,3},{5,1},... | collective-permute-start | bytes 294920 | tf_op jit(solution)/shard_map/ppermute | solution.py:349
  111.5 3.4 %collective-permute-start.43 = (bf16[384,128]{1,0:T(8,128)(2,1)S(1)}, bf16[384,128]{1,0:T(8,128)(2,1)S(1)}, u32[]{:S(2)}, u32[]{:S(2)}) collective-permute-start(bf16[384,128]{1,0:T(8,128)(2,1)S(1)} %get-tuple-element.104.refs_1_), channel_id=1, source_target_pairs={{0,16},{16,0},{1,17},{17,1},{2,18},{18,2},{3,19},{19,3},{4,20},{20... | collective-permute-start | bytes 294920 | tf_op jit(solution)/shard_map/ppermute | solution.py:352
  111.5 5.1 %collective-permute-start.44 = (bf16[384,128]{1,0:T(8,128)(2,1)S(1)}, bf16[384,128]{1,0:T(8,128)(2,1)S(1)}, u32[]{:S(2)}, u32[]{:S(2)}) collective-permute-start(bf16[384,128]{1,0:T(8,128)(2,1)S(1)} %collective-permute-done.35.refs_2_), channel_id=1, source_target_pairs={{0,16},{16,0},{1,17},{17,1},{2,18},{18,2},{3,19},{19,3},{4,20},{20... | collective-permute-start | bytes 294920 | tf_op jit(solution)/shard_map/ppermute | solution.py:352
  112.1 5.0 %collective-permute-start.45 = (bf16[384,128]{1,0:T(8,128)(2,1)S(1)}, bf16[384,128]{1,0:T(8,128)(2,1)S(1)}, u32[]{:S(2)}, u32[]{:S(2)}) collective-permute-start(bf16[384,128]{1,0:T(8,128)(2,1)S(1)} %collective-permute-done.36.refs_3_), channel_id=1, source_target_pairs={{0,16},{16,0},{1,17},{17,1},{2,18},{18,2},{3,19},{19,3},{4,20},{20... | collective-permute-start | bytes 294920 | tf_op jit(solution)/shard_map/ppermute | solution.py:352
  114.1 2.9 %collective-permute-start.46 = (bf16[384,128]{1,0:T(8,128)(2,1)S(1)}, bf16[384,128]{1,0:T(8,128)(2,1)S(1)}, u32[]{:S(2)}, u32[]{:S(2)}) collective-permute-start(bf16[384,128]{1,0:T(8,128)(2,1)S(1)} %collective-permute-done.37.refs_4_), channel_id=1, source_target_pairs={{0,16},{16,0},{1,17},{17,1},{2,18},{18,2},{3,19},{19,3},{4,20},{20... | collective-permute-start | bytes 294920 | tf_op jit(solution)/shard_map/ppermute | solution.py:352
  115.0 5.8 %collective-permute-start.47 = (bf16[384,128]{1,0:T(8,128)(2,1)S(1)}, bf16[384,128]{1,0:T(8,128)(2,1)S(1)}, u32[]{:S(2)}, u32[]{:S(2)}) collective-permute-start(bf16[384,128]{1,0:T(8,128)(2,1)S(1)} %collective-permute-done.38.refs_5_), channel_id=1, source_target_pairs={{0,16},{16,0},{1,17},{17,1},{2,18},{18,2},{3,19},{19,3},{4,20},{20... | collective-permute-start | bytes 294920 | tf_op jit(solution)/shard_map/ppermute | solution.py:352
  115.0 4.2 %collective-permute-start.41 = (bf16[192,128]{1,0:T(8,128)(2,1)S(1)}, bf16[192,128]{1,0:T(8,128)(2,1)S(1)}, u32[]{:S(2)}, u32[]{:S(2)}) collective-permute-start(bf16[192,128]{1,0:T(8,128)(2,1)S(1)} %get-tuple-element.105), channel_id=1, source_target_pairs={{0,4},{4,8},{8,12},{12,14},{14,10},{10,6},{6,2},{2,0},{1,5},{5,9},... | collective-permute-start | bytes 147464 | tf_op jit(solution)/shard_map/ppermute | solution.py:349
  116.6 4.1 %collective-permute-start.42 = (bf16[192,128]{1,0:T(8,128)(2,1)S(1)}, bf16[192,128]{1,0:T(8,128)(2,1)S(1)}, u32[]{:S(2)}, u32[]{:S(2)}) collective-permute-start(bf16[192,128]{1,0:T(8,128)(2,1)S(1)} %get-tuple-element.106), channel_id=1, source_target_pairs={{0,2},{4,0},{8,4},{12,8},{14,12},{10,14},{6,10},{2,6},{1,3},{5,1},... | collective-permute-start | bytes 147464 | tf_op jit(solution)/shard_map/ppermute | solution.py:349
  117.1 4.9 %collective-permute-start.48 = (bf16[384,128]{1,0:T(8,128)(2,1)S(1)}, bf16[384,128]{1,0:T(8,128)(2,1)S(1)}, u32[]{:S(2)}, u32[]{:S(2)}) collective-permute-start(bf16[384,128]{1,0:T(8,128)(2,1)S(1)} %collective-permute-done.39.front_ref.refs_6_), channel_id=1, source_target_pairs={{0,16},{16,0},{1,17},{17,1},{2,18},{18,2},{3,19},{19,3},{4,20},{20... | collective-permute-start | bytes 294920 | tf_op jit(solution)/shard_map/ppermute | solution.py:352
  117.1 4.9 %collective-permute-start.49 = (bf16[384,128]{1,0:T(8,128)(2,1)S(1)}, bf16[384,128]{1,0:T(8,128)(2,1)S(1)}, u32[]{:S(2)}, u32[]{:S(2)}) collective-permute-start(bf16[384,128]{1,0:T(8,128)(2,1)S(1)} %collective-permute-done.40.back_ref.refs_7_), channel_id=1, source_target_pairs={{0,16},{16,0},{1,17},{17,1},{2,18},{18,2},{3,19},{19,3},{4,20},{20... | collective-permute-start | bytes 294920 | tf_op jit(solution)/shard_map/ppermute | solution.py:352
  131.9 6.8 %collective-permute-start.52 = (bf16[1536,128]{1,0:T(8,128)(2,1)S(1)}, bf16[1536,128]{1,0:T(8,128)(2,1)S(1)}, u32[]{:S(2)}, u32[]{:S(2)}) collective-permute-start(bf16[1536,128]{1,0:T(8,128)(2,1)S(1)} %get-tuple-element.109.refs_3_), channel_id=1, source_target_pairs={{0,16},{16,0},{1,17},{17,1},{2,18},{18,2},{3,19},{19,3},{4,20},{20... | collective-permute-start | bytes 1179656 | tf_op jit(solution)/shard_map/ppermute | solution.py:352
  139.3 11.4 %collective-permute-start.53 = (bf16[1536,128]{1,0:T(8,128)(2,1)S(1)}, bf16[1536,128]{1,0:T(8,128)(2,1)S(1)}, u32[]{:S(2)}, u32[]{:S(2)}) collective-permute-start(bf16[1536,128]{1,0:T(8,128)(2,1)S(1)} %shard_map.88), channel_id=1, source_target_pairs={{0,4},{4,8},{8,12},{12,14},{14,10},{10,6},{6,2},{2,0},{1,5},{5,9},... | collective-permute-start | bytes 1179656 | tf_op jit(solution)/shard_map/ppermute | solution.py:349
  140.9 11.1 %collective-permute-start.54 = (bf16[1536,128]{1,0:T(8,128)(2,1)S(1)}, bf16[1536,128]{1,0:T(8,128)(2,1)S(1)}, u32[]{:S(2)}, u32[]{:S(2)}) collective-permute-start(bf16[1536,128]{1,0:T(8,128)(2,1)S(1)} %shard_map.88), channel_id=1, source_target_pairs={{0,2},{4,0},{8,4},{12,8},{14,12},{10,14},{6,10},{2,6},{1,3},{5,1},... | collective-permute-start | bytes 1179656 | tf_op jit(solution)/shard_map/ppermute | solution.py:349
  152.0 2.5 %collective-permute-start.57 = (bf16[1536,128]{1,0:T(8,128)(2,1)S(1)}, bf16[1536,128]{1,0:T(8,128)(2,1)S(1)}, u32[]{:S(2)}, u32[]{:S(2)}) collective-permute-start(bf16[1536,128]{1,0:T(8,128)(2,1)S(1)} %collective-permute-done.53.refs_2_), channel_id=1, source_target_pairs={{0,16},{16,0},{1,17},{17,1},{2,18},{18,2},{3,19},{19,3},{4,20},{20... | collective-permute-start | bytes 1179656 | tf_op jit(solution)/shard_map/ppermute | solution.py:352
  152.0 2.5 %collective-permute-start.58 = (bf16[1536,128]{1,0:T(8,128)(2,1)S(1)}, bf16[1536,128]{1,0:T(8,128)(2,1)S(1)}, u32[]{:S(2)}, u32[]{:S(2)}) collective-permute-start(bf16[1536,128]{1,0:T(8,128)(2,1)S(1)} %collective-permute-done.54.refs_3_), channel_id=1, source_target_pairs={{0,16},{16,0},{1,17},{17,1},{2,18},{18,2},{3,19},{19,3},{4,20},{20... | collective-permute-start | bytes 1179656 | tf_op jit(solution)/shard_map/ppermute | solution.py:352
  152.5 11.0 %collective-permute-start.55 = (bf16[1536,128]{1,0:T(8,128)(2,1)S(1)}, bf16[1536,128]{1,0:T(8,128)(2,1)S(1)}, u32[]{:S(2)}, u32[]{:S(2)}) collective-permute-start(bf16[1536,128]{1,0:T(8,128)(2,1)S(1)} %collective-permute-done.53.refs_2_), channel_id=1, source_target_pairs={{0,4},{4,8},{8,12},{12,14},{14,10},{10,6},{6,2},{2,0},{1,5},{5,9},... | collective-permute-start | bytes 1179656 | tf_op jit(solution)/shard_map/ppermute | solution.py:349
  154.0 10.7 %collective-permute-start.56 = (bf16[1536,128]{1,0:T(8,128)(2,1)S(1)}, bf16[1536,128]{1,0:T(8,128)(2,1)S(1)}, u32[]{:S(2)}, u32[]{:S(2)}) collective-permute-start(bf16[1536,128]{1,0:T(8,128)(2,1)S(1)} %collective-permute-done.54.refs_3_), channel_id=1, source_target_pairs={{0,2},{4,0},{8,4},{12,8},{14,12},{10,14},{6,10},{2,6},{1,3},{5,1},... | collective-permute-start | bytes 1179656 | tf_op jit(solution)/shard_map/ppermute | solution.py:349
  164.8 2.5 %collective-permute-start.61 = (bf16[1536,128]{1,0:T(8,128)(2,1)S(1)}, bf16[1536,128]{1,0:T(8,128)(2,1)S(1)}, u32[]{:S(2)}, u32[]{:S(2)}) collective-permute-start(bf16[1536,128]{1,0:T(8,128)(2,1)S(1)} %collective-permute-done.55.refs_2_), channel_id=1, source_target_pairs={{0,16},{16,0},{1,17},{17,1},{2,18},{18,2},{3,19},{19,3},{4,20},{20... | collective-permute-start | bytes 1179656 | tf_op jit(solution)/shard_map/ppermute | solution.py:352
  164.8 2.5 %collective-permute-start.62 = (bf16[1536,128]{1,0:T(8,128)(2,1)S(1)}, bf16[1536,128]{1,0:T(8,128)(2,1)S(1)}, u32[]{:S(2)}, u32[]{:S(2)}) collective-permute-start(bf16[1536,128]{1,0:T(8,128)(2,1)S(1)} %collective-permute-done.56.refs_3_), channel_id=1, source_target_pairs={{0,16},{16,0},{1,17},{17,1},{2,18},{18,2},{3,19},{19,3},{4,20},{20... | collective-permute-start | bytes 1179656 | tf_op jit(solution)/shard_map/ppermute | solution.py:352
  165.3 11.0 %collective-permute-start.59 = (bf16[1536,128]{1,0:T(8,128)(2,1)S(1)}, bf16[1536,128]{1,0:T(8,128)(2,1)S(1)}, u32[]{:S(2)}, u32[]{:S(2)}) collective-permute-start(bf16[1536,128]{1,0:T(8,128)(2,1)S(1)} %collective-permute-done.55.refs_2_), channel_id=1, source_target_pairs={{0,4},{4,8},{8,12},{12,14},{14,10},{10,6},{6,2},{2,0},{1,5},{5,9},... | collective-permute-start | bytes 1179656 | tf_op jit(solution)/shard_map/ppermute | solution.py:349
  166.5 10.7 %collective-permute-start.60 = (bf16[1536,128]{1,0:T(8,128)(2,1)S(1)}, bf16[1536,128]{1,0:T(8,128)(2,1)S(1)}, u32[]{:S(2)}, u32[]{:S(2)}) collective-permute-start(bf16[1536,128]{1,0:T(8,128)(2,1)S(1)} %collective-permute-done.56.refs_3_), channel_id=1, source_target_pairs={{0,2},{4,0},{8,4},{12,8},{14,12},{10,14},{6,10},{2,6},{1,3},{5,1},... | collective-permute-start | bytes 1179656 | tf_op jit(solution)/shard_map/ppermute | solution.py:349
  177.2 2.6 %collective-permute-start.65 = (bf16[1536,128]{1,0:T(8,128)(2,1)S(1)}, bf16[1536,128]{1,0:T(8,128)(2,1)S(1)}, u32[]{:S(2)}, u32[]{:S(2)}) collective-permute-start(bf16[1536,128]{1,0:T(8,128)(2,1)S(1)} %collective-permute-done.59.front_ref.refs_2_), channel_id=1, source_target_pairs={{0,16},{16,0},{1,17},{17,1},{2,18},{18,2},{3,19},{19,3},{4,20},{20... | collective-permute-start | bytes 1179656 | tf_op jit(solution)/shard_map/ppermute | solution.py:352
  177.2 2.6 %collective-permute-start.66 = (bf16[1536,128]{1,0:T(8,128)(2,1)S(1)}, bf16[1536,128]{1,0:T(8,128)(2,1)S(1)}, u32[]{:S(2)}, u32[]{:S(2)}) collective-permute-start(bf16[1536,128]{1,0:T(8,128)(2,1)S(1)} %collective-permute-done.60.back_ref.refs_3_), channel_id=1, source_target_pairs={{0,16},{16,0},{1,17},{17,1},{2,18},{18,2},{3,19},{19,3},{4,20},{20... | collective-permute-start | bytes 1179656 | tf_op jit(solution)/shard_map/ppermute | solution.py:352
  177.7 6.9 %collective-permute-start.63 = (bf16[768,128]{1,0:T(8,128)(2,1)S(1)}, bf16[768,128]{1,0:T(8,128)(2,1)S(1)}, u32[]{:S(2)}, u32[]{:S(2)}) collective-permute-start(bf16[768,128]{1,0:T(8,128)(2,1)S(1)} %get-tuple-element.121), channel_id=1, source_target_pairs={{0,4},{4,8},{8,12},{12,14},{14,10},{10,6},{6,2},{2,0},{1,5},{5,9},... | collective-permute-start | bytes 589832 | tf_op jit(solution)/shard_map/ppermute | solution.py:349
  178.3 6.5 %collective-permute-start.64 = (bf16[768,128]{1,0:T(8,128)(2,1)S(1)}, bf16[768,128]{1,0:T(8,128)(2,1)S(1)}, u32[]{:S(2)}, u32[]{:S(2)}) collective-permute-start(bf16[768,128]{1,0:T(8,128)(2,1)S(1)} %get-tuple-element.122), channel_id=1, source_target_pairs={{0,2},{4,0},{8,4},{12,8},{14,12},{10,14},{6,10},{2,6},{1,3},{5,1},... | collective-permute-start | bytes 589832 | tf_op jit(solution)/shard_map/ppermute | solution.py:349
  184.9 2.2 %collective-permute-start.67 = (bf16[768,128]{1,0:T(8,128)(2,1)S(1)}, bf16[768,128]{1,0:T(8,128)(2,1)S(1)}, u32[]{:S(2)}, u32[]{:S(2)}) collective-permute-start(bf16[768,128]{1,0:T(8,128)(2,1)S(1)} %collective-permute-done.63.refs_2_), channel_id=1, source_target_pairs={{0,16},{16,0},{1,17},{17,1},{2,18},{18,2},{3,19},{19,3},{4,20},{20... | collective-permute-start | bytes 589832 | tf_op jit(solution)/shard_map/ppermute | solution.py:352
  184.9 2.2 %collective-permute-start.68 = (bf16[768,128]{1,0:T(8,128)(2,1)S(1)}, bf16[768,128]{1,0:T(8,128)(2,1)S(1)}, u32[]{:S(2)}, u32[]{:S(2)}) collective-permute-start(bf16[768,128]{1,0:T(8,128)(2,1)S(1)} %collective-permute-done.64.refs_3_), channel_id=1, source_target_pairs={{0,16},{16,0},{1,17},{17,1},{2,18},{18,2},{3,19},{19,3},{4,20},{20... | collective-permute-start | bytes 589832 | tf_op jit(solution)/shard_map/ppermute | solution.py:352
  (5 other events, 7.0 us)

commit v2 on v1

--- a/solution.py
+++ b/solution.py
@@ -356,18 +356,15 @@
 
     local = inputs[0].T
     own = lax.dynamic_slice_in_dim(inputs[0], seg * half, half, 1).T
-    mid = half // 2
-    x_places = [(0, 0)] + [(k, 0) for step in range(1, last) for k in (step, n - step)] + [(last, 0), (last, mid)]
+    x_places = [(0, 0)] + [(k, 0) for step in range(1, last) for k in (step, n - step)] + [(last, 0)]
 
     early = None
     for phase in range(2):
         front = back = own
         mine, theirs = [own], [swap(own)]
         for step in range(1, last + 1):
-            if step == last:
-                front, back = halve(front, back)
             ready = front
-            front, back = hop(front, 1), hop(back, -1)
+            front, back = hop(front, 1), hop(back, -1) if step < last else None
             if phase == 0 and step == 1:
                 front, back, info, local = lax.optimization_barrier((front, back, info, local))
             if phase == 0 and step == 2:
@@ -378,8 +375,8 @@
                 front, back, bias_in, bias_out = lax.optimization_barrier(
                     (front, back, over_lanes(bias_in), over_lanes(bias_out))
                 )
-            mine += [front, back]
-            theirs += [swap(front), swap(back)]
+            mine += [front] if step == last else [front, back]
+            theirs += [swap(front)] if step == last else [swap(front), swap(back)]
         ahead = side // 3
         layout = (part, half, x_places)
         normed, other, block = first_matmul(

time: 190 us -> 187 us (0.984)
    ppermute x32 -> x30, starting transfers between devices: 33.9 us -> 31.8 us  [hop(): lax.ppermute(value, 'tp', [(ring[at], ring[(at + steps) % n]) for at in r...]
    ppermute x37 -> x35, starting transfers between devices: 6.66 us -> 7.22 us  [swap(): return lax.ppermute(value, 'segment', [(0, 1), (1, 0)])]
    ppermute x32 -> x30, waiting for transfers between devices: 57.4 us -> 57 us  [hop(): lax.ppermute(value, 'tp', [(ring[at], ring[(at + steps) % n]) for at in r...]
    ppermute x37 -> x35, waiting for transfers between devices: 3.95 us -> 4.05 us  [swap(): return lax.ppermute(value, 'segment', [(0, 1), (1, 0)])]
  transfers between devices with their start and end apart: 69 -> 65, of which waited for: 33 -> 31; matrix products, arithmetic and copies ran while one was open for 2% -> 2% of each run, Pallas kernels for 29% -> 29%
where the time goes in v2:
time: 187 us
  Pallas kernels  79.7 us (43%)
  waiting for transfers between devices  61 us (33%)
  starting transfers between devices  39 us (21%)
  local copies, waits for them, and re-layouts  5.73 us (3%)
    ppermute x30, waiting for transfers between devices, hop(): lax.ppermute(value, 'tp', [(ring[at], ring[(at + steps) % n]) for at in r...  57 us
    pallas_call x12, Pallas kernels, second_matmul(): results = call(*args)  44.4 us
    pallas_call x4, Pallas kernels, first_matmul(): results = call(info, bias, w, *args)  33.5 us
    ppermute x30, starting transfers between devices, hop(): lax.ppermute(value, 'tp', [(ring[at], ring[(at + steps) % n]) for at in r...  31.8 us
    ppermute x35, starting transfers between devices, swap(): return lax.ppermute(value, 'segment', [(0, 1), (1, 0)])  7.22 us
    ppermute x35, waiting for transfers between devices, swap(): return lax.ppermute(value, 'segment', [(0, 1), (1, 0)])  4.05 us
  transfers between devices with their start and end apart: 65, of which 31 were waited for; matrix products, arithmetic and copies ran while one was open for 2% of the time, Pallas kernels for 29%

profile of v2, /device:TPU:0, one launch (start us, length us, event | category | flops | bytes accessed | tf_op | source)
XLA Modules:
  0.0 186.6 jit_solution(16342736439360854592)
XLA Ops:
  0.0 0.9 constant_dynamic-slice_fusion
  1.0 3.1 %collective-permute-start = (bf16[384,128]{1,0:T(8,128)(2,1)S(1)}, bf16[384,128]{1,0:T(8,128)(2,1)S(1)}, u32[]{:S(2)}, u32[]{:S(2)}) collective-permute-start(bf16[384,128]{1,0:T(8,128)(2,1)S(1)} %bitcast.13), channel_id=1, source_target_pairs={{0,4},{4,8},{8,12},{12,14},{14,10},{10,6},{6,2},{2,0},{1,5},{5,9},... | collective-permute-start | bytes 294920 | tf_op jit(solution)/shard_map/ppermute | solution.py:349
  4.1 1.1 copy.9
  5.2 0.7 dynamic-slice_bitcast_fusion
  6.0 0.9 collective-permute-done.refs_2_
  6.8 2.0 %collective-permute-done.1.refs_3_ = bf16[384,128]{1,0:T(8,128)(2,1)} collective-permute-done((bf16[384,128]{1,0:T(8,128)(2,1)S(1)}, bf16[384,128]{1,0:T(8,128)(2,1)}, u32[]{:S(2)}, u32[]{:S(2)}) %collective-permute-start.1) | collective-permute-done | bytes 98336 | tf_op jit(solution)/shard_map/ppermute | solution.py:349
  8.8 1.6 collective-permute-start.2
  10.9 2.7 %collective-permute-done.2.refs_4_ = bf16[384,128]{1,0:T(8,128)(2,1)} collective-permute-done((bf16[384,128]{1,0:T(8,128)(2,1)S(1)}, bf16[384,128]{1,0:T(8,128)(2,1)}, u32[]{:S(2)}, u32[]{:S(2)}) %collective-permute-start.2) | collective-permute-done | bytes 98336 | tf_op jit(solution)/shard_map/ppermute | solution.py:349
  13.6 1.8 collective-permute-done.3.refs_5_
  15.3 1.6 broadcast_in_dim.22.refs_0_
  16.9 1.6 collective-permute-start.4
  19.5 0.7 reduce
  20.2 1.7 collective-permute-done.4.refs_6_
  21.9 1.6 collective-permute-done.5.refs_7_
  23.5 1.2 broadcast_in_dim.24.bias_ref
  24.9 1.6 collective-permute-start.6
  27.5 2.3 %collective-permute-done.6.refs_8_ = bf16[384,128]{1,0:T(8,128)(2,1)S(1)} collective-permute-done((bf16[384,128]{1,0:T(8,128)(2,1)}, bf16[384,128]{1,0:T(8,128)(2,1)S(1)}, u32[]{:S(2)}, u32[]{:S(2)}) %collective-permute-start.6) | collective-permute-done | bytes 98336 | tf_op jit(solution)/shard_map/ppermute | solution.py:349
  29.8 1.3 collective-permute-done.14.refs_16_
  31.0 10.5 %shard_map.73 = (bf16[6144,128]{1,0:T(8,128)(2,1)S(1)}, bf16[1536,128]{1,0:T(8,128)(2,1)S(1)}, bf16[512,6144]{1,0:T(8,128)(2,1)S(1)}) custom-call(s32[9]{0:T(128)S(1)} %pad_add_fusion.info_ref.refs_0_, f32[3072,128]{1,0:T(8,128)S(1)} %broadcast_in_dim.24.bias_ref, bf16[1,3072,6144]{2,1,0:T(8,128)(2,1)} %w_ref.7, f32[6144,128]{1,0:T(8,128)S(1)} %broadcast_in_dim.22.refs_0_, ...), custom_call_target="tpu_custom_call" | custom-call | flops 2415919104 | bytes 18874368 | tf_op jit(solution)/shard_map/pallas_call | solution.py:167
  41.8 6.6 %shard_map.74.here_ref.refs_2_ = bf16[1536,128]{1,0:T(8,128)(2,1)S(1)} custom-call(s32[9]{0:T(128)S(1)} %pad_add_fusion.info_ref.refs_0_, f32[3072,128]{1,0:T(8,128)S(1)} %broadcast_in_dim.24.bias_ref, bf16[1,3072,6144]{2,1,0:T(8,128)(2,1)} %w_ref.7, bf16[512,6144]{1,0:T(8,128)(2,1)S(1)} %get-tuple-element.75.refs_0_, ...), custom_call_target="tpu_custom_call" | custom-call | flops 2415919104 | bytes 18874368 | tf_op jit(solution)/shard_map/pallas_call | solution.py:167
  49.0 1.6 collective-permute-start.16
  51.1 5.8 %shard_map.76 = (f32[768,128]{1,0:T(8,128)S(1)}, bf16[768,6144]{1,0:T(8,128)(2,1)S(1)}) custom-call(s32[9]{0:T(128)S(1)} %pad_add_fusion.info_ref.refs_0_, bf16[1,768,24576]{2,1,0:T(8,128)(2,1)} %refs_1_.23, bf16[1536,128]{1,0:T(8,128)(2,1)S(1)} %shard_map.74.here_ref.refs_2_, bf16[1536,128]{1,0:T(8,128)(2,1)S(1)} %get-tuple-element.77.refs_3_), custom_call_target="tpu_custom_call" | custom-call | flops 603979776 | bytes 4718592 | tf_op jit(solution)/shard_map/pallas_call | solution.py:330
  56.8 3.5 %collective-permute-done.16.refs_2_ = bf16[1536,128]{1,0:T(8,128)(2,1)S(1)} collective-permute-done((bf16[1536,128]{1,0:T(8,128)(2,1)S(1)}, bf16[1536,128]{1,0:T(8,128)(2,1)S(1)}, u32[]{:S(2)}, u32[]{:S(2)}) %collective-permute-start.16) | collective-permute-done | bytes 393248 | tf_op jit(solution)/shard_map/ppermute | solution.py:349
  60.4 1.2 collective-permute-done.17.refs_3_
  62.6 1.6 collective-permute-start.19
  64.2 4.4 %shard_map.77 = (f32[768,128]{1,0:T(8,128)S(1)}, bf16[768,6144]{1,0:T(8,128)(2,1)S(1)}) custom-call(s32[9]{0:T(128)S(1)} %pad_add_fusion.info_ref.refs_0_, bf16[1,768,24576]{2,1,0:T(8,128)(2,1)} %refs_1_.23, bf16[1536,128]{1,0:T(8,128)(2,1)S(1)} %collective-permute-done.16.refs_2_, bf16[1536,128]{1,0:T(8,128)(2,1)S(1)} %collective-permute-done.17.refs_3_, ...), custom_call_target="tpu_custom_call" | custom-call | flops 1207959552 | bytes 9437184 | tf_op jit(solution)/shard_map/pallas_call | solution.py:330
  68.6 4.6 %collective-permute-done.18.refs_2_ = bf16[1536,128]{1,0:T(8,128)(2,1)S(1)} collective-permute-done((bf16[1536,128]{1,0:T(8,128)(2,1)S(1)}, bf16[1536,128]{1,0:T(8,128)(2,1)S(1)}, u32[]{:S(2)}, u32[]{:S(2)}) %collective-permute-start.18) | collective-permute-done | bytes 393248 | tf_op jit(solution)/shard_map/ppermute | solution.py:349
  74.3 1.6 collective-permute-start.23
  75.9 4.5 %shard_map.78 = (f32[768,128]{1,0:T(8,128)S(1)}, bf16[768,6144]{1,0:T(8,128)(2,1)S(1)}) custom-call(s32[9]{0:T(128)S(1)} %pad_add_fusion.info_ref.refs_0_, bf16[1,768,24576]{2,1,0:T(8,128)(2,1)} %refs_1_.23, bf16[1536,128]{1,0:T(8,128)(2,1)S(1)} %collective-permute-done.18.refs_2_, bf16[1536,128]{1,0:T(8,128)(2,1)S(1)} %collective-permute-done.19.refs_3_, ...), custom_call_target="tpu_custom_call" | custom-call | flops 1207959552 | bytes 9437184 | tf_op jit(solution)/shard_map/pallas_call | solution.py:330
  80.4 4.5 %collective-permute-done.22.front_ref.refs_2_ = bf16[1536,128]{1,0:T(8,128)(2,1)S(1)} collective-permute-done((bf16[1536,128]{1,0:T(8,128)(2,1)S(1)}, bf16[1536,128]{1,0:T(8,128)(2,1)S(1)}, u32[]{:S(2)}, u32[]{:S(2)}) %collective-permute-start.22) | collective-permute-done | bytes 393248 | tf_op jit(solution)/shard_map/ppermute | solution.py:349
  86.1 1.6 collective-permute-start.27
  87.7 3.8 %shard_map.80 = (f32[768,128]{1,0:T(8,128)S(1)}, bf16[768,3072]{1,0:T(8,128)(2,1)S(1)}) custom-call(s32[9]{0:T(128)S(1)} %pad_add_fusion.info_ref.refs_0_, bf16[1,768,24576]{2,1,0:T(8,128)(2,1)} %refs_1_.23, bf16[1536,128]{1,0:T(8,128)(2,1)S(1)} %collective-permute-done.22.front_ref.refs_2_, bf16[1536,128]{1,0:T(8,128)(2,1)S(1)} %collective-permute-done.23.back_ref.refs_3_, ...), custom_call_target="tpu_custom_call" | custom-call | flops 1207959552 | bytes 9437184 | tf_op jit(solution)/shard_map/pallas_call | solution.py:330
  91.5 1.0 collective-permute-done.26.refs_2_
  93.2 1.6 shard_map.81.refs_5_
  94.9 1.6 shard_map.82.kept_ref.refs_8_
  96.6 1.4 collective-permute-done.32.swapped_ref
  98.0 0.6 shard_map.83
  99.1 1.6 collective-permute-start.34
  100.7 2.8 %collective-permute-done.33.refs_2_ = bf16[384,128]{1,0:T(8,128)(2,1)S(1)} collective-permute-done((bf16[384,128]{1,0:T(8,128)(2,1)S(1)}, bf16[384,128]{1,0:T(8,128)(2,1)S(1)}, u32[]{:S(2)}, u32[]{:S(2)}) %collective-permute-start.33) | collective-permute-done | bytes 98336 | tf_op jit(solution)/shard_map/ppermute | solution.py:349
  104.0 1.6 collective-permute-start.36
  105.5 2.6 %collective-permute-done.35.refs_4_ = bf16[384,128]{1,0:T(8,128)(2,1)S(1)} collective-permute-done((bf16[384,128]{1,0:T(8,128)(2,1)S(1)}, bf16[384,128]{1,0:T(8,128)(2,1)S(1)}, u32[]{:S(2)}, u32[]{:S(2)}) %collective-permute-start.35) | collective-permute-done | bytes 98336 | tf_op jit(solution)/shard_map/ppermute | solution.py:349
  109.1 1.6 collective-permute-start.38
  110.7 2.1 %collective-permute-done.37.refs_6_ = bf16[384,128]{1,0:T(8,128)(2,1)S(1)} collective-permute-done((bf16[384,128]{1,0:T(8,128)(2,1)S(1)}, bf16[384,128]{1,0:T(8,128)(2,1)S(1)}, u32[]{:S(2)}, u32[]{:S(2)}) %collective-permute-start.37) | collective-permute-done | bytes 98336 | tf_op jit(solution)/shard_map/ppermute | solution.py:349
  114.3 3.1 %collective-permute-done.39.refs_8_ = bf16[384,128]{1,0:T(8,128)(2,1)S(1)} collective-permute-done((bf16[384,128]{1,0:T(8,128)(2,1)S(1)}, bf16[384,128]{1,0:T(8,128)(2,1)S(1)}, u32[]{:S(2)}, u32[]{:S(2)}) %collective-permute-start.39) | collective-permute-done | bytes 98336 | tf_op jit(solution)/shard_map/ppermute | solution.py:349
  117.4 1.3 collective-permute-done.47.refs_16_
  118.7 9.8 %shard_map.84 = (bf16[6144,128]{1,0:T(8,128)(2,1)S(1)}, bf16[1536,128]{1,0:T(8,128)(2,1)S(1)}, bf16[512,6144]{1,0:T(8,128)(2,1)S(1)}) custom-call(s32[9]{0:T(128)S(1)} %pad_add_fusion.info_ref.refs_0_, f32[3072,128]{1,0:T(8,128)S(1)} %broadcast_in_dim.24.bias_ref, bf16[1,3072,6144]{2,1,0:T(8,128)(2,1)} %w_ref.7, f32[6144,128]{1,0:T(8,128)S(1)} %broadcast_in_dim.22.refs_0_, ...), custom_call_target="tpu_custom_call" | custom-call | flops 2415919104 | bytes 18874368 | tf_op jit(solution)/shard_map/pallas_call | solution.py:167
  128.7 6.6 %shard_map.85.here_ref.refs_2_ = bf16[1536,128]{1,0:T(8,128)(2,1)S(1)} custom-call(s32[9]{0:T(128)S(1)} %pad_add_fusion.info_ref.refs_0_, f32[3072,128]{1,0:T(8,128)S(1)} %broadcast_in_dim.24.bias_ref, bf16[1,3072,6144]{2,1,0:T(8,128)(2,1)} %w_ref.7, bf16[512,6144]{1,0:T(8,128)(2,1)S(1)} %get-tuple-element.99.refs_0_, ...), custom_call_target="tpu_custom_call" | custom-call | flops 2415919104 | bytes 18874368 | tf_op jit(solution)/shard_map/pallas_call | solution.py:167
  136.4 1.6 collective-permute-start.50
  138.0 5.8 %shard_map.87 = (f32[768,128]{1,0:T(8,128)S(1)}, bf16[768,6144]{1,0:T(8,128)(2,1)S(1)}) custom-call(s32[9]{0:T(128)S(1)} %pad_add_fusion.info_ref.refs_0_, bf16[1,768,24576]{2,1,0:T(8,128)(2,1)} %refs_1_.23, bf16[1536,128]{1,0:T(8,128)(2,1)S(1)} %shard_map.85.here_ref.refs_2_, bf16[1536,128]{1,0:T(8,128)(2,1)S(1)} %get-tuple-element.101.refs_3_), custom_call_target="tpu_custom_call" | custom-call | flops 603979776 | bytes 4718592 | tf_op jit(solution)/shard_map/pallas_call | solution.py:330
  143.8 3.5 %collective-permute-done.49.refs_2_ = bf16[1536,128]{1,0:T(8,128)(2,1)S(1)} collective-permute-done((bf16[1536,128]{1,0:T(8,128)(2,1)S(1)}, bf16[1536,128]{1,0:T(8,128)(2,1)S(1)}, u32[]{:S(2)}, u32[]{:S(2)}) %collective-permute-start.49) | collective-permute-done | bytes 393248 | tf_op jit(solution)/shard_map/ppermute | solution.py:349
  148.0 1.6 collective-permute-start.51
  150.1 4.4 %shard_map.88 = (f32[768,128]{1,0:T(8,128)S(1)}, bf16[768,6144]{1,0:T(8,128)(2,1)S(1)}) custom-call(s32[9]{0:T(128)S(1)} %pad_add_fusion.info_ref.refs_0_, bf16[1,768,24576]{2,1,0:T(8,128)(2,1)} %refs_1_.23, bf16[1536,128]{1,0:T(8,128)(2,1)S(1)} %collective-permute-done.49.refs_2_, bf16[1536,128]{1,0:T(8,128)(2,1)S(1)} %collective-permute-done.50.refs_3_, ...), custom_call_target="tpu_custom_call" | custom-call | flops 1207959552 | bytes 9437184 | tf_op jit(solution)/shard_map/pallas_call | solution.py:330
  154.4 4.6 %collective-permute-done.51.refs_2_ = bf16[1536,128]{1,0:T(8,128)(2,1)S(1)} collective-permute-done((bf16[1536,128]{1,0:T(8,128)(2,1)S(1)}, bf16[1536,128]{1,0:T(8,128)(2,1)S(1)}, u32[]{:S(2)}, u32[]{:S(2)}) %collective-permute-start.51) | collective-permute-done | bytes 393248 | tf_op jit(solution)/shard_map/ppermute | solution.py:349
  159.0 1.3 collective-permute-done.52.refs_3_
  160.8 1.6 collective-permute-start.55
  162.9 4.5 %shard_map.89 = (f32[768,128]{1,0:T(8,128)S(1)}, bf16[768,6144]{1,0:T(8,128)(2,1)S(1)}) custom-call(s32[9]{0:T(128)S(1)} %pad_add_fusion.info_ref.refs_0_, bf16[1,768,24576]{2,1,0:T(8,128)(2,1)} %refs_1_.23, bf16[1536,128]{1,0:T(8,128)(2,1)S(1)} %collective-permute-done.51.refs_2_, bf16[1536,128]{1,0:T(8,128)(2,1)S(1)} %collective-permute-done.52.refs_3_, ...), custom_call_target="tpu_custom_call" | custom-call | flops 1207959552 | bytes 9437184 | tf_op jit(solution)/shard_map/pallas_call | solution.py:330
  167.4 4.5 %collective-permute-done.55.front_ref.refs_2_ = bf16[1536,128]{1,0:T(8,128)(2,1)S(1)} collective-permute-done((bf16[1536,128]{1,0:T(8,128)(2,1)S(1)}, bf16[1536,128]{1,0:T(8,128)(2,1)S(1)}, u32[]{:S(2)}, u32[]{:S(2)}) %collective-permute-start.55) | collective-permute-done | bytes 393248 | tf_op jit(solution)/shard_map/ppermute | solution.py:349
  171.9 1.3 collective-permute-done.56.back_ref.refs_3_
  173.7 1.6 collective-permute-start.59
  175.8 3.8 %shard_map.91 = (f32[768,128]{1,0:T(8,128)S(1)}, bf16[768,3072]{1,0:T(8,128)(2,1)S(1)}) custom-call(s32[9]{0:T(128)S(1)} %pad_add_fusion.info_ref.refs_0_, bf16[1,768,24576]{2,1,0:T(8,128)(2,1)} %refs_1_.23, bf16[1536,128]{1,0:T(8,128)(2,1)S(1)} %collective-permute-done.55.front_ref.refs_2_, bf16[1536,128]{1,0:T(8,128)(2,1)S(1)} %collective-permute-done.56.back_ref.refs_3_, ...), custom_call_target="tpu_custom_call" | custom-call | flops 1207959552 | bytes 9437184 | tf_op jit(solution)/shard_map/pallas_call | solution.py:330
  179.6 1.0 collective-permute-done.59.refs_2_
  180.6 1.3 collective-permute-done.60.refs_3_
  182.4 1.6 shard_map.92.refs_5_
  184.0 2.5 %shard_map.93 = bf16[128,768]{1,0:T(8,128)(2,1)} custom-call(s32[9]{0:T(128)S(1)} %pad_add_fusion.info_ref.refs_0_, bf16[1,768,24576]{2,1,0:T(8,128)(2,1)} %refs_1_.23, bf16[768,128]{1,0:T(8,128)(2,1)S(1)} %collective-permute-done.63.refs_2_, bf16[768,128]{1,0:T(8,128)(2,1)S(1)} %collective-permute-done.64.refs_3_, ...), custom_call_target="tpu_custom_call" | custom-call | flops 301989888 | bytes 2359296 | tf_op jit(solution)/shard_map/pallas_call | solution.py:330
  (96 shorter events, 16.7 us)
Async XLA Ops:
  1.0 5.8 %collective-permute-start = (bf16[384,128]{1,0:T(8,128)(2,1)S(1)}, bf16[384,128]{1,0:T(8,128)(2,1)S(1)}, u32[]{:S(2)}, u32[]{:S(2)}) collective-permute-start(bf16[384,128]{1,0:T(8,128)(2,1)S(1)} %bitcast.13), channel_id=1, source_target_pairs={{0,4},{4,8},{8,12},{12,14},{14,10},{10,6},{6,2},{2,0},{1,5},{5,9},... | collective-permute-start | bytes 294920 | tf_op jit(solution)/shard_map/ppermute | solution.py:349
  4.1 4.7 %collective-permute-start.1 = (bf16[384,128]{1,0:T(8,128)(2,1)S(1)}, bf16[384,128]{1,0:T(8,128)(2,1)}, u32[]{:S(2)}, u32[]{:S(2)}) collective-permute-start(bf16[384,128]{1,0:T(8,128)(2,1)S(1)} %bitcast.14), channel_id=1, source_target_pairs={{0,2},{4,0},{8,4},{12,8},{14,12},{10,14},{6,10},{2,6},{1,3},{5,1},... | collective-permute-start | bytes 294920 | tf_op jit(solution)/shard_map/ppermute | solution.py:349
  8.8 4.7 %collective-permute-start.2 = (bf16[384,128]{1,0:T(8,128)(2,1)S(1)}, bf16[384,128]{1,0:T(8,128)(2,1)}, u32[]{:S(2)}, u32[]{:S(2)}) collective-permute-start(bf16[384,128]{1,0:T(8,128)(2,1)S(1)} %collective-permute-done.refs_2_), channel_id=1, source_target_pairs={{0,4},{4,8},{8,12},{12,14},{14,10},{10,6},{6,2},{2,0},{1,5},{5,9},... | collective-permute-start | bytes 294920 | tf_op jit(solution)/shard_map/ppermute | solution.py:349
  10.4 4.9 %collective-permute-start.3 = (bf16[384,128]{1,0:T(8,128)(2,1)}, bf16[384,128]{1,0:T(8,128)(2,1)}, u32[]{:S(2)}, u32[]{:S(2)}) collective-permute-start(bf16[384,128]{1,0:T(8,128)(2,1)} %collective-permute-done.1.refs_3_), channel_id=1, source_target_pairs={{0,2},{4,0},{8,4},{12,8},{14,12},{10,14},{6,10},{2,6},{1,3},{5,1},... | collective-permute-start | bytes 294920 | tf_op jit(solution)/shard_map/ppermute | solution.py:349
  16.9 5.0 %collective-permute-start.4 = (bf16[384,128]{1,0:T(8,128)(2,1)}, bf16[384,128]{1,0:T(8,128)(2,1)}, u32[]{:S(2)}, u32[]{:S(2)}) collective-permute-start(bf16[384,128]{1,0:T(8,128)(2,1)} %collective-permute-done.2.refs_4_), channel_id=1, source_target_pairs={{0,4},{4,8},{8,12},{12,14},{14,10},{10,6},{6,2},{2,0},{1,5},{5,9},... | collective-permute-start | bytes 294920 | tf_op jit(solution)/shard_map/ppermute | solution.py:349
  18.6 4.9 %collective-permute-start.5 = (bf16[384,128]{1,0:T(8,128)(2,1)}, bf16[384,128]{1,0:T(8,128)(2,1)}, u32[]{:S(2)}, u32[]{:S(2)}) collective-permute-start(bf16[384,128]{1,0:T(8,128)(2,1)} %collective-permute-done.3.refs_5_), channel_id=1, source_target_pairs={{0,2},{4,0},{8,4},{12,8},{14,12},{10,14},{6,10},{2,6},{1,3},{5,1},... | collective-permute-start | bytes 294920 | tf_op jit(solution)/shard_map/ppermute | solution.py:349
  19.0 7.4 %collective-permute-start.7 = (bf16[384,128]{1,0:T(8,128)(2,1)S(1)}, bf16[384,128]{1,0:T(8,128)(2,1)}, u32[]{:S(2)}, u32[]{:S(2)}) collective-permute-start(bf16[384,128]{1,0:T(8,128)(2,1)S(1)} %bitcast.15), channel_id=1, source_target_pairs={{0,16},{16,0},{1,17},{17,1},{2,18},{18,2},{3,19},{19,3},{4,20},{20... | collective-permute-start | bytes 294920 | tf_op jit(solution)/shard_map/ppermute | solution.py:352
  19.0 7.9 %collective-permute-start.8 = (bf16[384,128]{1,0:T(8,128)(2,1)S(1)}, bf16[384,128]{1,0:T(8,128)(2,1)}, u32[]{:S(2)}, u32[]{:S(2)}) collective-permute-start(bf16[384,128]{1,0:T(8,128)(2,1)S(1)} %collective-permute-done.refs_2_), channel_id=1, source_target_pairs={{0,16},{16,0},{1,17},{17,1},{2,18},{18,2},{3,19},{19,3},{4,20},{20... | collective-permute-start | bytes 294920 | tf_op jit(solution)/shard_map/ppermute | solution.py:352
  19.5 7.5 %collective-permute-start.9 = (bf16[384,128]{1,0:T(8,128)(2,1)}, bf16[384,128]{1,0:T(8,128)(2,1)}, u32[]{:S(2)}, u32[]{:S(2)}) collective-permute-start(bf16[384,128]{1,0:T(8,128)(2,1)} %collective-permute-done.1.refs_3_), channel_id=1, source_target_pairs={{0,16},{16,0},{1,17},{17,1},{2,18},{18,2},{3,19},{19,3},{4,20},{20... | collective-permute-start | bytes 294920 | tf_op jit(solution)/shard_map/ppermute | solution.py:352
  24.9 4.9 %collective-permute-start.6 = (bf16[384,128]{1,0:T(8,128)(2,1)}, bf16[384,128]{1,0:T(8,128)(2,1)S(1)}, u32[]{:S(2)}, u32[]{:S(2)}) collective-permute-start(bf16[384,128]{1,0:T(8,128)(2,1)} %collective-permute-done.4.refs_6_), channel_id=1, source_target_pairs={{0,4},{4,8},{8,12},{12,14},{14,10},{10,6},{6,2},{2,0},{1,5},{5,9},... | collective-permute-start | bytes 294920 | tf_op jit(solution)/shard_map/ppermute | solution.py:349
  26.4 3.3 %collective-permute-start.10 = (bf16[384,128]{1,0:T(8,128)(2,1)}, bf16[384,128]{1,0:T(8,128)(2,1)S(1)}, u32[]{:S(2)}, u32[]{:S(2)}) collective-permute-start(bf16[384,128]{1,0:T(8,128)(2,1)} %collective-permute-done.2.refs_4_), channel_id=1, source_target_pairs={{0,16},{16,0},{1,17},{17,1},{2,18},{18,2},{3,19},{19,3},{4,20},{20... | collective-permute-start | bytes 294920 | tf_op jit(solution)/shard_map/ppermute | solution.py:352
  26.4 3.3 %collective-permute-start.11 = (bf16[384,128]{1,0:T(8,128)(2,1)}, bf16[384,128]{1,0:T(8,128)(2,1)S(1)}, u32[]{:S(2)}, u32[]{:S(2)}) collective-permute-start(bf16[384,128]{1,0:T(8,128)(2,1)} %collective-permute-done.3.refs_5_), channel_id=1, source_target_pairs={{0,16},{16,0},{1,17},{17,1},{2,18},{18,2},{3,19},{19,3},{4,20},{20... | collective-permute-start | bytes 294920 | tf_op jit(solution)/shard_map/ppermute | solution.py:352
  26.9 2.8 %collective-permute-start.12 = (bf16[384,128]{1,0:T(8,128)(2,1)}, bf16[384,128]{1,0:T(8,128)(2,1)S(1)}, u32[]{:S(2)}, u32[]{:S(2)}) collective-permute-start(bf16[384,128]{1,0:T(8,128)(2,1)} %collective-permute-done.4.refs_6_), channel_id=1, source_target_pairs={{0,16},{16,0},{1,17},{17,1},{2,18},{18,2},{3,19},{19,3},{4,20},{20... | collective-permute-start | bytes 294920 | tf_op jit(solution)/shard_map/ppermute | solution.py:352
  27.0 2.7 %collective-permute-start.13 = (bf16[384,128]{1,0:T(8,128)(2,1)}, bf16[384,128]{1,0:T(8,128)(2,1)S(1)}, u32[]{:S(2)}, u32[]{:S(2)}) collective-permute-start(bf16[384,128]{1,0:T(8,128)(2,1)} %collective-permute-done.5.refs_7_), channel_id=1, source_target_pairs={{0,16},{16,0},{1,17},{17,1},{2,18},{18,2},{3,19},{19,3},{4,20},{20... | collective-permute-start | bytes 294920 | tf_op jit(solution)/shard_map/ppermute | solution.py:352
  29.7 1.3 collective-permute-start.14
  41.6 6.8 %collective-permute-start.15 = (bf16[1536,128]{1,0:T(8,128)(2,1)S(1)}, bf16[1536,128]{1,0:T(8,128)(2,1)S(1)}, u32[]{:S(2)}, u32[]{:S(2)}) collective-permute-start(bf16[1536,128]{1,0:T(8,128)(2,1)S(1)} %get-tuple-element.77.refs_3_), channel_id=1, source_target_pairs={{0,16},{16,0},{1,17},{17,1},{2,18},{18,2},{3,19},{19,3},{4,20},{20... | collective-permute-start | bytes 1179656 | tf_op jit(solution)/shard_map/ppermute | solution.py:352
  49.0 11.4 %collective-permute-start.16 = (bf16[1536,128]{1,0:T(8,128)(2,1)S(1)}, bf16[1536,128]{1,0:T(8,128)(2,1)S(1)}, u32[]{:S(2)}, u32[]{:S(2)}) collective-permute-start(bf16[1536,128]{1,0:T(8,128)(2,1)S(1)} %shard_map.75), channel_id=1, source_target_pairs={{0,4},{4,8},{8,12},{12,14},{14,10},{10,6},{6,2},{2,0},{1,5},{5,9},... | collective-permute-start | bytes 1179656 | tf_op jit(solution)/shard_map/ppermute | solution.py:349
  50.5 11.1 %collective-permute-start.17 = (bf16[1536,128]{1,0:T(8,128)(2,1)S(1)}, bf16[1536,128]{1,0:T(8,128)(2,1)S(1)}, u32[]{:S(2)}, u32[]{:S(2)}) collective-permute-start(bf16[1536,128]{1,0:T(8,128)(2,1)S(1)} %shard_map.75), channel_id=1, source_target_pairs={{0,2},{4,0},{8,4},{12,8},{14,12},{10,14},{6,10},{2,6},{1,3},{5,1},... | collective-permute-start | bytes 1179656 | tf_op jit(solution)/shard_map/ppermute | solution.py:349
  61.6 2.5 %collective-permute-start.20 = (bf16[1536,128]{1,0:T(8,128)(2,1)S(1)}, bf16[1536,128]{1,0:T(8,128)(2,1)S(1)}, u32[]{:S(2)}, u32[]{:S(2)}) collective-permute-start(bf16[1536,128]{1,0:T(8,128)(2,1)S(1)} %collective-permute-done.16.refs_2_), channel_id=1, source_target_pairs={{0,16},{16,0},{1,17},{17,1},{2,18},{18,2},{3,19},{19,3},{4,20},{20... | collective-permute-start | bytes 1179656 | tf_op jit(solution)/shard_map/ppermute | solution.py:352
  61.6 2.5 %collective-permute-start.21 = (bf16[1536,128]{1,0:T(8,128)(2,1)S(1)}, bf16[1536,128]{1,0:T(8,128)(2,1)S(1)}, u32[]{:S(2)}, u32[]{:S(2)}) collective-permute-start(bf16[1536,128]{1,0:T(8,128)(2,1)S(1)} %collective-permute-done.17.refs_3_), channel_id=1, source_target_pairs={{0,16},{16,0},{1,17},{17,1},{2,18},{18,2},{3,19},{19,3},{4,20},{20... | collective-permute-start | bytes 1179656 | tf_op jit(solution)/shard_map/ppermute | solution.py:352
  62.1 11.0 %collective-permute-start.18 = (bf16[1536,128]{1,0:T(8,128)(2,1)S(1)}, bf16[1536,128]{1,0:T(8,128)(2,1)S(1)}, u32[]{:S(2)}, u32[]{:S(2)}) collective-permute-start(bf16[1536,128]{1,0:T(8,128)(2,1)S(1)} %collective-permute-done.16.refs_2_), channel_id=1, source_target_pairs={{0,4},{4,8},{8,12},{12,14},{14,10},{10,6},{6,2},{2,0},{1,5},{5,9},... | collective-permute-start | bytes 1179656 | tf_op jit(solution)/shard_map/ppermute | solution.py:349
  62.6 10.7 %collective-permute-start.19 = (bf16[1536,128]{1,0:T(8,128)(2,1)S(1)}, bf16[1536,128]{1,0:T(8,128)(2,1)S(1)}, u32[]{:S(2)}, u32[]{:S(2)}) collective-permute-start(bf16[1536,128]{1,0:T(8,128)(2,1)S(1)} %collective-permute-done.17.refs_3_), channel_id=1, source_target_pairs={{0,2},{4,0},{8,4},{12,8},{14,12},{10,14},{6,10},{2,6},{1,3},{5,1},... | collective-permute-start | bytes 1179656 | tf_op jit(solution)/shard_map/ppermute | solution.py:349
  73.3 2.5 %collective-permute-start.24 = (bf16[1536,128]{1,0:T(8,128)(2,1)S(1)}, bf16[1536,128]{1,0:T(8,128)(2,1)S(1)}, u32[]{:S(2)}, u32[]{:S(2)}) collective-permute-start(bf16[1536,128]{1,0:T(8,128)(2,1)S(1)} %collective-permute-done.18.refs_2_), channel_id=1, source_target_pairs={{0,16},{16,0},{1,17},{17,1},{2,18},{18,2},{3,19},{19,3},{4,20},{20... | collective-permute-start | bytes 1179656 | tf_op jit(solution)/shard_map/ppermute | solution.py:352
  73.3 2.5 %collective-permute-start.25 = (bf16[1536,128]{1,0:T(8,128)(2,1)S(1)}, bf16[1536,128]{1,0:T(8,128)(2,1)S(1)}, u32[]{:S(2)}, u32[]{:S(2)}) collective-permute-start(bf16[1536,128]{1,0:T(8,128)(2,1)S(1)} %collective-permute-done.19.refs_3_), channel_id=1, source_target_pairs={{0,16},{16,0},{1,17},{17,1},{2,18},{18,2},{3,19},{19,3},{4,20},{20... | collective-permute-start | bytes 1179656 | tf_op jit(solution)/shard_map/ppermute | solution.py:352
  73.8 11.0 %collective-permute-start.22 = (bf16[1536,128]{1,0:T(8,128)(2,1)S(1)}, bf16[1536,128]{1,0:T(8,128)(2,1)S(1)}, u32[]{:S(2)}, u32[]{:S(2)}) collective-permute-start(bf16[1536,128]{1,0:T(8,128)(2,1)S(1)} %collective-permute-done.18.refs_2_), channel_id=1, source_target_pairs={{0,4},{4,8},{8,12},{12,14},{14,10},{10,6},{6,2},{2,0},{1,5},{5,9},... | collective-permute-start | bytes 1179656 | tf_op jit(solution)/shard_map/ppermute | solution.py:349
  74.3 10.7 %collective-permute-start.23 = (bf16[1536,128]{1,0:T(8,128)(2,1)S(1)}, bf16[1536,128]{1,0:T(8,128)(2,1)S(1)}, u32[]{:S(2)}, u32[]{:S(2)}) collective-permute-start(bf16[1536,128]{1,0:T(8,128)(2,1)S(1)} %collective-permute-done.19.refs_3_), channel_id=1, source_target_pairs={{0,2},{4,0},{8,4},{12,8},{14,12},{10,14},{6,10},{2,6},{1,3},{5,1},... | collective-permute-start | bytes 1179656 | tf_op jit(solution)/shard_map/ppermute | solution.py:349
  85.0 2.6 %collective-permute-start.28 = (bf16[1536,128]{1,0:T(8,128)(2,1)S(1)}, bf16[1536,128]{1,0:T(8,128)(2,1)S(1)}, u32[]{:S(2)}, u32[]{:S(2)}) collective-permute-start(bf16[1536,128]{1,0:T(8,128)(2,1)S(1)} %collective-permute-done.22.front_ref.refs_2_), channel_id=1, source_target_pairs={{0,16},{16,0},{1,17},{17,1},{2,18},{18,2},{3,19},{19,3},{4,20},{20... | collective-permute-start | bytes 1179656 | tf_op jit(solution)/shard_map/ppermute | solution.py:352
  85.0 2.6 %collective-permute-start.29 = (bf16[1536,128]{1,0:T(8,128)(2,1)S(1)}, bf16[1536,128]{1,0:T(8,128)(2,1)S(1)}, u32[]{:S(2)}, u32[]{:S(2)}) collective-permute-start(bf16[1536,128]{1,0:T(8,128)(2,1)S(1)} %collective-permute-done.23.back_ref.refs_3_), channel_id=1, source_target_pairs={{0,16},{16,0},{1,17},{17,1},{2,18},{18,2},{3,19},{19,3},{4,20},{20... | collective-permute-start | bytes 1179656 | tf_op jit(solution)/shard_map/ppermute | solution.py:352
  85.6 6.9 %collective-permute-start.26 = (bf16[768,128]{1,0:T(8,128)(2,1)S(1)}, bf16[768,128]{1,0:T(8,128)(2,1)S(1)}, u32[]{:S(2)}, u32[]{:S(2)}) collective-permute-start(bf16[768,128]{1,0:T(8,128)(2,1)S(1)} %get-tuple-element.89), channel_id=1, source_target_pairs={{0,4},{4,8},{8,12},{12,14},{14,10},{10,6},{6,2},{2,0},{1,5},{5,9},... | collective-permute-start | bytes 589832 | tf_op jit(solution)/shard_map/ppermute | solution.py:349
  86.1 6.6 %collective-permute-start.27 = (bf16[768,128]{1,0:T(8,128)(2,1)S(1)}, bf16[768,128]{1,0:T(8,128)(2,1)S(1)}, u32[]{:S(2)}, u32[]{:S(2)}) collective-permute-start(bf16[768,128]{1,0:T(8,128)(2,1)S(1)} %get-tuple-element.90), channel_id=1, source_target_pairs={{0,2},{4,0},{8,4},{12,8},{14,12},{10,14},{6,10},{2,6},{1,3},{5,1},... | collective-permute-start | bytes 589832 | tf_op jit(solution)/shard_map/ppermute | solution.py:349
  92.7 2.2 %collective-permute-start.30 = (bf16[768,128]{1,0:T(8,128)(2,1)S(1)}, bf16[768,128]{1,0:T(8,128)(2,1)S(1)}, u32[]{:S(2)}, u32[]{:S(2)}) collective-permute-start(bf16[768,128]{1,0:T(8,128)(2,1)S(1)} %collective-permute-done.26.refs_2_), channel_id=1, source_target_pairs={{0,16},{16,0},{1,17},{17,1},{2,18},{18,2},{3,19},{19,3},{4,20},{20... | collective-permute-start | bytes 589832 | tf_op jit(solution)/shard_map/ppermute | solution.py:352
  92.7 2.2 %collective-permute-start.31 = (bf16[768,128]{1,0:T(8,128)(2,1)S(1)}, bf16[768,128]{1,0:T(8,128)(2,1)S(1)}, u32[]{:S(2)}, u32[]{:S(2)}) collective-permute-start(bf16[768,128]{1,0:T(8,128)(2,1)S(1)} %collective-permute-done.27.refs_3_), channel_id=1, source_target_pairs={{0,16},{16,0},{1,17},{17,1},{2,18},{18,2},{3,19},{19,3},{4,20},{20... | collective-permute-start | bytes 589832 | tf_op jit(solution)/shard_map/ppermute | solution.py:352
  96.5 1.5 collective-permute-start.32
  98.6 4.9 %collective-permute-start.33 = (bf16[384,128]{1,0:T(8,128)(2,1)S(1)}, bf16[384,128]{1,0:T(8,128)(2,1)S(1)}, u32[]{:S(2)}, u32[]{:S(2)}) collective-permute-start(bf16[384,128]{1,0:T(8,128)(2,1)S(1)} %get-tuple-element.98.refs_1_), channel_id=1, source_target_pairs={{0,4},{4,8},{8,12},{12,14},{14,10},{10,6},{6,2},{2,0},{1,5},{5,9},... | collective-permute-start | bytes 294920 | tf_op jit(solution)/shard_map/ppermute | solution.py:349
  99.1 4.8 %collective-permute-start.34 = (bf16[384,128]{1,0:T(8,128)(2,1)S(1)}, bf16[384,128]{1,0:T(8,128)(2,1)S(1)}, u32[]{:S(2)}, u32[]{:S(2)}) collective-permute-start(bf16[384,128]{1,0:T(8,128)(2,1)S(1)} %get-tuple-element.98.refs_1_), channel_id=1, source_target_pairs={{0,2},{4,0},{8,4},{12,8},{14,12},{10,14},{6,10},{2,6},{1,3},{5,1},... | collective-permute-start | bytes 294920 | tf_op jit(solution)/shard_map/ppermute | solution.py:349
  103.5 4.6 %collective-permute-start.35 = (bf16[384,128]{1,0:T(8,128)(2,1)S(1)}, bf16[384,128]{1,0:T(8,128)(2,1)S(1)}, u32[]{:S(2)}, u32[]{:S(2)}) collective-permute-start(bf16[384,128]{1,0:T(8,128)(2,1)S(1)} %collective-permute-done.33.refs_2_), channel_id=1, source_target_pairs={{0,4},{4,8},{8,12},{12,14},{14,10},{10,6},{6,2},{2,0},{1,5},{5,9},... | collective-permute-start | bytes 294920 | tf_op jit(solution)/shard_map/ppermute | solution.py:349
  104.0 5.1 %collective-permute-start.36 = (bf16[384,128]{1,0:T(8,128)(2,1)S(1)}, bf16[384,128]{1,0:T(8,128)(2,1)S(1)}, u32[]{:S(2)}, u32[]{:S(2)}) collective-permute-start(bf16[384,128]{1,0:T(8,128)(2,1)S(1)} %collective-permute-done.34.refs_3_), channel_id=1, source_target_pairs={{0,2},{4,0},{8,4},{12,8},{14,12},{10,14},{6,10},{2,6},{1,3},{5,1},... | collective-permute-start | bytes 294920 | tf_op jit(solution)/shard_map/ppermute | solution.py:349
  108.1 4.6 %collective-permute-start.37 = (bf16[384,128]{1,0:T(8,128)(2,1)S(1)}, bf16[384,128]{1,0:T(8,128)(2,1)S(1)}, u32[]{:S(2)}, u32[]{:S(2)}) collective-permute-start(bf16[384,128]{1,0:T(8,128)(2,1)S(1)} %collective-permute-done.35.refs_4_), channel_id=1, source_target_pairs={{0,4},{4,8},{8,12},{12,14},{14,10},{10,6},{6,2},{2,0},{1,5},{5,9},... | collective-permute-start | bytes 294920 | tf_op jit(solution)/shard_map/ppermute | solution.py:349
  108.6 4.6 %collective-permute-start.40 = (bf16[384,128]{1,0:T(8,128)(2,1)S(1)}, bf16[384,128]{1,0:T(8,128)(2,1)S(1)}, u32[]{:S(2)}, u32[]{:S(2)}) collective-permute-start(bf16[384,128]{1,0:T(8,128)(2,1)S(1)} %get-tuple-element.98.refs_1_), channel_id=1, source_target_pairs={{0,16},{16,0},{1,17},{17,1},{2,18},{18,2},{3,19},{19,3},{4,20},{20... | collective-permute-start | bytes 294920 | tf_op jit(solution)/shard_map/ppermute | solution.py:352
  108.6 4.6 %collective-permute-start.41 = (bf16[384,128]{1,0:T(8,128)(2,1)S(1)}, bf16[384,128]{1,0:T(8,128)(2,1)S(1)}, u32[]{:S(2)}, u32[]{:S(2)}) collective-permute-start(bf16[384,128]{1,0:T(8,128)(2,1)S(1)} %collective-permute-done.33.refs_2_), channel_id=1, source_target_pairs={{0,16},{16,0},{1,17},{17,1},{2,18},{18,2},{3,19},{19,3},{4,20},{20... | collective-permute-start | bytes 294920 | tf_op jit(solution)/shard_map/ppermute | solution.py:352
  109.1 4.6 %collective-permute-start.42 = (bf16[384,128]{1,0:T(8,128)(2,1)S(1)}, bf16[384,128]{1,0:T(8,128)(2,1)S(1)}, u32[]{:S(2)}, u32[]{:S(2)}) collective-permute-start(bf16[384,128]{1,0:T(8,128)(2,1)S(1)} %collective-permute-done.34.refs_3_), channel_id=1, source_target_pairs={{0,16},{16,0},{1,17},{17,1},{2,18},{18,2},{3,19},{19,3},{4,20},{20... | collective-permute-start | bytes 294920 | tf_op jit(solution)/shard_map/ppermute | solution.py:352
  109.1 5.2 %collective-permute-start.38 = (bf16[384,128]{1,0:T(8,128)(2,1)S(1)}, bf16[384,128]{1,0:T(8,128)(2,1)S(1)}, u32[]{:S(2)}, u32[]{:S(2)}) collective-permute-start(bf16[384,128]{1,0:T(8,128)(2,1)S(1)} %collective-permute-done.36.refs_5_), channel_id=1, source_target_pairs={{0,2},{4,0},{8,4},{12,8},{14,12},{10,14},{6,10},{2,6},{1,3},{5,1},... | collective-permute-start | bytes 294920 | tf_op jit(solution)/shard_map/ppermute | solution.py:349
  112.8 4.6 %collective-permute-start.39 = (bf16[384,128]{1,0:T(8,128)(2,1)S(1)}, bf16[384,128]{1,0:T(8,128)(2,1)S(1)}, u32[]{:S(2)}, u32[]{:S(2)}) collective-permute-start(bf16[384,128]{1,0:T(8,128)(2,1)S(1)} %collective-permute-done.37.refs_6_), channel_id=1, source_target_pairs={{0,4},{4,8},{8,12},{12,14},{14,10},{10,6},{6,2},{2,0},{1,5},{5,9},... | collective-permute-start | bytes 294920 | tf_op jit(solution)/shard_map/ppermute | solution.py:349
  113.2 4.2 %collective-permute-start.43 = (bf16[384,128]{1,0:T(8,128)(2,1)S(1)}, bf16[384,128]{1,0:T(8,128)(2,1)S(1)}, u32[]{:S(2)}, u32[]{:S(2)}) collective-permute-start(bf16[384,128]{1,0:T(8,128)(2,1)S(1)} %collective-permute-done.35.refs_4_), channel_id=1, source_target_pairs={{0,16},{16,0},{1,17},{17,1},{2,18},{18,2},{3,19},{19,3},{4,20},{20... | collective-permute-start | bytes 294920 | tf_op jit(solution)/shard_map/ppermute | solution.py:352
  113.2 4.2 %collective-permute-start.44 = (bf16[384,128]{1,0:T(8,128)(2,1)S(1)}, bf16[384,128]{1,0:T(8,128)(2,1)S(1)}, u32[]{:S(2)}, u32[]{:S(2)}) collective-permute-start(bf16[384,128]{1,0:T(8,128)(2,1)S(1)} %collective-permute-done.36.refs_5_), channel_id=1, source_target_pairs={{0,16},{16,0},{1,17},{17,1},{2,18},{18,2},{3,19},{19,3},{4,20},{20... | collective-permute-start | bytes 294920 | tf_op jit(solution)/shard_map/ppermute | solution.py:352
  113.7 3.7 %collective-permute-start.45 = (bf16[384,128]{1,0:T(8,128)(2,1)S(1)}, bf16[384,128]{1,0:T(8,128)(2,1)S(1)}, u32[]{:S(2)}, u32[]{:S(2)}) collective-permute-start(bf16[384,128]{1,0:T(8,128)(2,1)S(1)} %collective-permute-done.37.refs_6_), channel_id=1, source_target_pairs={{0,16},{16,0},{1,17},{17,1},{2,18},{18,2},{3,19},{19,3},{4,20},{20... | collective-permute-start | bytes 294920 | tf_op jit(solution)/shard_map/ppermute | solution.py:352
  114.3 3.1 %collective-permute-start.46 = (bf16[384,128]{1,0:T(8,128)(2,1)S(1)}, bf16[384,128]{1,0:T(8,128)(2,1)S(1)}, u32[]{:S(2)}, u32[]{:S(2)}) collective-permute-start(bf16[384,128]{1,0:T(8,128)(2,1)S(1)} %collective-permute-done.38.refs_7_), channel_id=1, source_target_pairs={{0,16},{16,0},{1,17},{17,1},{2,18},{18,2},{3,19},{19,3},{4,20},{20... | collective-permute-start | bytes 294920 | tf_op jit(solution)/shard_map/ppermute | solution.py:352
  128.5 6.8 %collective-permute-start.48 = (bf16[1536,128]{1,0:T(8,128)(2,1)S(1)}, bf16[1536,128]{1,0:T(8,128)(2,1)S(1)}, u32[]{:S(2)}, u32[]{:S(2)}) collective-permute-start(bf16[1536,128]{1,0:T(8,128)(2,1)S(1)} %get-tuple-element.101.refs_3_), channel_id=1, source_target_pairs={{0,16},{16,0},{1,17},{17,1},{2,18},{18,2},{3,19},{19,3},{4,20},{20... | collective-permute-start | bytes 1179656 | tf_op jit(solution)/shard_map/ppermute | solution.py:352
  135.9 11.4 %collective-permute-start.49 = (bf16[1536,128]{1,0:T(8,128)(2,1)S(1)}, bf16[1536,128]{1,0:T(8,128)(2,1)S(1)}, u32[]{:S(2)}, u32[]{:S(2)}) collective-permute-start(bf16[1536,128]{1,0:T(8,128)(2,1)S(1)} %shard_map.86), channel_id=1, source_target_pairs={{0,4},{4,8},{8,12},{12,14},{14,10},{10,6},{6,2},{2,0},{1,5},{5,9},... | collective-permute-start | bytes 1179656 | tf_op jit(solution)/shard_map/ppermute | solution.py:349
  136.4 11.1 %collective-permute-start.50 = (bf16[1536,128]{1,0:T(8,128)(2,1)S(1)}, bf16[1536,128]{1,0:T(8,128)(2,1)S(1)}, u32[]{:S(2)}, u32[]{:S(2)}) collective-permute-start(bf16[1536,128]{1,0:T(8,128)(2,1)S(1)} %shard_map.86), channel_id=1, source_target_pairs={{0,2},{4,0},{8,4},{12,8},{14,12},{10,14},{6,10},{2,6},{1,3},{5,1},... | collective-permute-start | bytes 1179656 | tf_op jit(solution)/shard_map/ppermute | solution.py:349
  147.5 2.5 %collective-permute-start.53 = (bf16[1536,128]{1,0:T(8,128)(2,1)S(1)}, bf16[1536,128]{1,0:T(8,128)(2,1)S(1)}, u32[]{:S(2)}, u32[]{:S(2)}) collective-permute-start(bf16[1536,128]{1,0:T(8,128)(2,1)S(1)} %collective-permute-done.49.refs_2_), channel_id=1, source_target_pairs={{0,16},{16,0},{1,17},{17,1},{2,18},{18,2},{3,19},{19,3},{4,20},{20... | collective-permute-start | bytes 1179656 | tf_op jit(solution)/shard_map/ppermute | solution.py:352
  147.5 2.5 %collective-permute-start.54 = (bf16[1536,128]{1,0:T(8,128)(2,1)S(1)}, bf16[1536,128]{1,0:T(8,128)(2,1)S(1)}, u32[]{:S(2)}, u32[]{:S(2)}) collective-permute-start(bf16[1536,128]{1,0:T(8,128)(2,1)S(1)} %collective-permute-done.50.refs_3_), channel_id=1, source_target_pairs={{0,16},{16,0},{1,17},{17,1},{2,18},{18,2},{3,19},{19,3},{4,20},{20... | collective-permute-start | bytes 1179656 | tf_op jit(solution)/shard_map/ppermute | solution.py:352
  148.0 11.0 %collective-permute-start.51 = (bf16[1536,128]{1,0:T(8,128)(2,1)S(1)}, bf16[1536,128]{1,0:T(8,128)(2,1)S(1)}, u32[]{:S(2)}, u32[]{:S(2)}) collective-permute-start(bf16[1536,128]{1,0:T(8,128)(2,1)S(1)} %collective-permute-done.49.refs_2_), channel_id=1, source_target_pairs={{0,4},{4,8},{8,12},{12,14},{14,10},{10,6},{6,2},{2,0},{1,5},{5,9},... | collective-permute-start | bytes 1179656 | tf_op jit(solution)/shard_map/ppermute | solution.py:349
  149.6 10.7 %collective-permute-start.52 = (bf16[1536,128]{1,0:T(8,128)(2,1)S(1)}, bf16[1536,128]{1,0:T(8,128)(2,1)S(1)}, u32[]{:S(2)}, u32[]{:S(2)}) collective-permute-start(bf16[1536,128]{1,0:T(8,128)(2,1)S(1)} %collective-permute-done.50.refs_3_), channel_id=1, source_target_pairs={{0,2},{4,0},{8,4},{12,8},{14,12},{10,14},{6,10},{2,6},{1,3},{5,1},... | collective-permute-start | bytes 1179656 | tf_op jit(solution)/shard_map/ppermute | solution.py:349
  160.3 2.5 %collective-permute-start.57 = (bf16[1536,128]{1,0:T(8,128)(2,1)S(1)}, bf16[1536,128]{1,0:T(8,128)(2,1)S(1)}, u32[]{:S(2)}, u32[]{:S(2)}) collective-permute-start(bf16[1536,128]{1,0:T(8,128)(2,1)S(1)} %collective-permute-done.51.refs_2_), channel_id=1, source_target_pairs={{0,16},{16,0},{1,17},{17,1},{2,18},{18,2},{3,19},{19,3},{4,20},{20... | collective-permute-start | bytes 1179656 | tf_op jit(solution)/shard_map/ppermute | solution.py:352
  160.3 2.5 %collective-permute-start.58 = (bf16[1536,128]{1,0:T(8,128)(2,1)S(1)}, bf16[1536,128]{1,0:T(8,128)(2,1)S(1)}, u32[]{:S(2)}, u32[]{:S(2)}) collective-permute-start(bf16[1536,128]{1,0:T(8,128)(2,1)S(1)} %collective-permute-done.52.refs_3_), channel_id=1, source_target_pairs={{0,16},{16,0},{1,17},{17,1},{2,18},{18,2},{3,19},{19,3},{4,20},{20... | collective-permute-start | bytes 1179656 | tf_op jit(solution)/shard_map/ppermute | solution.py:352
  160.8 11.0 %collective-permute-start.55 = (bf16[1536,128]{1,0:T(8,128)(2,1)S(1)}, bf16[1536,128]{1,0:T(8,128)(2,1)S(1)}, u32[]{:S(2)}, u32[]{:S(2)}) collective-permute-start(bf16[1536,128]{1,0:T(8,128)(2,1)S(1)} %collective-permute-done.51.refs_2_), channel_id=1, source_target_pairs={{0,4},{4,8},{8,12},{12,14},{14,10},{10,6},{6,2},{2,0},{1,5},{5,9},... | collective-permute-start | bytes 1179656 | tf_op jit(solution)/shard_map/ppermute | solution.py:349
  162.4 10.7 %collective-permute-start.56 = (bf16[1536,128]{1,0:T(8,128)(2,1)S(1)}, bf16[1536,128]{1,0:T(8,128)(2,1)S(1)}, u32[]{:S(2)}, u32[]{:S(2)}) collective-permute-start(bf16[1536,128]{1,0:T(8,128)(2,1)S(1)} %collective-permute-done.52.refs_3_), channel_id=1, source_target_pairs={{0,2},{4,0},{8,4},{12,8},{14,12},{10,14},{6,10},{2,6},{1,3},{5,1},... | collective-permute-start | bytes 1179656 | tf_op jit(solution)/shard_map/ppermute | solution.py:349
  173.1 2.6 %collective-permute-start.61 = (bf16[1536,128]{1,0:T(8,128)(2,1)S(1)}, bf16[1536,128]{1,0:T(8,128)(2,1)S(1)}, u32[]{:S(2)}, u32[]{:S(2)}) collective-permute-start(bf16[1536,128]{1,0:T(8,128)(2,1)S(1)} %collective-permute-done.55.front_ref.refs_2_), channel_id=1, source_target_pairs={{0,16},{16,0},{1,17},{17,1},{2,18},{18,2},{3,19},{19,3},{4,20},{20... | collective-permute-start | bytes 1179656 | tf_op jit(solution)/shard_map/ppermute | solution.py:352
  173.2 2.6 %collective-permute-start.62 = (bf16[1536,128]{1,0:T(8,128)(2,1)S(1)}, bf16[1536,128]{1,0:T(8,128)(2,1)S(1)}, u32[]{:S(2)}, u32[]{:S(2)}) collective-permute-start(bf16[1536,128]{1,0:T(8,128)(2,1)S(1)} %collective-permute-done.56.back_ref.refs_3_), channel_id=1, source_target_pairs={{0,16},{16,0},{1,17},{17,1},{2,18},{18,2},{3,19},{19,3},{4,20},{20... | collective-permute-start | bytes 1179656 | tf_op jit(solution)/shard_map/ppermute | solution.py:352
  173.7 6.9 %collective-permute-start.59 = (bf16[768,128]{1,0:T(8,128)(2,1)S(1)}, bf16[768,128]{1,0:T(8,128)(2,1)S(1)}, u32[]{:S(2)}, u32[]{:S(2)}) collective-permute-start(bf16[768,128]{1,0:T(8,128)(2,1)S(1)} %get-tuple-element.113), channel_id=1, source_target_pairs={{0,4},{4,8},{8,12},{12,14},{14,10},{10,6},{6,2},{2,0},{1,5},{5,9},... | collective-permute-start | bytes 589832 | tf_op jit(solution)/shard_map/ppermute | solution.py:349
  175.3 6.5 %collective-permute-start.60 = (bf16[768,128]{1,0:T(8,128)(2,1)S(1)}, bf16[768,128]{1,0:T(8,128)(2,1)S(1)}, u32[]{:S(2)}, u32[]{:S(2)}) collective-permute-start(bf16[768,128]{1,0:T(8,128)(2,1)S(1)} %get-tuple-element.114), channel_id=1, source_target_pairs={{0,2},{4,0},{8,4},{12,8},{14,12},{10,14},{6,10},{2,6},{1,3},{5,1},... | collective-permute-start | bytes 589832 | tf_op jit(solution)/shard_map/ppermute | solution.py:349
  181.9 2.2 %collective-permute-start.63 = (bf16[768,128]{1,0:T(8,128)(2,1)S(1)}, bf16[768,128]{1,0:T(8,128)(2,1)S(1)}, u32[]{:S(2)}, u32[]{:S(2)}) collective-permute-start(bf16[768,128]{1,0:T(8,128)(2,1)S(1)} %collective-permute-done.59.refs_2_), channel_id=1, source_target_pairs={{0,16},{16,0},{1,17},{17,1},{2,18},{18,2},{3,19},{19,3},{4,20},{20... | collective-permute-start | bytes 589832 | tf_op jit(solution)/shard_map/ppermute | solution.py:352
  181.9 2.2 %collective-permute-start.64 = (bf16[768,128]{1,0:T(8,128)(2,1)S(1)}, bf16[768,128]{1,0:T(8,128)(2,1)S(1)}, u32[]{:S(2)}, u32[]{:S(2)}) collective-permute-start(bf16[768,128]{1,0:T(8,128)(2,1)S(1)} %collective-permute-done.60.refs_3_), channel_id=1, source_target_pairs={{0,16},{16,0},{1,17},{17,1},{2,18},{18,2},{3,19},{19,3},{4,20},{20... | collective-permute-start | bytes 589832 | tf_op jit(solution)/shard_map/ppermute | solution.py:352
  (1 other events, 1.3 us)

commit v3 on v2

--- a/solution.py
+++ b/solution.py
@@ -247,7 +247,7 @@
     joined, refs = refs[-1], refs[:-1]
     if coming:
         next_buf, refs = refs[-1], refs[:-1]
-    depth, tile = w_ref.shape[1], 256
+    depth, tile = w_ref.shape[1], 384
     tiles = depth // tile
 
     def start(t, carry):
@@ -318,12 +318,12 @@
     if buf is None:
         scratch += [
             pltpu.VMEM((depth, total), jnp.bfloat16),
-            pltpu.SemaphoreType.DMA((depth // 256, len(pieces))),
+            pltpu.SemaphoreType.DMA((depth // 384, len(pieces))),
         ]
     if coming:
         outs.append(jax.ShapeDtypeStruct((depth, ahead), jnp.bfloat16))
         out_specs.append(VM)
-        scratch.append(pltpu.SemaphoreType.DMA((depth // 256, len(coming))))
+        scratch.append(pltpu.SemaphoreType.DMA((depth // 384, len(coming))))
     kernel = functools.partial(second_kernel, places, coming, held, acc is None, ending)
     cost = dict(flops=2 * depth * total * tokens, moved=2 * depth * total)
     call = pallas(kernel, outs, [SM, ANY] + [VM] * (len(args) - 2), out_specs, scratch, **cost)

time: 187 us -> 186 us (level)
  transfers between devices with their start and end apart: 65 -> 65, of which waited for: 31 -> 31; matrix products, arithmetic and copies ran while one was open for 2% -> 2% of each run, Pallas kernels for 29% -> 28%
where the time goes in v3:
time: 186 us
  Pallas kernels  78.5 us (42%)
  waiting for transfers between devices  61.7 us (33%)
  starting transfers between devices  39 us (21%)
  local copies, waits for them, and re-layouts  5.73 us (3%)
    ppermute x30, waiting for transfers between devices, hop(): lax.ppermute(value, 'tp', [(ring[at], ring[(at + steps) % n]) for at in r...  57.6 us
    pallas_call x12, Pallas kernels, second_matmul(): results = call(*args)  43.2 us
    pallas_call x4, Pallas kernels, first_matmul(): results = call(info, bias, w, *args)  33.5 us
    ppermute x30, starting transfers between devices, hop(): lax.ppermute(value, 'tp', [(ring[at], ring[(at + steps) % n]) for at in r...  31.8 us
    ppermute x35, starting transfers between devices, swap(): return lax.ppermute(value, 'segment', [(0, 1), (1, 0)])  7.22 us
    ppermute x35, waiting for transfers between devices, swap(): return lax.ppermute(value, 'segment', [(0, 1), (1, 0)])  4.05 us
  transfers between devices with their start and end apart: 65, of which 31 were waited for; matrix products, arithmetic and copies ran while one was open for 2% of the time, Pallas kernels for 28%

profile of v3, /device:TPU:0, one launch (start us, length us, event | category | flops | bytes accessed | tf_op | source)
XLA Modules:
  0.0 186.0 jit_solution(6399859606937062670)
XLA Ops:
  0.0 0.9 constant_dynamic-slice_fusion
  1.0 3.1 %collective-permute-start = (bf16[384,128]{1,0:T(8,128)(2,1)S(1)}, bf16[384,128]{1,0:T(8,128)(2,1)S(1)}, u32[]{:S(2)}, u32[]{:S(2)}) collective-permute-start(bf16[384,128]{1,0:T(8,128)(2,1)S(1)} %bitcast.13), channel_id=1, source_target_pairs={{0,4},{4,8},{8,12},{12,14},{14,10},{10,6},{6,2},{2,0},{1,5},{5,9},... | collective-permute-start | bytes 294920 | tf_op jit(solution)/shard_map/ppermute | solution.py:349
  4.1 1.1 copy.9
  5.2 0.7 dynamic-slice_bitcast_fusion
  6.0 0.9 collective-permute-done.refs_2_
  6.8 2.0 %collective-permute-done.1.refs_3_ = bf16[384,128]{1,0:T(8,128)(2,1)} collective-permute-done((bf16[384,128]{1,0:T(8,128)(2,1)S(1)}, bf16[384,128]{1,0:T(8,128)(2,1)}, u32[]{:S(2)}, u32[]{:S(2)}) %collective-permute-start.1) | collective-permute-done | bytes 98336 | tf_op jit(solution)/shard_map/ppermute | solution.py:349
  8.8 1.6 collective-permute-start.2
  10.9 2.7 %collective-permute-done.2.refs_4_ = bf16[384,128]{1,0:T(8,128)(2,1)} collective-permute-done((bf16[384,128]{1,0:T(8,128)(2,1)S(1)}, bf16[384,128]{1,0:T(8,128)(2,1)}, u32[]{:S(2)}, u32[]{:S(2)}) %collective-permute-start.2) | collective-permute-done | bytes 98336 | tf_op jit(solution)/shard_map/ppermute | solution.py:349
  13.6 1.8 collective-permute-done.3.refs_5_
  15.3 1.6 broadcast_in_dim.22.refs_0_
  16.9 1.6 collective-permute-start.4
  19.5 0.7 reduce
  20.2 1.7 collective-permute-done.4.refs_6_
  21.9 1.6 collective-permute-done.5.refs_7_
  23.5 1.2 broadcast_in_dim.24.bias_ref
  24.9 1.6 collective-permute-start.6
  27.5 2.3 %collective-permute-done.6.refs_8_ = bf16[384,128]{1,0:T(8,128)(2,1)S(1)} collective-permute-done((bf16[384,128]{1,0:T(8,128)(2,1)}, bf16[384,128]{1,0:T(8,128)(2,1)S(1)}, u32[]{:S(2)}, u32[]{:S(2)}) %collective-permute-start.6) | collective-permute-done | bytes 98336 | tf_op jit(solution)/shard_map/ppermute | solution.py:349
  29.8 1.3 collective-permute-done.14.refs_16_
  31.0 10.5 %shard_map.73 = (bf16[6144,128]{1,0:T(8,128)(2,1)S(1)}, bf16[1536,128]{1,0:T(8,128)(2,1)S(1)}, bf16[512,6144]{1,0:T(8,128)(2,1)S(1)}) custom-call(s32[9]{0:T(128)S(1)} %pad_add_fusion.info_ref.refs_0_, f32[3072,128]{1,0:T(8,128)S(1)} %broadcast_in_dim.24.bias_ref, bf16[1,3072,6144]{2,1,0:T(8,128)(2,1)} %w_ref.7, f32[6144,128]{1,0:T(8,128)S(1)} %broadcast_in_dim.22.refs_0_, ...), custom_call_target="tpu_custom_call" | custom-call | flops 2415919104 | bytes 18874368 | tf_op jit(solution)/shard_map/pallas_call | solution.py:167
  41.8 6.6 %shard_map.74.here_ref.refs_2_ = bf16[1536,128]{1,0:T(8,128)(2,1)S(1)} custom-call(s32[9]{0:T(128)S(1)} %pad_add_fusion.info_ref.refs_0_, f32[3072,128]{1,0:T(8,128)S(1)} %broadcast_in_dim.24.bias_ref, bf16[1,3072,6144]{2,1,0:T(8,128)(2,1)} %w_ref.7, bf16[512,6144]{1,0:T(8,128)(2,1)S(1)} %get-tuple-element.75.refs_0_, ...), custom_call_target="tpu_custom_call" | custom-call | flops 2415919104 | bytes 18874368 | tf_op jit(solution)/shard_map/pallas_call | solution.py:167
  49.0 1.6 collective-permute-start.16
  51.1 5.7 %shard_map.76 = (f32[768,128]{1,0:T(8,128)S(1)}, bf16[768,6144]{1,0:T(8,128)(2,1)S(1)}) custom-call(s32[9]{0:T(128)S(1)} %pad_add_fusion.info_ref.refs_0_, bf16[1,768,24576]{2,1,0:T(8,128)(2,1)} %refs_1_.23, bf16[1536,128]{1,0:T(8,128)(2,1)S(1)} %shard_map.74.here_ref.refs_2_, bf16[1536,128]{1,0:T(8,128)(2,1)S(1)} %get-tuple-element.77.refs_3_), custom_call_target="tpu_custom_call" | custom-call | flops 603979776 | bytes 4718592 | tf_op jit(solution)/shard_map/pallas_call | solution.py:330
  56.8 3.6 %collective-permute-done.16.refs_2_ = bf16[1536,128]{1,0:T(8,128)(2,1)S(1)} collective-permute-done((bf16[1536,128]{1,0:T(8,128)(2,1)S(1)}, bf16[1536,128]{1,0:T(8,128)(2,1)S(1)}, u32[]{:S(2)}, u32[]{:S(2)}) %collective-permute-start.16) | collective-permute-done | bytes 393248 | tf_op jit(solution)/shard_map/ppermute | solution.py:349
  60.4 1.2 collective-permute-done.17.refs_3_
  62.6 1.6 collective-permute-start.19
  64.2 4.4 %shard_map.77 = (f32[768,128]{1,0:T(8,128)S(1)}, bf16[768,6144]{1,0:T(8,128)(2,1)S(1)}) custom-call(s32[9]{0:T(128)S(1)} %pad_add_fusion.info_ref.refs_0_, bf16[1,768,24576]{2,1,0:T(8,128)(2,1)} %refs_1_.23, bf16[1536,128]{1,0:T(8,128)(2,1)S(1)} %collective-permute-done.16.refs_2_, bf16[1536,128]{1,0:T(8,128)(2,1)S(1)} %collective-permute-done.17.refs_3_, ...), custom_call_target="tpu_custom_call" | custom-call | flops 1207959552 | bytes 9437184 | tf_op jit(solution)/shard_map/pallas_call | solution.py:330
  68.5 4.6 %collective-permute-done.18.refs_2_ = bf16[1536,128]{1,0:T(8,128)(2,1)S(1)} collective-permute-done((bf16[1536,128]{1,0:T(8,128)(2,1)S(1)}, bf16[1536,128]{1,0:T(8,128)(2,1)S(1)}, u32[]{:S(2)}, u32[]{:S(2)}) %collective-permute-start.18) | collective-permute-done | bytes 393248 | tf_op jit(solution)/shard_map/ppermute | solution.py:349
  74.3 1.6 collective-permute-start.23
  75.9 4.5 %shard_map.78 = (f32[768,128]{1,0:T(8,128)S(1)}, bf16[768,6144]{1,0:T(8,128)(2,1)S(1)}) custom-call(s32[9]{0:T(128)S(1)} %pad_add_fusion.info_ref.refs_0_, bf16[1,768,24576]{2,1,0:T(8,128)(2,1)} %refs_1_.23, bf16[1536,128]{1,0:T(8,128)(2,1)S(1)} %collective-permute-done.18.refs_2_, bf16[1536,128]{1,0:T(8,128)(2,1)S(1)} %collective-permute-done.19.refs_3_, ...), custom_call_target="tpu_custom_call" | custom-call | flops 1207959552 | bytes 9437184 | tf_op jit(solution)/shard_map/pallas_call | solution.py:330
  80.4 4.5 %collective-permute-done.22.front_ref.refs_2_ = bf16[1536,128]{1,0:T(8,128)(2,1)S(1)} collective-permute-done((bf16[1536,128]{1,0:T(8,128)(2,1)S(1)}, bf16[1536,128]{1,0:T(8,128)(2,1)S(1)}, u32[]{:S(2)}, u32[]{:S(2)}) %collective-permute-start.22) | collective-permute-done | bytes 393248 | tf_op jit(solution)/shard_map/ppermute | solution.py:349
  86.1 1.6 collective-permute-start.27
  87.7 3.6 %shard_map.80 = (f32[768,128]{1,0:T(8,128)S(1)}, bf16[768,3072]{1,0:T(8,128)(2,1)S(1)}) custom-call(s32[9]{0:T(128)S(1)} %pad_add_fusion.info_ref.refs_0_, bf16[1,768,24576]{2,1,0:T(8,128)(2,1)} %refs_1_.23, bf16[1536,128]{1,0:T(8,128)(2,1)S(1)} %collective-permute-done.22.front_ref.refs_2_, bf16[1536,128]{1,0:T(8,128)(2,1)S(1)} %collective-permute-done.23.back_ref.refs_3_, ...), custom_call_target="tpu_custom_call" | custom-call | flops 1207959552 | bytes 9437184 | tf_op jit(solution)/shard_map/pallas_call | solution.py:330
  91.2 1.2 collective-permute-done.26.refs_2_
  93.2 1.5 shard_map.81.refs_5_
  94.7 1.5 shard_map.82.kept_ref.refs_8_
  96.4 1.4 collective-permute-done.32.swapped_ref
  97.8 0.6 shard_map.83
  98.9 1.6 collective-permute-start.34
  100.5 2.8 %collective-permute-done.33.refs_2_ = bf16[384,128]{1,0:T(8,128)(2,1)S(1)} collective-permute-done((bf16[384,128]{1,0:T(8,128)(2,1)S(1)}, bf16[384,128]{1,0:T(8,128)(2,1)S(1)}, u32[]{:S(2)}, u32[]{:S(2)}) %collective-permute-start.33) | collective-permute-done | bytes 98336 | tf_op jit(solution)/shard_map/ppermute | solution.py:349
  103.7 1.6 collective-permute-start.36
  105.3 2.6 %collective-permute-done.35.refs_4_ = bf16[384,128]{1,0:T(8,128)(2,1)S(1)} collective-permute-done((bf16[384,128]{1,0:T(8,128)(2,1)S(1)}, bf16[384,128]{1,0:T(8,128)(2,1)S(1)}, u32[]{:S(2)}, u32[]{:S(2)}) %collective-permute-start.35) | collective-permute-done | bytes 98336 | tf_op jit(solution)/shard_map/ppermute | solution.py:349
  108.9 1.6 collective-permute-start.38
  110.4 2.1 %collective-permute-done.37.refs_6_ = bf16[384,128]{1,0:T(8,128)(2,1)S(1)} collective-permute-done((bf16[384,128]{1,0:T(8,128)(2,1)S(1)}, bf16[384,128]{1,0:T(8,128)(2,1)S(1)}, u32[]{:S(2)}, u32[]{:S(2)}) %collective-permute-start.37) | collective-permute-done | bytes 98336 | tf_op jit(solution)/shard_map/ppermute | solution.py:349
  114.1 3.1 %collective-permute-done.39.refs_8_ = bf16[384,128]{1,0:T(8,128)(2,1)S(1)} collective-permute-done((bf16[384,128]{1,0:T(8,128)(2,1)S(1)}, bf16[384,128]{1,0:T(8,128)(2,1)S(1)}, u32[]{:S(2)}, u32[]{:S(2)}) %collective-permute-start.39) | collective-permute-done | bytes 98336 | tf_op jit(solution)/shard_map/ppermute | solution.py:349
  117.2 1.3 collective-permute-done.47.refs_16_
  118.4 9.8 %shard_map.84 = (bf16[6144,128]{1,0:T(8,128)(2,1)S(1)}, bf16[1536,128]{1,0:T(8,128)(2,1)S(1)}, bf16[512,6144]{1,0:T(8,128)(2,1)S(1)}) custom-call(s32[9]{0:T(128)S(1)} %pad_add_fusion.info_ref.refs_0_, f32[3072,128]{1,0:T(8,128)S(1)} %broadcast_in_dim.24.bias_ref, bf16[1,3072,6144]{2,1,0:T(8,128)(2,1)} %w_ref.7, f32[6144,128]{1,0:T(8,128)S(1)} %broadcast_in_dim.22.refs_0_, ...), custom_call_target="tpu_custom_call" | custom-call | flops 2415919104 | bytes 18874368 | tf_op jit(solution)/shard_map/pallas_call | solution.py:167
  128.5 6.6 %shard_map.85.here_ref.refs_2_ = bf16[1536,128]{1,0:T(8,128)(2,1)S(1)} custom-call(s32[9]{0:T(128)S(1)} %pad_add_fusion.info_ref.refs_0_, f32[3072,128]{1,0:T(8,128)S(1)} %broadcast_in_dim.24.bias_ref, bf16[1,3072,6144]{2,1,0:T(8,128)(2,1)} %w_ref.7, bf16[512,6144]{1,0:T(8,128)(2,1)S(1)} %get-tuple-element.99.refs_0_, ...), custom_call_target="tpu_custom_call" | custom-call | flops 2415919104 | bytes 18874368 | tf_op jit(solution)/shard_map/pallas_call | solution.py:167
  136.2 1.6 collective-permute-start.50
  137.7 5.7 %shard_map.87 = (f32[768,128]{1,0:T(8,128)S(1)}, bf16[768,6144]{1,0:T(8,128)(2,1)S(1)}) custom-call(s32[9]{0:T(128)S(1)} %pad_add_fusion.info_ref.refs_0_, bf16[1,768,24576]{2,1,0:T(8,128)(2,1)} %refs_1_.23, bf16[1536,128]{1,0:T(8,128)(2,1)S(1)} %shard_map.85.here_ref.refs_2_, bf16[1536,128]{1,0:T(8,128)(2,1)S(1)} %get-tuple-element.101.refs_3_), custom_call_target="tpu_custom_call" | custom-call | flops 603979776 | bytes 4718592 | tf_op jit(solution)/shard_map/pallas_call | solution.py:330
  143.5 3.6 %collective-permute-done.49.refs_2_ = bf16[1536,128]{1,0:T(8,128)(2,1)S(1)} collective-permute-done((bf16[1536,128]{1,0:T(8,128)(2,1)S(1)}, bf16[1536,128]{1,0:T(8,128)(2,1)S(1)}, u32[]{:S(2)}, u32[]{:S(2)}) %collective-permute-start.49) | collective-permute-done | bytes 393248 | tf_op jit(solution)/shard_map/ppermute | solution.py:349
  147.8 1.6 collective-permute-start.51
  149.8 4.4 %shard_map.88 = (f32[768,128]{1,0:T(8,128)S(1)}, bf16[768,6144]{1,0:T(8,128)(2,1)S(1)}) custom-call(s32[9]{0:T(128)S(1)} %pad_add_fusion.info_ref.refs_0_, bf16[1,768,24576]{2,1,0:T(8,128)(2,1)} %refs_1_.23, bf16[1536,128]{1,0:T(8,128)(2,1)S(1)} %collective-permute-done.49.refs_2_, bf16[1536,128]{1,0:T(8,128)(2,1)S(1)} %collective-permute-done.50.refs_3_, ...), custom_call_target="tpu_custom_call" | custom-call | flops 1207959552 | bytes 9437184 | tf_op jit(solution)/shard_map/pallas_call | solution.py:330
  154.2 4.6 %collective-permute-done.51.refs_2_ = bf16[1536,128]{1,0:T(8,128)(2,1)S(1)} collective-permute-done((bf16[1536,128]{1,0:T(8,128)(2,1)S(1)}, bf16[1536,128]{1,0:T(8,128)(2,1)S(1)}, u32[]{:S(2)}, u32[]{:S(2)}) %collective-permute-start.51) | collective-permute-done | bytes 393248 | tf_op jit(solution)/shard_map/ppermute | solution.py:349
  158.8 1.3 collective-permute-done.52.refs_3_
  160.6 1.6 collective-permute-start.55
  162.6 4.5 %shard_map.89 = (f32[768,128]{1,0:T(8,128)S(1)}, bf16[768,6144]{1,0:T(8,128)(2,1)S(1)}) custom-call(s32[9]{0:T(128)S(1)} %pad_add_fusion.info_ref.refs_0_, bf16[1,768,24576]{2,1,0:T(8,128)(2,1)} %refs_1_.23, bf16[1536,128]{1,0:T(8,128)(2,1)S(1)} %collective-permute-done.51.refs_2_, bf16[1536,128]{1,0:T(8,128)(2,1)S(1)} %collective-permute-done.52.refs_3_, ...), custom_call_target="tpu_custom_call" | custom-call | flops 1207959552 | bytes 9437184 | tf_op jit(solution)/shard_map/pallas_call | solution.py:330
  167.1 4.5 %collective-permute-done.55.front_ref.refs_2_ = bf16[1536,128]{1,0:T(8,128)(2,1)S(1)} collective-permute-done((bf16[1536,128]{1,0:T(8,128)(2,1)S(1)}, bf16[1536,128]{1,0:T(8,128)(2,1)S(1)}, u32[]{:S(2)}, u32[]{:S(2)}) %collective-permute-start.55) | collective-permute-done | bytes 393248 | tf_op jit(solution)/shard_map/ppermute | solution.py:349
  171.6 1.3 collective-permute-done.56.back_ref.refs_3_
  173.4 1.6 collective-permute-start.59
  175.5 3.6 %shard_map.91 = (f32[768,128]{1,0:T(8,128)S(1)}, bf16[768,3072]{1,0:T(8,128)(2,1)S(1)}) custom-call(s32[9]{0:T(128)S(1)} %pad_add_fusion.info_ref.refs_0_, bf16[1,768,24576]{2,1,0:T(8,128)(2,1)} %refs_1_.23, bf16[1536,128]{1,0:T(8,128)(2,1)S(1)} %collective-permute-done.55.front_ref.refs_2_, bf16[1536,128]{1,0:T(8,128)(2,1)S(1)} %collective-permute-done.56.back_ref.refs_3_, ...), custom_call_target="tpu_custom_call" | custom-call | flops 1207959552 | bytes 9437184 | tf_op jit(solution)/shard_map/pallas_call | solution.py:330
  179.1 1.2 collective-permute-done.59.refs_2_
  180.3 1.3 collective-permute-done.60.refs_3_
  182.1 1.5 shard_map.92.refs_5_
  183.7 2.4 %shard_map.93 = bf16[128,768]{1,0:T(8,128)(2,1)} custom-call(s32[9]{0:T(128)S(1)} %pad_add_fusion.info_ref.refs_0_, bf16[1,768,24576]{2,1,0:T(8,128)(2,1)} %refs_1_.23, bf16[768,128]{1,0:T(8,128)(2,1)S(1)} %collective-permute-done.63.refs_2_, bf16[768,128]{1,0:T(8,128)(2,1)S(1)} %collective-permute-done.64.refs_3_, ...), custom_call_target="tpu_custom_call" | custom-call | flops 301989888 | bytes 2359296 | tf_op jit(solution)/shard_map/pallas_call | solution.py:330
  (96 shorter events, 16.7 us)
Async XLA Ops:
  1.0 5.8 %collective-permute-start = (bf16[384,128]{1,0:T(8,128)(2,1)S(1)}, bf16[384,128]{1,0:T(8,128)(2,1)S(1)}, u32[]{:S(2)}, u32[]{:S(2)}) collective-permute-start(bf16[384,128]{1,0:T(8,128)(2,1)S(1)} %bitcast.13), channel_id=1, source_target_pairs={{0,4},{4,8},{8,12},{12,14},{14,10},{10,6},{6,2},{2,0},{1,5},{5,9},... | collective-permute-start | bytes 294920 | tf_op jit(solution)/shard_map/ppermute | solution.py:349
  4.1 4.7 %collective-permute-start.1 = (bf16[384,128]{1,0:T(8,128)(2,1)S(1)}, bf16[384,128]{1,0:T(8,128)(2,1)}, u32[]{:S(2)}, u32[]{:S(2)}) collective-permute-start(bf16[384,128]{1,0:T(8,128)(2,1)S(1)} %bitcast.14), channel_id=1, source_target_pairs={{0,2},{4,0},{8,4},{12,8},{14,12},{10,14},{6,10},{2,6},{1,3},{5,1},... | collective-permute-start | bytes 294920 | tf_op jit(solution)/shard_map/ppermute | solution.py:349
  8.8 4.7 %collective-permute-start.2 = (bf16[384,128]{1,0:T(8,128)(2,1)S(1)}, bf16[384,128]{1,0:T(8,128)(2,1)}, u32[]{:S(2)}, u32[]{:S(2)}) collective-permute-start(bf16[384,128]{1,0:T(8,128)(2,1)S(1)} %collective-permute-done.refs_2_), channel_id=1, source_target_pairs={{0,4},{4,8},{8,12},{12,14},{14,10},{10,6},{6,2},{2,0},{1,5},{5,9},... | collective-permute-start | bytes 294920 | tf_op jit(solution)/shard_map/ppermute | solution.py:349
  10.4 4.9 %collective-permute-start.3 = (bf16[384,128]{1,0:T(8,128)(2,1)}, bf16[384,128]{1,0:T(8,128)(2,1)}, u32[]{:S(2)}, u32[]{:S(2)}) collective-permute-start(bf16[384,128]{1,0:T(8,128)(2,1)} %collective-permute-done.1.refs_3_), channel_id=1, source_target_pairs={{0,2},{4,0},{8,4},{12,8},{14,12},{10,14},{6,10},{2,6},{1,3},{5,1},... | collective-permute-start | bytes 294920 | tf_op jit(solution)/shard_map/ppermute | solution.py:349
  16.9 5.0 %collective-permute-start.4 = (bf16[384,128]{1,0:T(8,128)(2,1)}, bf16[384,128]{1,0:T(8,128)(2,1)}, u32[]{:S(2)}, u32[]{:S(2)}) collective-permute-start(bf16[384,128]{1,0:T(8,128)(2,1)} %collective-permute-done.2.refs_4_), channel_id=1, source_target_pairs={{0,4},{4,8},{8,12},{12,14},{14,10},{10,6},{6,2},{2,0},{1,5},{5,9},... | collective-permute-start | bytes 294920 | tf_op jit(solution)/shard_map/ppermute | solution.py:349
  18.6 4.9 %collective-permute-start.5 = (bf16[384,128]{1,0:T(8,128)(2,1)}, bf16[384,128]{1,0:T(8,128)(2,1)}, u32[]{:S(2)}, u32[]{:S(2)}) collective-permute-start(bf16[384,128]{1,0:T(8,128)(2,1)} %collective-permute-done.3.refs_5_), channel_id=1, source_target_pairs={{0,2},{4,0},{8,4},{12,8},{14,12},{10,14},{6,10},{2,6},{1,3},{5,1},... | collective-permute-start | bytes 294920 | tf_op jit(solution)/shard_map/ppermute | solution.py:349
  19.0 7.4 %collective-permute-start.7 = (bf16[384,128]{1,0:T(8,128)(2,1)S(1)}, bf16[384,128]{1,0:T(8,128)(2,1)}, u32[]{:S(2)}, u32[]{:S(2)}) collective-permute-start(bf16[384,128]{1,0:T(8,128)(2,1)S(1)} %bitcast.15), channel_id=1, source_target_pairs={{0,16},{16,0},{1,17},{17,1},{2,18},{18,2},{3,19},{19,3},{4,20},{20... | collective-permute-start | bytes 294920 | tf_op jit(solution)/shard_map/ppermute | solution.py:352
  19.0 7.9 %collective-permute-start.8 = (bf16[384,128]{1,0:T(8,128)(2,1)S(1)}, bf16[384,128]{1,0:T(8,128)(2,1)}, u32[]{:S(2)}, u32[]{:S(2)}) collective-permute-start(bf16[384,128]{1,0:T(8,128)(2,1)S(1)} %collective-permute-done.refs_2_), channel_id=1, source_target_pairs={{0,16},{16,0},{1,17},{17,1},{2,18},{18,2},{3,19},{19,3},{4,20},{20... | collective-permute-start | bytes 294920 | tf_op jit(solution)/shard_map/ppermute | solution.py:352
  19.5 7.5 %collective-permute-start.9 = (bf16[384,128]{1,0:T(8,128)(2,1)}, bf16[384,128]{1,0:T(8,128)(2,1)}, u32[]{:S(2)}, u32[]{:S(2)}) collective-permute-start(bf16[384,128]{1,0:T(8,128)(2,1)} %collective-permute-done.1.refs_3_), channel_id=1, source_target_pairs={{0,16},{16,0},{1,17},{17,1},{2,18},{18,2},{3,19},{19,3},{4,20},{20... | collective-permute-start | bytes 294920 | tf_op jit(solution)/shard_map/ppermute | solution.py:352
  24.9 4.9 %collective-permute-start.6 = (bf16[384,128]{1,0:T(8,128)(2,1)}, bf16[384,128]{1,0:T(8,128)(2,1)S(1)}, u32[]{:S(2)}, u32[]{:S(2)}) collective-permute-start(bf16[384,128]{1,0:T(8,128)(2,1)} %collective-permute-done.4.refs_6_), channel_id=1, source_target_pairs={{0,4},{4,8},{8,12},{12,14},{14,10},{10,6},{6,2},{2,0},{1,5},{5,9},... | collective-permute-start | bytes 294920 | tf_op jit(solution)/shard_map/ppermute | solution.py:349
  26.4 3.3 %collective-permute-start.10 = (bf16[384,128]{1,0:T(8,128)(2,1)}, bf16[384,128]{1,0:T(8,128)(2,1)S(1)}, u32[]{:S(2)}, u32[]{:S(2)}) collective-permute-start(bf16[384,128]{1,0:T(8,128)(2,1)} %collective-permute-done.2.refs_4_), channel_id=1, source_target_pairs={{0,16},{16,0},{1,17},{17,1},{2,18},{18,2},{3,19},{19,3},{4,20},{20... | collective-permute-start | bytes 294920 | tf_op jit(solution)/shard_map/ppermute | solution.py:352
  26.4 3.3 %collective-permute-start.11 = (bf16[384,128]{1,0:T(8,128)(2,1)}, bf16[384,128]{1,0:T(8,128)(2,1)S(1)}, u32[]{:S(2)}, u32[]{:S(2)}) collective-permute-start(bf16[384,128]{1,0:T(8,128)(2,1)} %collective-permute-done.3.refs_5_), channel_id=1, source_target_pairs={{0,16},{16,0},{1,17},{17,1},{2,18},{18,2},{3,19},{19,3},{4,20},{20... | collective-permute-start | bytes 294920 | tf_op jit(solution)/shard_map/ppermute | solution.py:352
  26.9 2.8 %collective-permute-start.12 = (bf16[384,128]{1,0:T(8,128)(2,1)}, bf16[384,128]{1,0:T(8,128)(2,1)S(1)}, u32[]{:S(2)}, u32[]{:S(2)}) collective-permute-start(bf16[384,128]{1,0:T(8,128)(2,1)} %collective-permute-done.4.refs_6_), channel_id=1, source_target_pairs={{0,16},{16,0},{1,17},{17,1},{2,18},{18,2},{3,19},{19,3},{4,20},{20... | collective-permute-start | bytes 294920 | tf_op jit(solution)/shard_map/ppermute | solution.py:352
  27.0 2.7 %collective-permute-start.13 = (bf16[384,128]{1,0:T(8,128)(2,1)}, bf16[384,128]{1,0:T(8,128)(2,1)S(1)}, u32[]{:S(2)}, u32[]{:S(2)}) collective-permute-start(bf16[384,128]{1,0:T(8,128)(2,1)} %collective-permute-done.5.refs_7_), channel_id=1, source_target_pairs={{0,16},{16,0},{1,17},{17,1},{2,18},{18,2},{3,19},{19,3},{4,20},{20... | collective-permute-start | bytes 294920 | tf_op jit(solution)/shard_map/ppermute | solution.py:352
  29.7 1.3 collective-permute-start.14
  41.6 6.8 %collective-permute-start.15 = (bf16[1536,128]{1,0:T(8,128)(2,1)S(1)}, bf16[1536,128]{1,0:T(8,128)(2,1)S(1)}, u32[]{:S(2)}, u32[]{:S(2)}) collective-permute-start(bf16[1536,128]{1,0:T(8,128)(2,1)S(1)} %get-tuple-element.77.refs_3_), channel_id=1, source_target_pairs={{0,16},{16,0},{1,17},{17,1},{2,18},{18,2},{3,19},{19,3},{4,20},{20... | collective-permute-start | bytes 1179656 | tf_op jit(solution)/shard_map/ppermute | solution.py:352
  49.0 11.4 %collective-permute-start.16 = (bf16[1536,128]{1,0:T(8,128)(2,1)S(1)}, bf16[1536,128]{1,0:T(8,128)(2,1)S(1)}, u32[]{:S(2)}, u32[]{:S(2)}) collective-permute-start(bf16[1536,128]{1,0:T(8,128)(2,1)S(1)} %shard_map.75), channel_id=1, source_target_pairs={{0,4},{4,8},{8,12},{12,14},{14,10},{10,6},{6,2},{2,0},{1,5},{5,9},... | collective-permute-start | bytes 1179656 | tf_op jit(solution)/shard_map/ppermute | solution.py:349
  50.5 11.1 %collective-permute-start.17 = (bf16[1536,128]{1,0:T(8,128)(2,1)S(1)}, bf16[1536,128]{1,0:T(8,128)(2,1)S(1)}, u32[]{:S(2)}, u32[]{:S(2)}) collective-permute-start(bf16[1536,128]{1,0:T(8,128)(2,1)S(1)} %shard_map.75), channel_id=1, source_target_pairs={{0,2},{4,0},{8,4},{12,8},{14,12},{10,14},{6,10},{2,6},{1,3},{5,1},... | collective-permute-start | bytes 1179656 | tf_op jit(solution)/shard_map/ppermute | solution.py:349
  61.6 2.5 %collective-permute-start.20 = (bf16[1536,128]{1,0:T(8,128)(2,1)S(1)}, bf16[1536,128]{1,0:T(8,128)(2,1)S(1)}, u32[]{:S(2)}, u32[]{:S(2)}) collective-permute-start(bf16[1536,128]{1,0:T(8,128)(2,1)S(1)} %collective-permute-done.16.refs_2_), channel_id=1, source_target_pairs={{0,16},{16,0},{1,17},{17,1},{2,18},{18,2},{3,19},{19,3},{4,20},{20... | collective-permute-start | bytes 1179656 | tf_op jit(solution)/shard_map/ppermute | solution.py:352
  61.6 2.5 %collective-permute-start.21 = (bf16[1536,128]{1,0:T(8,128)(2,1)S(1)}, bf16[1536,128]{1,0:T(8,128)(2,1)S(1)}, u32[]{:S(2)}, u32[]{:S(2)}) collective-permute-start(bf16[1536,128]{1,0:T(8,128)(2,1)S(1)} %collective-permute-done.17.refs_3_), channel_id=1, source_target_pairs={{0,16},{16,0},{1,17},{17,1},{2,18},{18,2},{3,19},{19,3},{4,20},{20... | collective-permute-start | bytes 1179656 | tf_op jit(solution)/shard_map/ppermute | solution.py:352
  62.1 11.0 %collective-permute-start.18 = (bf16[1536,128]{1,0:T(8,128)(2,1)S(1)}, bf16[1536,128]{1,0:T(8,128)(2,1)S(1)}, u32[]{:S(2)}, u32[]{:S(2)}) collective-permute-start(bf16[1536,128]{1,0:T(8,128)(2,1)S(1)} %collective-permute-done.16.refs_2_), channel_id=1, source_target_pairs={{0,4},{4,8},{8,12},{12,14},{14,10},{10,6},{6,2},{2,0},{1,5},{5,9},... | collective-permute-start | bytes 1179656 | tf_op jit(solution)/shard_map/ppermute | solution.py:349
  62.6 10.7 %collective-permute-start.19 = (bf16[1536,128]{1,0:T(8,128)(2,1)S(1)}, bf16[1536,128]{1,0:T(8,128)(2,1)S(1)}, u32[]{:S(2)}, u32[]{:S(2)}) collective-permute-start(bf16[1536,128]{1,0:T(8,128)(2,1)S(1)} %collective-permute-done.17.refs_3_), channel_id=1, source_target_pairs={{0,2},{4,0},{8,4},{12,8},{14,12},{10,14},{6,10},{2,6},{1,3},{5,1},... | collective-permute-start | bytes 1179656 | tf_op jit(solution)/shard_map/ppermute | solution.py:349
  73.3 2.5 %collective-permute-start.24 = (bf16[1536,128]{1,0:T(8,128)(2,1)S(1)}, bf16[1536,128]{1,0:T(8,128)(2,1)S(1)}, u32[]{:S(2)}, u32[]{:S(2)}) collective-permute-start(bf16[1536,128]{1,0:T(8,128)(2,1)S(1)} %collective-permute-done.18.refs_2_), channel_id=1, source_target_pairs={{0,16},{16,0},{1,17},{17,1},{2,18},{18,2},{3,19},{19,3},{4,20},{20... | collective-permute-start | bytes 1179656 | tf_op jit(solution)/shard_map/ppermute | solution.py:352
  73.3 2.5 %collective-permute-start.25 = (bf16[1536,128]{1,0:T(8,128)(2,1)S(1)}, bf16[1536,128]{1,0:T(8,128)(2,1)S(1)}, u32[]{:S(2)}, u32[]{:S(2)}) collective-permute-start(bf16[1536,128]{1,0:T(8,128)(2,1)S(1)} %collective-permute-done.19.refs_3_), channel_id=1, source_target_pairs={{0,16},{16,0},{1,17},{17,1},{2,18},{18,2},{3,19},{19,3},{4,20},{20... | collective-permute-start | bytes 1179656 | tf_op jit(solution)/shard_map/ppermute | solution.py:352
  73.8 11.0 %collective-permute-start.22 = (bf16[1536,128]{1,0:T(8,128)(2,1)S(1)}, bf16[1536,128]{1,0:T(8,128)(2,1)S(1)}, u32[]{:S(2)}, u32[]{:S(2)}) collective-permute-start(bf16[1536,128]{1,0:T(8,128)(2,1)S(1)} %collective-permute-done.18.refs_2_), channel_id=1, source_target_pairs={{0,4},{4,8},{8,12},{12,14},{14,10},{10,6},{6,2},{2,0},{1,5},{5,9},... | collective-permute-start | bytes 1179656 | tf_op jit(solution)/shard_map/ppermute | solution.py:349
  74.3 10.7 %collective-permute-start.23 = (bf16[1536,128]{1,0:T(8,128)(2,1)S(1)}, bf16[1536,128]{1,0:T(8,128)(2,1)S(1)}, u32[]{:S(2)}, u32[]{:S(2)}) collective-permute-start(bf16[1536,128]{1,0:T(8,128)(2,1)S(1)} %collective-permute-done.19.refs_3_), channel_id=1, source_target_pairs={{0,2},{4,0},{8,4},{12,8},{14,12},{10,14},{6,10},{2,6},{1,3},{5,1},... | collective-permute-start | bytes 1179656 | tf_op jit(solution)/shard_map/ppermute | solution.py:349
  85.0 2.6 %collective-permute-start.28 = (bf16[1536,128]{1,0:T(8,128)(2,1)S(1)}, bf16[1536,128]{1,0:T(8,128)(2,1)S(1)}, u32[]{:S(2)}, u32[]{:S(2)}) collective-permute-start(bf16[1536,128]{1,0:T(8,128)(2,1)S(1)} %collective-permute-done.22.front_ref.refs_2_), channel_id=1, source_target_pairs={{0,16},{16,0},{1,17},{17,1},{2,18},{18,2},{3,19},{19,3},{4,20},{20... | collective-permute-start | bytes 1179656 | tf_op jit(solution)/shard_map/ppermute | solution.py:352
  85.0 2.6 %collective-permute-start.29 = (bf16[1536,128]{1,0:T(8,128)(2,1)S(1)}, bf16[1536,128]{1,0:T(8,128)(2,1)S(1)}, u32[]{:S(2)}, u32[]{:S(2)}) collective-permute-start(bf16[1536,128]{1,0:T(8,128)(2,1)S(1)} %collective-permute-done.23.back_ref.refs_3_), channel_id=1, source_target_pairs={{0,16},{16,0},{1,17},{17,1},{2,18},{18,2},{3,19},{19,3},{4,20},{20... | collective-permute-start | bytes 1179656 | tf_op jit(solution)/shard_map/ppermute | solution.py:352
  85.6 6.9 %collective-permute-start.26 = (bf16[768,128]{1,0:T(8,128)(2,1)S(1)}, bf16[768,128]{1,0:T(8,128)(2,1)S(1)}, u32[]{:S(2)}, u32[]{:S(2)}) collective-permute-start(bf16[768,128]{1,0:T(8,128)(2,1)S(1)} %get-tuple-element.89), channel_id=1, source_target_pairs={{0,4},{4,8},{8,12},{12,14},{14,10},{10,6},{6,2},{2,0},{1,5},{5,9},... | collective-permute-start | bytes 589832 | tf_op jit(solution)/shard_map/ppermute | solution.py:349
  86.1 6.6 %collective-permute-start.27 = (bf16[768,128]{1,0:T(8,128)(2,1)S(1)}, bf16[768,128]{1,0:T(8,128)(2,1)S(1)}, u32[]{:S(2)}, u32[]{:S(2)}) collective-permute-start(bf16[768,128]{1,0:T(8,128)(2,1)S(1)} %get-tuple-element.90), channel_id=1, source_target_pairs={{0,2},{4,0},{8,4},{12,8},{14,12},{10,14},{6,10},{2,6},{1,3},{5,1},... | collective-permute-start | bytes 589832 | tf_op jit(solution)/shard_map/ppermute | solution.py:349
  92.7 2.0 %collective-permute-start.30 = (bf16[768,128]{1,0:T(8,128)(2,1)S(1)}, bf16[768,128]{1,0:T(8,128)(2,1)S(1)}, u32[]{:S(2)}, u32[]{:S(2)}) collective-permute-start(bf16[768,128]{1,0:T(8,128)(2,1)S(1)} %collective-permute-done.26.refs_2_), channel_id=1, source_target_pairs={{0,16},{16,0},{1,17},{17,1},{2,18},{18,2},{3,19},{19,3},{4,20},{20... | collective-permute-start | bytes 589832 | tf_op jit(solution)/shard_map/ppermute | solution.py:352
  92.7 2.0 %collective-permute-start.31 = (bf16[768,128]{1,0:T(8,128)(2,1)S(1)}, bf16[768,128]{1,0:T(8,128)(2,1)S(1)}, u32[]{:S(2)}, u32[]{:S(2)}) collective-permute-start(bf16[768,128]{1,0:T(8,128)(2,1)S(1)} %collective-permute-done.27.refs_3_), channel_id=1, source_target_pairs={{0,16},{16,0},{1,17},{17,1},{2,18},{18,2},{3,19},{19,3},{4,20},{20... | collective-permute-start | bytes 589832 | tf_op jit(solution)/shard_map/ppermute | solution.py:352
  96.3 1.5 collective-permute-start.32
  98.4 4.9 %collective-permute-start.33 = (bf16[384,128]{1,0:T(8,128)(2,1)S(1)}, bf16[384,128]{1,0:T(8,128)(2,1)S(1)}, u32[]{:S(2)}, u32[]{:S(2)}) collective-permute-start(bf16[384,128]{1,0:T(8,128)(2,1)S(1)} %get-tuple-element.98.refs_1_), channel_id=1, source_target_pairs={{0,4},{4,8},{8,12},{12,14},{14,10},{10,6},{6,2},{2,0},{1,5},{5,9},... | collective-permute-start | bytes 294920 | tf_op jit(solution)/shard_map/ppermute | solution.py:349
  98.9 4.8 %collective-permute-start.34 = (bf16[384,128]{1,0:T(8,128)(2,1)S(1)}, bf16[384,128]{1,0:T(8,128)(2,1)S(1)}, u32[]{:S(2)}, u32[]{:S(2)}) collective-permute-start(bf16[384,128]{1,0:T(8,128)(2,1)S(1)} %get-tuple-element.98.refs_1_), channel_id=1, source_target_pairs={{0,2},{4,0},{8,4},{12,8},{14,12},{10,14},{6,10},{2,6},{1,3},{5,1},... | collective-permute-start | bytes 294920 | tf_op jit(solution)/shard_map/ppermute | solution.py:349
  103.3 4.6 %collective-permute-start.35 = (bf16[384,128]{1,0:T(8,128)(2,1)S(1)}, bf16[384,128]{1,0:T(8,128)(2,1)S(1)}, u32[]{:S(2)}, u32[]{:S(2)}) collective-permute-start(bf16[384,128]{1,0:T(8,128)(2,1)S(1)} %collective-permute-done.33.refs_2_), channel_id=1, source_target_pairs={{0,4},{4,8},{8,12},{12,14},{14,10},{10,6},{6,2},{2,0},{1,5},{5,9},... | collective-permute-start | bytes 294920 | tf_op jit(solution)/shard_map/ppermute | solution.py:349
  103.7 5.1 %collective-permute-start.36 = (bf16[384,128]{1,0:T(8,128)(2,1)S(1)}, bf16[384,128]{1,0:T(8,128)(2,1)S(1)}, u32[]{:S(2)}, u32[]{:S(2)}) collective-permute-start(bf16[384,128]{1,0:T(8,128)(2,1)S(1)} %collective-permute-done.34.refs_3_), channel_id=1, source_target_pairs={{0,2},{4,0},{8,4},{12,8},{14,12},{10,14},{6,10},{2,6},{1,3},{5,1},... | collective-permute-start | bytes 294920 | tf_op jit(solution)/shard_map/ppermute | solution.py:349
  107.9 4.6 %collective-permute-start.37 = (bf16[384,128]{1,0:T(8,128)(2,1)S(1)}, bf16[384,128]{1,0:T(8,128)(2,1)S(1)}, u32[]{:S(2)}, u32[]{:S(2)}) collective-permute-start(bf16[384,128]{1,0:T(8,128)(2,1)S(1)} %collective-permute-done.35.refs_4_), channel_id=1, source_target_pairs={{0,4},{4,8},{8,12},{12,14},{14,10},{10,6},{6,2},{2,0},{1,5},{5,9},... | collective-permute-start | bytes 294920 | tf_op jit(solution)/shard_map/ppermute | solution.py:349
  108.3 4.6 %collective-permute-start.40 = (bf16[384,128]{1,0:T(8,128)(2,1)S(1)}, bf16[384,128]{1,0:T(8,128)(2,1)S(1)}, u32[]{:S(2)}, u32[]{:S(2)}) collective-permute-start(bf16[384,128]{1,0:T(8,128)(2,1)S(1)} %get-tuple-element.98.refs_1_), channel_id=1, source_target_pairs={{0,16},{16,0},{1,17},{17,1},{2,18},{18,2},{3,19},{19,3},{4,20},{20... | collective-permute-start | bytes 294920 | tf_op jit(solution)/shard_map/ppermute | solution.py:352
  108.3 4.6 %collective-permute-start.41 = (bf16[384,128]{1,0:T(8,128)(2,1)S(1)}, bf16[384,128]{1,0:T(8,128)(2,1)S(1)}, u32[]{:S(2)}, u32[]{:S(2)}) collective-permute-start(bf16[384,128]{1,0:T(8,128)(2,1)S(1)} %collective-permute-done.33.refs_2_), channel_id=1, source_target_pairs={{0,16},{16,0},{1,17},{17,1},{2,18},{18,2},{3,19},{19,3},{4,20},{20... | collective-permute-start | bytes 294920 | tf_op jit(solution)/shard_map/ppermute | solution.py:352
  108.9 4.6 %collective-permute-start.42 = (bf16[384,128]{1,0:T(8,128)(2,1)S(1)}, bf16[384,128]{1,0:T(8,128)(2,1)S(1)}, u32[]{:S(2)}, u32[]{:S(2)}) collective-permute-start(bf16[384,128]{1,0:T(8,128)(2,1)S(1)} %collective-permute-done.34.refs_3_), channel_id=1, source_target_pairs={{0,16},{16,0},{1,17},{17,1},{2,18},{18,2},{3,19},{19,3},{4,20},{20... | collective-permute-start | bytes 294920 | tf_op jit(solution)/shard_map/ppermute | solution.py:352
  108.9 5.2 %collective-permute-start.38 = (bf16[384,128]{1,0:T(8,128)(2,1)S(1)}, bf16[384,128]{1,0:T(8,128)(2,1)S(1)}, u32[]{:S(2)}, u32[]{:S(2)}) collective-permute-start(bf16[384,128]{1,0:T(8,128)(2,1)S(1)} %collective-permute-done.36.refs_5_), channel_id=1, source_target_pairs={{0,2},{4,0},{8,4},{12,8},{14,12},{10,14},{6,10},{2,6},{1,3},{5,1},... | collective-permute-start | bytes 294920 | tf_op jit(solution)/shard_map/ppermute | solution.py:349
  112.5 4.6 %collective-permute-start.39 = (bf16[384,128]{1,0:T(8,128)(2,1)S(1)}, bf16[384,128]{1,0:T(8,128)(2,1)S(1)}, u32[]{:S(2)}, u32[]{:S(2)}) collective-permute-start(bf16[384,128]{1,0:T(8,128)(2,1)S(1)} %collective-permute-done.37.refs_6_), channel_id=1, source_target_pairs={{0,4},{4,8},{8,12},{12,14},{14,10},{10,6},{6,2},{2,0},{1,5},{5,9},... | collective-permute-start | bytes 294920 | tf_op jit(solution)/shard_map/ppermute | solution.py:349
  113.0 4.2 %collective-permute-start.43 = (bf16[384,128]{1,0:T(8,128)(2,1)S(1)}, bf16[384,128]{1,0:T(8,128)(2,1)S(1)}, u32[]{:S(2)}, u32[]{:S(2)}) collective-permute-start(bf16[384,128]{1,0:T(8,128)(2,1)S(1)} %collective-permute-done.35.refs_4_), channel_id=1, source_target_pairs={{0,16},{16,0},{1,17},{17,1},{2,18},{18,2},{3,19},{19,3},{4,20},{20... | collective-permute-start | bytes 294920 | tf_op jit(solution)/shard_map/ppermute | solution.py:352
  113.0 4.2 %collective-permute-start.44 = (bf16[384,128]{1,0:T(8,128)(2,1)S(1)}, bf16[384,128]{1,0:T(8,128)(2,1)S(1)}, u32[]{:S(2)}, u32[]{:S(2)}) collective-permute-start(bf16[384,128]{1,0:T(8,128)(2,1)S(1)} %collective-permute-done.36.refs_5_), channel_id=1, source_target_pairs={{0,16},{16,0},{1,17},{17,1},{2,18},{18,2},{3,19},{19,3},{4,20},{20... | collective-permute-start | bytes 294920 | tf_op jit(solution)/shard_map/ppermute | solution.py:352
  113.5 3.7 %collective-permute-start.45 = (bf16[384,128]{1,0:T(8,128)(2,1)S(1)}, bf16[384,128]{1,0:T(8,128)(2,1)S(1)}, u32[]{:S(2)}, u32[]{:S(2)}) collective-permute-start(bf16[384,128]{1,0:T(8,128)(2,1)S(1)} %collective-permute-done.37.refs_6_), channel_id=1, source_target_pairs={{0,16},{16,0},{1,17},{17,1},{2,18},{18,2},{3,19},{19,3},{4,20},{20... | collective-permute-start | bytes 294920 | tf_op jit(solution)/shard_map/ppermute | solution.py:352
  114.1 3.1 %collective-permute-start.46 = (bf16[384,128]{1,0:T(8,128)(2,1)S(1)}, bf16[384,128]{1,0:T(8,128)(2,1)S(1)}, u32[]{:S(2)}, u32[]{:S(2)}) collective-permute-start(bf16[384,128]{1,0:T(8,128)(2,1)S(1)} %collective-permute-done.38.refs_7_), channel_id=1, source_target_pairs={{0,16},{16,0},{1,17},{17,1},{2,18},{18,2},{3,19},{19,3},{4,20},{20... | collective-permute-start | bytes 294920 | tf_op jit(solution)/shard_map/ppermute | solution.py:352
  128.3 6.8 %collective-permute-start.48 = (bf16[1536,128]{1,0:T(8,128)(2,1)S(1)}, bf16[1536,128]{1,0:T(8,128)(2,1)S(1)}, u32[]{:S(2)}, u32[]{:S(2)}) collective-permute-start(bf16[1536,128]{1,0:T(8,128)(2,1)S(1)} %get-tuple-element.101.refs_3_), channel_id=1, source_target_pairs={{0,16},{16,0},{1,17},{17,1},{2,18},{18,2},{3,19},{19,3},{4,20},{20... | collective-permute-start | bytes 1179656 | tf_op jit(solution)/shard_map/ppermute | solution.py:352
  135.7 11.4 %collective-permute-start.49 = (bf16[1536,128]{1,0:T(8,128)(2,1)S(1)}, bf16[1536,128]{1,0:T(8,128)(2,1)S(1)}, u32[]{:S(2)}, u32[]{:S(2)}) collective-permute-start(bf16[1536,128]{1,0:T(8,128)(2,1)S(1)} %shard_map.86), channel_id=1, source_target_pairs={{0,4},{4,8},{8,12},{12,14},{14,10},{10,6},{6,2},{2,0},{1,5},{5,9},... | collective-permute-start | bytes 1179656 | tf_op jit(solution)/shard_map/ppermute | solution.py:349
  136.2 11.1 %collective-permute-start.50 = (bf16[1536,128]{1,0:T(8,128)(2,1)S(1)}, bf16[1536,128]{1,0:T(8,128)(2,1)S(1)}, u32[]{:S(2)}, u32[]{:S(2)}) collective-permute-start(bf16[1536,128]{1,0:T(8,128)(2,1)S(1)} %shard_map.86), channel_id=1, source_target_pairs={{0,2},{4,0},{8,4},{12,8},{14,12},{10,14},{6,10},{2,6},{1,3},{5,1},... | collective-permute-start | bytes 1179656 | tf_op jit(solution)/shard_map/ppermute | solution.py:349
  147.3 2.5 %collective-permute-start.53 = (bf16[1536,128]{1,0:T(8,128)(2,1)S(1)}, bf16[1536,128]{1,0:T(8,128)(2,1)S(1)}, u32[]{:S(2)}, u32[]{:S(2)}) collective-permute-start(bf16[1536,128]{1,0:T(8,128)(2,1)S(1)} %collective-permute-done.49.refs_2_), channel_id=1, source_target_pairs={{0,16},{16,0},{1,17},{17,1},{2,18},{18,2},{3,19},{19,3},{4,20},{20... | collective-permute-start | bytes 1179656 | tf_op jit(solution)/shard_map/ppermute | solution.py:352
  147.3 2.5 %collective-permute-start.54 = (bf16[1536,128]{1,0:T(8,128)(2,1)S(1)}, bf16[1536,128]{1,0:T(8,128)(2,1)S(1)}, u32[]{:S(2)}, u32[]{:S(2)}) collective-permute-start(bf16[1536,128]{1,0:T(8,128)(2,1)S(1)} %collective-permute-done.50.refs_3_), channel_id=1, source_target_pairs={{0,16},{16,0},{1,17},{17,1},{2,18},{18,2},{3,19},{19,3},{4,20},{20... | collective-permute-start | bytes 1179656 | tf_op jit(solution)/shard_map/ppermute | solution.py:352
  147.8 11.0 %collective-permute-start.51 = (bf16[1536,128]{1,0:T(8,128)(2,1)S(1)}, bf16[1536,128]{1,0:T(8,128)(2,1)S(1)}, u32[]{:S(2)}, u32[]{:S(2)}) collective-permute-start(bf16[1536,128]{1,0:T(8,128)(2,1)S(1)} %collective-permute-done.49.refs_2_), channel_id=1, source_target_pairs={{0,4},{4,8},{8,12},{12,14},{14,10},{10,6},{6,2},{2,0},{1,5},{5,9},... | collective-permute-start | bytes 1179656 | tf_op jit(solution)/shard_map/ppermute | solution.py:349
  149.3 10.7 %collective-permute-start.52 = (bf16[1536,128]{1,0:T(8,128)(2,1)S(1)}, bf16[1536,128]{1,0:T(8,128)(2,1)S(1)}, u32[]{:S(2)}, u32[]{:S(2)}) collective-permute-start(bf16[1536,128]{1,0:T(8,128)(2,1)S(1)} %collective-permute-done.50.refs_3_), channel_id=1, source_target_pairs={{0,2},{4,0},{8,4},{12,8},{14,12},{10,14},{6,10},{2,6},{1,3},{5,1},... | collective-permute-start | bytes 1179656 | tf_op jit(solution)/shard_map/ppermute | solution.py:349
  160.1 2.5 %collective-permute-start.57 = (bf16[1536,128]{1,0:T(8,128)(2,1)S(1)}, bf16[1536,128]{1,0:T(8,128)(2,1)S(1)}, u32[]{:S(2)}, u32[]{:S(2)}) collective-permute-start(bf16[1536,128]{1,0:T(8,128)(2,1)S(1)} %collective-permute-done.51.refs_2_), channel_id=1, source_target_pairs={{0,16},{16,0},{1,17},{17,1},{2,18},{18,2},{3,19},{19,3},{4,20},{20... | collective-permute-start | bytes 1179656 | tf_op jit(solution)/shard_map/ppermute | solution.py:352
  160.1 2.5 %collective-permute-start.58 = (bf16[1536,128]{1,0:T(8,128)(2,1)S(1)}, bf16[1536,128]{1,0:T(8,128)(2,1)S(1)}, u32[]{:S(2)}, u32[]{:S(2)}) collective-permute-start(bf16[1536,128]{1,0:T(8,128)(2,1)S(1)} %collective-permute-done.52.refs_3_), channel_id=1, source_target_pairs={{0,16},{16,0},{1,17},{17,1},{2,18},{18,2},{3,19},{19,3},{4,20},{20... | collective-permute-start | bytes 1179656 | tf_op jit(solution)/shard_map/ppermute | solution.py:352
  160.6 11.0 %collective-permute-start.55 = (bf16[1536,128]{1,0:T(8,128)(2,1)S(1)}, bf16[1536,128]{1,0:T(8,128)(2,1)S(1)}, u32[]{:S(2)}, u32[]{:S(2)}) collective-permute-start(bf16[1536,128]{1,0:T(8,128)(2,1)S(1)} %collective-permute-done.51.refs_2_), channel_id=1, source_target_pairs={{0,4},{4,8},{8,12},{12,14},{14,10},{10,6},{6,2},{2,0},{1,5},{5,9},... | collective-permute-start | bytes 1179656 | tf_op jit(solution)/shard_map/ppermute | solution.py:349
  162.2 10.7 %collective-permute-start.56 = (bf16[1536,128]{1,0:T(8,128)(2,1)S(1)}, bf16[1536,128]{1,0:T(8,128)(2,1)S(1)}, u32[]{:S(2)}, u32[]{:S(2)}) collective-permute-start(bf16[1536,128]{1,0:T(8,128)(2,1)S(1)} %collective-permute-done.52.refs_3_), channel_id=1, source_target_pairs={{0,2},{4,0},{8,4},{12,8},{14,12},{10,14},{6,10},{2,6},{1,3},{5,1},... | collective-permute-start | bytes 1179656 | tf_op jit(solution)/shard_map/ppermute | solution.py:349
  172.9 2.6 %collective-permute-start.61 = (bf16[1536,128]{1,0:T(8,128)(2,1)S(1)}, bf16[1536,128]{1,0:T(8,128)(2,1)S(1)}, u32[]{:S(2)}, u32[]{:S(2)}) collective-permute-start(bf16[1536,128]{1,0:T(8,128)(2,1)S(1)} %collective-permute-done.55.front_ref.refs_2_), channel_id=1, source_target_pairs={{0,16},{16,0},{1,17},{17,1},{2,18},{18,2},{3,19},{19,3},{4,20},{20... | collective-permute-start | bytes 1179656 | tf_op jit(solution)/shard_map/ppermute | solution.py:352
  172.9 2.6 %collective-permute-start.62 = (bf16[1536,128]{1,0:T(8,128)(2,1)S(1)}, bf16[1536,128]{1,0:T(8,128)(2,1)S(1)}, u32[]{:S(2)}, u32[]{:S(2)}) collective-permute-start(bf16[1536,128]{1,0:T(8,128)(2,1)S(1)} %collective-permute-done.56.back_ref.refs_3_), channel_id=1, source_target_pairs={{0,16},{16,0},{1,17},{17,1},{2,18},{18,2},{3,19},{19,3},{4,20},{20... | collective-permute-start | bytes 1179656 | tf_op jit(solution)/shard_map/ppermute | solution.py:352
  173.4 6.9 %collective-permute-start.59 = (bf16[768,128]{1,0:T(8,128)(2,1)S(1)}, bf16[768,128]{1,0:T(8,128)(2,1)S(1)}, u32[]{:S(2)}, u32[]{:S(2)}) collective-permute-start(bf16[768,128]{1,0:T(8,128)(2,1)S(1)} %get-tuple-element.113), channel_id=1, source_target_pairs={{0,4},{4,8},{8,12},{12,14},{14,10},{10,6},{6,2},{2,0},{1,5},{5,9},... | collective-permute-start | bytes 589832 | tf_op jit(solution)/shard_map/ppermute | solution.py:349
  175.1 6.5 %collective-permute-start.60 = (bf16[768,128]{1,0:T(8,128)(2,1)S(1)}, bf16[768,128]{1,0:T(8,128)(2,1)S(1)}, u32[]{:S(2)}, u32[]{:S(2)}) collective-permute-start(bf16[768,128]{1,0:T(8,128)(2,1)S(1)} %get-tuple-element.114), channel_id=1, source_target_pairs={{0,2},{4,0},{8,4},{12,8},{14,12},{10,14},{6,10},{2,6},{1,3},{5,1},... | collective-permute-start | bytes 589832 | tf_op jit(solution)/shard_map/ppermute | solution.py:349
  181.6 2.0 %collective-permute-start.63 = (bf16[768,128]{1,0:T(8,128)(2,1)S(1)}, bf16[768,128]{1,0:T(8,128)(2,1)S(1)}, u32[]{:S(2)}, u32[]{:S(2)}) collective-permute-start(bf16[768,128]{1,0:T(8,128)(2,1)S(1)} %collective-permute-done.59.refs_2_), channel_id=1, source_target_pairs={{0,16},{16,0},{1,17},{17,1},{2,18},{18,2},{3,19},{19,3},{4,20},{20... | collective-permute-start | bytes 589832 | tf_op jit(solution)/shard_map/ppermute | solution.py:352
  181.6 2.0 %collective-permute-start.64 = (bf16[768,128]{1,0:T(8,128)(2,1)S(1)}, bf16[768,128]{1,0:T(8,128)(2,1)S(1)}, u32[]{:S(2)}, u32[]{:S(2)}) collective-permute-start(bf16[768,128]{1,0:T(8,128)(2,1)S(1)} %collective-permute-done.60.refs_3_), channel_id=1, source_target_pairs={{0,16},{16,0},{1,17},{17,1},{2,18},{18,2},{3,19},{19,3},{4,20},{20... | collective-permute-start | bytes 589832 | tf_op jit(solution)/shard_map/ppermute | solution.py:352
  (1 other events, 1.3 us)
